TPU v7x, 512 devices: a whole 4x4x16 slice. The times are simulated.
512 devices in a mesh: ia: 64 (over x, z_lo, core), jb: 8 (over y, z_hi).
Axes of the slice: x: 4, y: 4, z: 16 (z_hi: 2, z_lo: 8; z = z_hi * 8 + z_lo), core: 2. Of those that a mesh axis runs over, the one named last changes fastest.
Arguments:
- density: bfloat16 [8000, 100000], P('ia', 'jb'), may hold values from -6 to 6
- chol_vectors: bfloat16 [100000, 512], P('jb', 'ia'), may hold values from -0.01953125 to 0.01953125
- virt_coef: bfloat16 [1000, 1100], P('jb'), may hold values from -0.1875 to 0.1875
Outputs:
- half_back: float32 [8, 512, 1100], P(None, ('ia', 'jb'))
All inputs are finite; a program needn't handle non-finite values.
Results may differ from a plain program's by a relative error of at most 0.0003.
Values may be sent and summed in bfloat16 or wider, within the bound.
No kernel may reach another device: no remote copies, remote signals or barrier semaphores. Data moves between devices by JAX's collectives and lax.ppermute only.
A program may use at most 64 MiB of HBM per device.

v0:
```python
import jax
import jax.numpy as jnp
from jax import lax
from jax.sharding import Mesh
from jax.sharding import PartitionSpec as P

JB = ("jb_0", "jb_1")
IA_JB = ("ia", "jb_0", "jb_1")


def from_root(shard, axis, root):
    return lax.dynamic_index_in_dim(lax.all_gather(shard, axis), root, 0, keepdims=False)


def summed_rows(shard, axes, dim):
    for axis in axes:
        shard = lax.psum_scatter(shard, axis, scatter_dimension=dim, tiled=True)
    return shard


def on_device(density, chol_vectors, virt_coef):
    row_count = density.shape[0]
    groups = lax.axis_size(JB)
    slab_devices = lax.axis_size("ia")
    all_vectors = lax.all_gather(chol_vectors, "ia", axis=1, tiled=True)
    gamma_part = jnp.dot(density, all_vectors, preferred_element_type=jnp.float32)
    owner_row = lax.axis_index("ia") % groups
    coef_block = from_root(virt_coef, JB, owner_row).astype(jnp.float32)
    chol_count = gamma_part.shape[1]
    group_width = chol_count // slab_devices
    reduced = summed_rows(gamma_part.reshape(row_count, slab_devices, group_width), JB, 2)
    summed = jnp.einsum("arq,an->rqn", reduced, coef_block, precision=lax.Precision.HIGHEST)
    regrouped = lax.all_to_all(summed, "ia", split_axis=0, concat_axis=0, tiled=True)
    occ_slab = slab_devices // groups
    return jnp.sum(
        regrouped.reshape(occ_slab, groups, regrouped.shape[1], regrouped.shape[2]), axis=1
    )


def solution(mesh):
    split = Mesh(mesh.devices.reshape(mesh.shape["ia"], 4, 2), ("ia", "jb_0", "jb_1"))
    return jax.shard_map(
        on_device,
        mesh=split,
        in_specs=(P("ia", JB), P(JB, "ia"), P(JB, None)),
        out_specs=P(None, IA_JB, None),
        check_vma=False,
    )
```

profile of v0, /device:TPU:1, one launch (start us, length us, event | category | flops | bytes accessed | tf_op | source)
XLA Modules:
  0.0 315.7 jit_solution(6847420634601952481)
XLA Ops:
  7.4 0.0 copy-start
  7.4 0.0 all-gather.5.cloned.1.call-start
  7.4 0.7 all-gather.5.cloned.1.call-update
  8.1 0.0 reduce-scatter.3.cloned.1.call-start
  8.1 140.4 %all-gather.5.cloned.1.call-done = bf16[12500,512]{0,1:T(8,128)(2,1)} async-done(((bf16[12500,8]{0,1:T(8,128)(2,1)}), bf16[12500,512]{0,1:T(8,128)(2,1)}) %all-gather.5.cloned.1.call-update) | async-done | bytes 12800016 | tf_op jit(solution)/shard_map/all_gather | solution.py:25
  148.5 0.0 copy-done
  148.5 6.5 %convolution_bitcast_fusion.1 = f32[125,64,8]{0,2,1:T(8,128)S(1)} fusion(bf16[125,12500]{0,1:T(8,128)(2,1)S(1)} %copy-done, bf16[12500,512]{0,1:T(8,128)(2,1)} %all-gather.5.cloned.1.call-done), kind=kOutput, calls=%fused_computation.1 | convolution fusion | flops 1600000000 | bytes 16181000 | tf_op jit(solution)/shard_map/dot_general | solution.py:26
  155.1 0.8 copy.6
  155.8 0.0 reduce-scatter.3.cloned.1.call-update
  155.8 0.0 all-gather.7.cloned.1.call-start
  155.9 0.5 all-gather.7.cloned.1.call-update
  156.4 0.0 reduce-scatter.5.cloned.1.call-start
  156.5 21.4 %reduce-scatter.3.cloned.1.call-done = f32[125,64,2]{0,1,2:T(8,128)} async-done(((f32[125,64,8]{0,1,2:T(8,128)}), f32[125,64,2]{0,1,2:T(8,128)}) %reduce-scatter.3.cloned.1.call-update) | async-done | bytes 64016 | tf_op jit(solution)/shard_map/reduce_scatter | solution.py:17
  177.9 0.0 reduce-scatter.5.cloned.1.call-update
  178.0 98.3 %all-gather.7.cloned.1.call-done = bf16[8,125,1100]{1,2,0:T(8,128)(2,1)} async-done(((bf16[1,125,1100]{1,2,0:T(8,128)(2,1)}), bf16[8,125,1100]{1,2,0:T(8,128)(2,1)}) %all-gather.7.cloned.1.call-update) | async-done | bytes 2200016 | tf_op jit(solution)/shard_map/all_gather | solution.py:12
  276.3 0.0 reduce-scatter.5.cloned.1.call-done
  276.3 1.4 convolution_bitcast_fusion
  277.7 0.3 copy.7
  278.0 29.9 %all_to_all.5 = f32[64,1,1100]{2,1,0:T(1,128)S(1)} all-to-all(f32[64,1,1100]{2,1,0:T(1,128)S(1)} %copy.7), channel_id=1, replica_groups=mesh['ia'=64,'jb_0'=4,'jb_1'=2] {'ia'}, dimensions={0} | all-to-all | bytes 563200 | tf_op jit(solution)/shard_map/all_to_all | solution.py:33
  307.9 0.1 bitcast_reduce_fusion
  308.0 0.6 reduce_sum.12
Async XLA Ops:
  7.4 141.2 %copy-start = (bf16[125,12500]{0,1:T(8,128)(2,1)S(1)}, bf16[125,12500]{0,1:T(8,128)(2,1)}, u32[]{:S(2)}) copy-start(bf16[125,12500]{0,1:T(8,128)(2,1)} %param.3) | copy-start | bytes 9375004
  7.4 141.2 %all-gather.5.cloned.1.call-start = ((), (), s32[]{:S(2)}) async-start(), calls=%async_computation.3 | async-start | bytes 13045760 | tf_op jit(solution)/shard_map/all_gather | solution.py:25
  8.1 169.8 %reduce-scatter.3.cloned.1.call-start = ((), (), s32[]{:S(2)}) async-start(), calls=%async_computation.4 | async-start | bytes 327680 | tf_op jit(solution)/shard_map/reduce_scatter | solution.py:17
  155.8 120.4 %all-gather.7.cloned.1.call-start = ((), (), s32[]{:S(2)}) async-start(), calls=%async_computation.6 | async-start | bytes 2543616 | tf_op jit(solution)/shard_map/all_gather | solution.py:12
  156.4 119.9 %reduce-scatter.5.cloned.1.call-start = ((), (), s32[]{:S(2)}) async-start(), calls=%async_computation.5 | async-start | bytes 98304 | tf_op jit(solution)/shard_map/reduce_scatter | solution.py:17
Sparse Core Ops, SparseCore 0:
  10.3 138.1 all-gather.4
  156.0 21.9 reduce-scatter.2
  180.7 33.1 reduce-scatter.4
Sparse Core Ops, SparseCore 1:
  159.5 116.7 all-gather.6
where the time goes:
time: 316 us
  waiting for transfers between devices  261 us (83%)
  blocking collectives  29.9 us (9%)
  between operations  14.6 us (5%)
  matrix products  7.89 us (2%)
    all_gather x1, waiting for transfers between devices, on_device(): all_vectors = lax.all_gather(chol_vectors, 'ia', axis=1, tiled=True)  140 us
    all_gather x1, waiting for transfers between devices, from_root(): lax.all_gather(shard, axis)  98.3 us
    all_to_all x1, blocking collectives, on_device(): lax.all_to_all(summed, 'ia', split_axis=0, concat_axis=0, tiled=True)  29.9 us
    reduce_scatter x2, waiting for transfers between devices, summed_rows(): shard = lax.psum_scatter(shard, axis, scatter_dimension=dim, tiled=True)  21.4 us
    dot_general x1, matrix products, on_device(): jnp.dot(density, all_vectors, preferred_element_type=jnp.float32)  6.51 us
  transfers between devices with their start and end apart: 4, of which 3 were waited for; matrix products, arithmetic and copies ran while one was open for 0% of the time, Pallas kernels for 0%

commit v1 on v0

v1 whole, which is shorter than its diff:
```python
import jax
import jax.numpy as jnp
from jax import lax
from jax.experimental import pallas as pl
from jax.experimental.pallas import tpu as pltpu
from jax.sharding import Mesh
from jax.sharding import PartitionSpec as P


AXES = ("x", "zl", "c", "y", "zh")
X, ZL, C, Y, ZH = 4, 8, 2, 4, 2
FOLD = (0, 2, 4, 6, 7, 5, 3, 1)
STEPS = (0, -1, 1, -2, 2, -3, 3, 4)
SHIFTS = (0, 1, 3, 2)
LANES = 128


def fold_ring(step):
    return [(FOLD[i], FOLD[(i + step) % ZL]) for i in range(ZL)]


def swap(shard, axis):
    return lax.ppermute(shard, axis, [(0, 1), (1, 0)])


def exchange(shard, axes):
    return lax.all_to_all(shard, axes, split_axis=0, concat_axis=0, tiled=True)


def gathered(shard, axes, count):
    return exchange(jnp.broadcast_to(shard[None], (count,) + shard.shape), axes)


def ring_gather(piece):
    parts = [piece]
    up, down = piece, piece
    for _ in range(1, ZL // 2):
        up = lax.ppermute(up, "zl", fold_ring(1))
        down = lax.ppermute(down, "zl", fold_ring(-1))
        parts += [up, down]
    half = piece.shape[0] // 2
    first = lax.ppermute(up[:half], "zl", fold_ring(1))
    second = lax.ppermute(down[half:], "zl", fold_ring(-1))
    return parts + [first, second]


def ring_source(step):
    here = lax.axis_index("zl")
    place = jnp.where(lax.rem(here, 2) == 0, here // 2, (2 * ZL - 1 - here) // 2)
    place = lax.rem(place + step + ZL, ZL)
    return jnp.where(place < ZL // 2, 2 * place, 2 * ZL - 1 - 2 * place)


def contract_kernel(*refs):
    parts, pieces, (_, out, acc) = refs[: ZL + 1], refs[ZL + 1 : ZL + 1 + 2 * X], refs[ZL + 1 + 2 * X :]
    index = pl.program_id(0)
    width = parts[0].shape[0]
    rows = pieces[0].shape[1]

    @pl.when(index == 0)
    def _():
        acc[...] = jnp.zeros_like(acc)

    left = jnp.concatenate([part[...] for part in parts], axis=0)
    for slot, piece in enumerate(pieces):
        source = lax.rem(lax.axis_index("x") - SHIFTS[slot // 2] + X, X)
        acc[2 * source + slot % 2, :, :rows] += jnp.dot(left, piece[...], preferred_element_type=jnp.float32)

    @pl.when(index == pl.num_programs(0) - 1)
    def _():
        for piece in range(2 * X):
            for slot in range(ZL):
                for part in range(2):
                    for owner in range(ZH):
                        got = acc[piece, pl.ds(slot * width + part * 16 + owner, 8, stride=2), :]
                        start = part * 1024 + (slot * ZH + owner) * 8 + piece
                        out[pl.ds(start, 8, stride=LANES), :] = got


def contract(parts, pieces, ready):
    width, quarter = parts[0].shape
    rows = pieces[0].shape[1]
    columns = ZL * width
    block = 5 * LANES
    lefts = [pl.BlockSpec((part.shape[0], block), lambda k: (0, k)) for part in parts]
    rights = [pl.BlockSpec((block, rows), lambda k: (k, 0))] * len(pieces)
    return pl.pallas_call(
        contract_kernel,
        grid=(quarter // block,),
        out_shape=jax.ShapeDtypeStruct((columns * 2 * X, LANES), jnp.float32),
        in_specs=lefts + rights + [pl.BlockSpec(memory_space=pl.ANY)],
        out_specs=pl.BlockSpec((columns * 2 * X, LANES), lambda k: (0, 0)),
        scratch_shapes=[pltpu.VMEM((2 * X, columns, LANES), jnp.float32)],
        cost_estimate=pl.CostEstimate(
            flops=2 * columns * quarter * 2 * X * LANES, bytes_accessed=8 << 20, transcendentals=0
        ),
        name="contract",
    )(*parts, *pieces, ready)


def regroup_kernel(got, out):
    for slot in range(ZL):
        target = ring_source(STEPS[slot])
        for owner in range(ZH):
            tile = slot * ZH + owner
            total = got[0, tile]
            for source in range(1, X * Y):
                total += got[source, tile]
            out[owner, target] = total


def regroup(got):
    return pl.pallas_call(
        regroup_kernel,
        out_shape=jax.ShapeDtypeStruct((ZH, ZL, 2 * X, LANES), jnp.float32),
        cost_estimate=pl.CostEstimate(flops=1 << 18, bytes_accessed=1 << 20, transcendentals=0),
        name="regroup",
    )(got)


def on_device(density, chol_vectors, virt_coef):
    rows, inner = density.shape
    width = chol_vectors.shape[1]
    virt_rows, nao = virt_coef.shape
    core, half = lax.axis_index("c"), lax.axis_index("zh")
    block = 5 * LANES
    quarter = -(-inner // (X * block)) * block
    pad = X * quarter - inner

    vectors = jnp.pad(chol_vectors.T, ((0, 0), (0, pad))).reshape(width, X, quarter)
    vectors = exchange(vectors.transpose(1, 0, 2), "x").reshape(X * width, quarter)
    parts = ring_gather(vectors)

    dens = jnp.pad(density.T, ((0, pad), (0, 0)))
    pieces = []
    for shift in SHIFTS:
        start = lax.rem(lax.axis_index("x") + shift, X) * quarter
        piece = lax.dynamic_slice(dens, (start, 0), (quarter, rows))
        if shift:
            piece = lax.ppermute(piece, "x", [(i, (i + shift) % X) for i in range(X)])
        pieces += [piece, swap(piece, "c")]

    coef = virt_coef.T
    part = -(-nao // (X * C * 16)) * 16
    coef = jnp.pad(coef, ((0, X * C * part - nao), (0, LANES - virt_rows)))
    mine = lax.axis_index("x") * C + core
    far = swap(lax.dynamic_slice(coef, (mine * part, 0), (part, LANES)), "zh")
    far = gathered(far, ("x", "c"), X * C).reshape(X * C * part, LANES)
    pair = jnp.where(half == core, jnp.stack([coef, far]), jnp.stack([far, coef]))
    coefs = gathered(pair, "y", Y)

    gamma = contract(parts, pieces, coefs)
    gamma = exchange(gamma.reshape(X * Y, ZL * ZH * 2 * X, LANES), ("x", "y"))
    gamma = regroup(gamma.reshape(X * Y, ZL * ZH, 2 * X, LANES))
    gamma = exchange(gamma.reshape(ZH * ZL, 2 * X, LANES), ("zh", "zl"))
    gamma = jnp.sum(gamma.reshape(ZH, 2, ZL // 2, X, 2, LANES), axis=0)
    gamma = gamma.transpose(2, 0, 1, 3, 4).reshape(2 * X, ZL // 2 * 2, LANES)
    out = jnp.einsum(
        "ibr,bnr->in",
        gamma,
        coefs.reshape(2 * Y, X * C * part, LANES).astype(jnp.float32),
        precision=lax.Precision.HIGHEST,
    )
    return out[:, None, :nao]


def solution(mesh):
    split = Mesh(mesh.devices.reshape(X, ZL, C, Y, ZH), AXES)
    return jax.shard_map(
        on_device,
        mesh=split,
        in_specs=(P(("x", "zl", "c"), ("y", "zh")), P(("y", "zh"), ("x", "zl", "c")), P(("y", "zh"), None)),
        out_specs=P(None, AXES, None),
        check_vma=False,
    )
```

time: 316 us -> 195 us (0.62)
  the two profiles are of different devices: /device:TPU:1 before, /device:TPU:32 now
where the time goes in v1:
time: 195 us; the launch traced here: 193 us
  starting transfers between devices  74.7 us (38%)
  waiting for transfers between devices  50.4 us (26%)
  blocking collectives  41.9 us (21%)
  local copies, waits for them, and re-layouts  13.3 us (7%)
  Pallas kernels  10.6 us (5%)
    all_to_all x2, blocking collectives, exchange(): return lax.all_to_all(shard, axes, split_axis=0, concat_axis=0, tiled=True)  41.9 us
    ppermute x5, starting transfers between devices, swap(): return lax.ppermute(shard, axis, [(0, 1), (1, 0)])  23.5 us
    ppermute x3, waiting for transfers between devices, ring_gather(): up = lax.ppermute(up, 'zl', fold_ring(1))  12.6 us
    all_to_all x3, starting transfers between devices, exchange(): return lax.all_to_all(shard, axes, split_axis=0, concat_axis=0, tiled=True)  12.1 us
    ppermute x3, starting transfers between devices, ring_gather(): down = lax.ppermute(down, 'zl', fold_ring(-1))  11.9 us
    all_to_all x3, waiting for transfers between devices, exchange(): return lax.all_to_all(shard, axes, split_axis=0, concat_axis=0, tiled=True)  11.4 us
    ppermute x3, waiting for transfers between devices, on_device(): piece = lax.ppermute(piece, 'x', [(i, (i + shift) % X) for i in range(X)])  10.6 us
    ppermute x3, starting transfers between devices, on_device(): piece = lax.ppermute(piece, 'x', [(i, (i + shift) % X) for i in range(X)])  9.59 us
  transfers between devices with their start and end apart: 19, of which 10 were waited for; matrix products, arithmetic and copies ran while one was open for 3% of the time, Pallas kernels for 0%

profile of v1, /device:TPU:32, one launch (start us, length us, event | category | flops | bytes accessed | tf_op | source)
XLA Modules:
  0.0 193.4 jit_solution(10918985171529113638)
XLA Ops:
  0.0 0.8 pad_dynamic-slice_fusion.4
  0.8 14.8 %collective-permute-start.15 = (bf16[144,128]{1,0:T(8,128)(2,1)S(1)}, bf16[144,128]{1,0:T(8,128)(2,1)S(1)}, u32[]{:S(2)}, u32[]{:S(2)}) collective-permute-start(bf16[144,128]{1,0:T(8,128)(2,1)S(1)} %pad_dynamic-slice_fusion.4), channel_id=1, source_target_pairs={{0,1},{1,0},{2,3},{3,2},{4,5},{5,4},{6,7},{7,6},{8,9},{9,8},{10,11... | collective-permute-start | bytes 110600 | tf_op jit(solution)/shard_map/ppermute | solution.py:23
  15.6 2.4 %collective-permute-done.15 = bf16[144,128]{1,0:T(8,128)(2,1)S(1)} collective-permute-done((bf16[144,128]{1,0:T(8,128)(2,1)S(1)}, bf16[144,128]{1,0:T(8,128)(2,1)S(1)}, u32[]{:S(2)}, u32[]{:S(2)}) %collective-permute-start.15) | collective-permute-done | bytes 36896 | tf_op jit(solution)/shard_map/ppermute | solution.py:23
  18.0 0.8 broadcast_in_dim.6
  18.8 4.3 %all-to-all-start.1 = ((bf16[8,144,128]{2,1,0:T(8,128)(2,1)}), bf16[8,144,128]{2,1,0:T(8,128)(2,1)S(1)}, u32[]{:S(2)}, u32[]{:S(2)}) async-start(bf16[8,144,128]{2,1,0:T(8,128)(2,1)} %broadcast_in_dim.6), calls=%async_computation.1 | async-start | bytes 589824 | tf_op jit(solution)/shard_map/all_to_all | solution.py:27
  23.1 1.6 pad.12
  24.7 1.0 pad_bitcast_fusion
  25.8 5.2 %all-to-all-done.1 = bf16[8,144,128]{2,1,0:T(8,128)(2,1)S(1)} async-done(((bf16[8,144,128]{2,1,0:T(8,128)(2,1)}), bf16[8,144,128]{2,1,0:T(8,128)(2,1)S(1)}, u32[]{:S(2)}, u32[]{:S(2)}) %all-to-all-start.1) | async-done | bytes 294944 | tf_op jit(solution)/shard_map/all_to_all | solution.py:27
  31.0 3.4 %all-to-all-start = ((bf16[4,8,3200]{2,1,0:T(8,128)(2,1)}), bf16[4,8,3200]{2,1,0:T(8,128)(2,1)S(1)}, u32[]{:S(2)}, u32[]{:S(2)}) async-start(bf16[4,8,3200]{2,1,0:T(8,128)(2,1)} %bitcast.2), calls=%async_computation | async-start | bytes 409600 | tf_op jit(solution)/shard_map/all_to_all | solution.py:27
  34.3 0.1 maximum_select_fusion
  34.4 6.2 %all-to-all-done = bf16[4,8,3200]{2,1,0:T(8,128)(2,1)S(1)} async-done(((bf16[4,8,3200]{2,1,0:T(8,128)(2,1)}), bf16[4,8,3200]{2,1,0:T(8,128)(2,1)S(1)}, u32[]{:S(2)}, u32[]{:S(2)}) %all-to-all-start) | async-done | bytes 204832 | tf_op jit(solution)/shard_map/all_to_all | solution.py:27
  40.7 1.7 broadcast_in_dim.7
  42.4 4.5 %all-to-all-start.2 = ((bf16[4,2,1152,128]{3,2,1,0:T(8,128)(2,1)}), bf16[4,2,1152,128]{3,2,1,0:T(8,128)(2,1)S(1)}, u32[]{:S(2)}, u32[]{:S(2)}) async-start(bf16[4,2,1152,128]{3,2,1,0:T(8,128)(2,1)} %broadcast_in_dim.7), calls=%async_computation.2 | async-start | bytes 4718592 | tf_op jit(solution)/shard_map/all_to_all | solution.py:27
  46.9 3.4 %pad_dynamic-slice_fusion = (bf16[3200,125]{1,0:T(8,128)(2,1)S(1)}, bf16[3200,125]{1,0:T(8,128)(2,1)S(1)}, bf16[3200,125]{1,0:T(8,128)(2,1)S(1)}, bf16[3200,125]{1,0:T(8,128)(2,1)S(1)}) fusion(s32[]{:T(128)S(6)} %select_n.30, bf16[12500,125]{1,0:T(8,128)(2,1)} %bitcast.25, s32[]{:T(128)S(6)} %select_n.28, s32[]{:T(128)S(6)} %select_n.29, s32[]{:T(128)S(6)} %select_n.27), kind=kLoop, calls=%fused_computation.1 | loop fusion | bytes 6325016 | tf_op jit(solution)/shard_map/dynamic_slice | solution.py:138
  50.3 0.0 copy-start.2
  50.3 2.5 %collective-permute-start.13 = (bf16[3200,125]{1,0:T(8,128)(2,1)S(1)}, bf16[3200,125]{1,0:T(8,128)(2,1)S(1)}, u32[]{:S(2)}, u32[]{:S(2)}) collective-permute-start(bf16[3200,125]{1,0:T(8,128)(2,1)S(1)} %get-tuple-element.5), channel_id=1, source_target_pairs={{0,256},{128,384},{256,0},{384,128},{1,257},{129,385},{257,1},{385... | collective-permute-start | bytes 2400008 | tf_op jit(solution)/shard_map/ppermute | solution.py:140
  52.8 3.3 %collective-permute-start.9 = (bf16[3200,125]{1,0:T(8,128)(2,1)S(1)}, bf16[3200,125]{1,0:T(8,128)(2,1)S(1)}, u32[]{:S(2)}, u32[]{:S(2)}) collective-permute-start(bf16[3200,125]{1,0:T(8,128)(2,1)S(1)} %get-tuple-element.6), channel_id=1, source_target_pairs={{0,128},{128,256},{256,384},{384,0},{1,129},{129,257},{257,385},{3... | collective-permute-start | bytes 2400008 | tf_op jit(solution)/shard_map/ppermute | solution.py:140
  56.1 3.7 %collective-permute-start.11 = (bf16[3200,125]{1,0:T(8,128)(2,1)S(1)}, bf16[3200,125]{1,0:T(8,128)(2,1)S(1)}, u32[]{:S(2)}, u32[]{:S(2)}) collective-permute-start(bf16[3200,125]{1,0:T(8,128)(2,1)S(1)} %get-tuple-element.7), channel_id=1, source_target_pairs={{0,384},{128,0},{256,128},{384,256},{1,385},{129,1},{257,129},{385... | collective-permute-start | bytes 2400008 | tf_op jit(solution)/shard_map/ppermute | solution.py:140
  59.9 2.9 %collective-permute-start.1 = (bf16[32,3200]{1,0:T(8,128)(2,1)S(1)}, bf16[32,3200]{1,0:T(8,128)(2,1)S(1)}, u32[]{:S(2)}, u32[]{:S(2)}) collective-permute-start(bf16[32,3200]{1,0:T(8,128)(2,1)S(1)} %bitcast.29), channel_id=1, source_target_pairs={{0,16},{32,0},{64,32},{96,64},{112,96},{80,112},{48,80},{16,48},{1... | collective-permute-start | bytes 614408 | tf_op jit(solution)/shard_map/ppermute | solution.py:39
  62.8 0.0 copy-done.9
  62.8 3.0 %collective-permute-start = (bf16[32,3200]{1,0:T(8,128)(2,1)S(1)}, bf16[32,3200]{1,0:T(8,128)(2,1)S(1)}, u32[]{:S(2)}, u32[]{:S(2)}) collective-permute-start(bf16[32,3200]{1,0:T(8,128)(2,1)S(1)} %bitcast.30), channel_id=1, source_target_pairs={{0,32},{32,64},{64,96},{96,112},{112,80},{80,48},{48,16},{16,0},{1... | collective-permute-start | bytes 614408 | tf_op jit(solution)/shard_map/ppermute | solution.py:38
  65.8 4.0 %collective-permute-done.1.refs_2_ = bf16[32,3200]{1,0:T(8,128)(2,1)S(1)} collective-permute-done((bf16[32,3200]{1,0:T(8,128)(2,1)S(1)}, bf16[32,3200]{1,0:T(8,128)(2,1)S(1)}, u32[]{:S(2)}, u32[]{:S(2)}) %collective-permute-start.1) | collective-permute-done | bytes 204832 | tf_op jit(solution)/shard_map/ppermute | solution.py:39
  69.7 4.7 %collective-permute-start.3 = (bf16[32,3200]{1,0:T(8,128)(2,1)S(1)}, bf16[32,3200]{1,0:T(8,128)(2,1)S(1)}, u32[]{:S(2)}, u32[]{:S(2)}) collective-permute-start(bf16[32,3200]{1,0:T(8,128)(2,1)S(1)} %collective-permute-done.1.refs_2_), channel_id=1, source_target_pairs={{0,16},{32,0},{64,32},{96,64},{112,96},{80,112},{48,80},{16,48},{1... | collective-permute-start | bytes 614408 | tf_op jit(solution)/shard_map/ppermute | solution.py:39
  74.4 0.0 collective-permute-done.refs_1_
  74.4 0.0 copy-start.13
  74.4 1.9 collective-permute-start.8
  76.4 0.0 collective-permute-done.13.refs_15_
  76.4 0.0 copy-start.3
  76.4 2.4 %collective-permute-start.14 = (bf16[3200,125]{1,0:T(8,128)(2,1)S(1)}, bf16[3200,125]{1,0:T(8,128)(2,1)S(1)}, u32[]{:S(2)}, u32[]{:S(2)}) collective-permute-start(bf16[3200,125]{1,0:T(8,128)(2,1)S(1)} %collective-permute-done.13.refs_15_), channel_id=1, source_target_pairs={{0,8},{8,0},{1,9},{9,1},{2,10},{10,2},{3,11},{11,3},{4,12},{12,4},... | collective-permute-start | bytes 2400008 | tf_op jit(solution)/shard_map/ppermute | solution.py:23
  78.8 10.6 %collective-permute-done.9.refs_11_ = bf16[3200,125]{1,0:T(8,128)(2,1)S(1)} collective-permute-done((bf16[3200,125]{1,0:T(8,128)(2,1)S(1)}, bf16[3200,125]{1,0:T(8,128)(2,1)S(1)}, u32[]{:S(2)}, u32[]{:S(2)}) %collective-permute-start.9) | collective-permute-done | bytes 800032 | tf_op jit(solution)/shard_map/ppermute | solution.py:140
  89.4 1.9 collective-permute-start.10
  91.3 0.0 collective-permute-done.11.refs_13_
  91.3 0.0 copy-start.5
  91.3 2.4 %collective-permute-start.12 = (bf16[3200,125]{1,0:T(8,128)(2,1)S(1)}, bf16[3200,125]{1,0:T(8,128)(2,1)}, u32[]{:S(2)}, u32[]{:S(2)}) collective-permute-start(bf16[3200,125]{1,0:T(8,128)(2,1)S(1)} %collective-permute-done.11.refs_13_), channel_id=1, source_target_pairs={{0,8},{8,0},{1,9},{9,1},{2,10},{10,2},{3,11},{11,3},{4,12},{12,4},... | collective-permute-start | bytes 2400008 | tf_op jit(solution)/shard_map/ppermute | solution.py:23
  93.7 0.0 collective-permute-done.3.refs_4_
  93.7 0.0 copy-start.14
  93.8 3.2 %collective-permute-start.2 = (bf16[32,3200]{1,0:T(8,128)(2,1)S(1)}, bf16[32,3200]{1,0:T(8,128)(2,1)S(1)}, u32[]{:S(2)}, u32[]{:S(2)}) collective-permute-start(bf16[32,3200]{1,0:T(8,128)(2,1)S(1)} %collective-permute-done.refs_1_), channel_id=1, source_target_pairs={{0,32},{32,64},{64,96},{96,112},{112,80},{80,48},{48,16},{16,0},{1... | collective-permute-start | bytes 614408 | tf_op jit(solution)/shard_map/ppermute | solution.py:38
  97.0 6.6 %collective-permute-done.2.refs_3_ = bf16[32,3200]{1,0:T(8,128)(2,1)S(1)} collective-permute-done((bf16[32,3200]{1,0:T(8,128)(2,1)S(1)}, bf16[32,3200]{1,0:T(8,128)(2,1)S(1)}, u32[]{:S(2)}, u32[]{:S(2)}) %collective-permute-start.2) | collective-permute-done | bytes 204832 | tf_op jit(solution)/shard_map/ppermute | solution.py:38
  103.5 4.3 %collective-permute-start.5 = (bf16[32,3200]{1,0:T(8,128)(2,1)S(1)}, bf16[32,3200]{1,0:T(8,128)(2,1)S(1)}, u32[]{:S(2)}, u32[]{:S(2)}) collective-permute-start(bf16[32,3200]{1,0:T(8,128)(2,1)S(1)} %collective-permute-done.3.refs_4_), channel_id=1, source_target_pairs={{0,16},{32,0},{64,32},{96,64},{112,96},{80,112},{48,80},{16,48},{1... | collective-permute-start | bytes 614408 | tf_op jit(solution)/shard_map/ppermute | solution.py:39
  107.9 3.9 %collective-permute-done.5.refs_6_ = bf16[32,3200]{1,0:T(8,128)(2,1)S(1)} collective-permute-done((bf16[32,3200]{1,0:T(8,128)(2,1)S(1)}, bf16[32,3200]{1,0:T(8,128)(2,1)S(1)}, u32[]{:S(2)}, u32[]{:S(2)}) %collective-permute-start.5) | collective-permute-done | bytes 204832 | tf_op jit(solution)/shard_map/ppermute | solution.py:39
  111.8 0.0 copy-done.12
  111.8 0.0 copy-done.13
  111.8 0.0 copy-done.14
  111.8 3.0 %collective-permute-start.4 = (bf16[32,3200]{1,0:T(8,128)(2,1)S(1)}, bf16[32,3200]{1,0:T(8,128)(2,1)S(1)}, u32[]{:S(2)}, u32[]{:S(2)}) collective-permute-start(bf16[32,3200]{1,0:T(8,128)(2,1)S(1)} %collective-permute-done.2.refs_3_), channel_id=1, source_target_pairs={{0,32},{32,64},{64,96},{96,112},{112,80},{80,48},{48,16},{16,0},{1... | collective-permute-start | bytes 614408 | tf_op jit(solution)/shard_map/ppermute | solution.py:38
  114.8 6.0 %collective-permute-done.4.refs_5_ = bf16[32,3200]{1,0:T(8,128)(2,1)S(1)} collective-permute-done((bf16[32,3200]{1,0:T(8,128)(2,1)S(1)}, bf16[32,3200]{1,0:T(8,128)(2,1)S(1)}, u32[]{:S(2)}, u32[]{:S(2)}) %collective-permute-start.4) | collective-permute-done | bytes 204832 | tf_op jit(solution)/shard_map/ppermute | solution.py:38
  120.9 6.5 %collective-permute-start.7 = (bf16[16,3200]{1,0:T(8,128)(2,1)S(1)}, bf16[16,3200]{1,0:T(8,128)(2,1)S(1)}, u32[]{:S(2)}, u32[]{:S(2)}) collective-permute-start(bf16[16,3200]{1,0:T(8,128)(2,1)S(1)} %slice.13), channel_id=1, source_target_pairs={{0,16},{32,0},{64,32},{96,64},{112,96},{80,112},{48,80},{16,48},{1... | collective-permute-start | bytes 307208 | tf_op jit(solution)/shard_map/ppermute | solution.py:43
  127.3 0.0 collective-permute-done.8.refs_10_
  127.4 1.9 collective-permute-start.6
  129.3 0.3 collective-permute-done.7.refs_8_
  129.6 5.3 %collective-permute-done.6.refs_7_ = bf16[16,3200]{1,0:T(8,128)(2,1)S(1)} collective-permute-done((bf16[16,3200]{1,0:T(8,128)(2,1)S(1)}, bf16[16,3200]{1,0:T(8,128)(2,1)S(1)}, u32[]{:S(2)}, u32[]{:S(2)}) %collective-permute-start.6) | collective-permute-done | bytes 102432 | tf_op jit(solution)/shard_map/ppermute | solution.py:42
  134.8 0.0 collective-permute-done.14.refs_16_
  134.8 0.0 collective-permute-done.10.refs_12_
  134.9 0.6 copy-done.17
  135.5 0.3 copy-done.7
  135.7 0.9 copy-done.8
  136.7 0.0 collective-permute-done.12.refs_14_
  136.7 0.0 all-to-all-done.2.refs_17_
  136.7 1.4 copy-done
  138.1 8.7 %contract.1 = f32[2048,128]{1,0:T(8,128)} custom-call(bf16[32,3200]{1,0:T(8,128)(2,1)} %bitcast.31, bf16[32,3200]{1,0:T(8,128)(2,1)} %copy-done.13, bf16[32,3200]{1,0:T(8,128)(2,1)} %copy-done.12, bf16[32,3200]{1,0:T(8,128)(2,1)} %copy-done.15, bf16[32,3200]{1,0:T(8,128)(2,1)} %copy-done.14, bf16[32,3200]{1,0:T(8,128)(2,1)} %copy-done.11, ...), custom_call_target="tpu_custom_call" | custom-call | flops 1677721600 | bytes 8388608 | tf_op jit(solution)/shard_map/contract/pallas_call | solution.py:87
  146.9 19.9 %all_to_all.25 = f32[16,128,128]{2,1,0:T(8,128)} all-to-all(f32[16,128,128]{2,1,0:T(8,128)} %bitcast.24), channel_id=1, replica_groups=mesh['x'=4,'zl'=8,'c'=2,'y'=4,'zh'=2] {'x','y'}, dimensions={0} | all-to-all | bytes 2097152 | tf_op jit(solution)/shard_map/all_to_all | solution.py:27
  166.7 1.9 regroup.1
  168.6 22.1 %all_to_all.26 = f32[16,8,128]{2,1,0:T(8,128)S(1)} all-to-all(f32[16,8,128]{2,1,0:T(8,128)} %bitcast.32), channel_id=1, replica_groups=mesh['x'=4,'zl'=8,'c'=2,'y'=4,'zh'=2] {'zh','zl'}, dimensions={0} | all-to-all | bytes 131072 | tf_op jit(solution)/shard_map/all_to_all | solution.py:27
  190.8 1.9 convolution_bitcast_fusion
  192.7 0.7 copy.8
  (28 shorter events, 0.1 us)
Async XLA Ops:
  0.8 17.2 %collective-permute-start.15 = (bf16[144,128]{1,0:T(8,128)(2,1)S(1)}, bf16[144,128]{1,0:T(8,128)(2,1)S(1)}, u32[]{:S(2)}, u32[]{:S(2)}) collective-permute-start(bf16[144,128]{1,0:T(8,128)(2,1)S(1)} %pad_dynamic-slice_fusion.4), channel_id=1, source_target_pairs={{0,1},{1,0},{2,3},{3,2},{4,5},{5,4},{6,7},{7,6},{8,9},{9,8},{10,11... | collective-permute-start | bytes 110600 | tf_op jit(solution)/shard_map/ppermute | solution.py:23
  18.8 12.2 %all-to-all-start.1 = ((bf16[8,144,128]{2,1,0:T(8,128)(2,1)}), bf16[8,144,128]{2,1,0:T(8,128)(2,1)S(1)}, u32[]{:S(2)}, u32[]{:S(2)}) async-start(bf16[8,144,128]{2,1,0:T(8,128)(2,1)} %broadcast_in_dim.6), calls=%async_computation.1 | async-start | bytes 589824 | tf_op jit(solution)/shard_map/all_to_all | solution.py:27
  31.0 9.7 %all-to-all-start = ((bf16[4,8,3200]{2,1,0:T(8,128)(2,1)}), bf16[4,8,3200]{2,1,0:T(8,128)(2,1)S(1)}, u32[]{:S(2)}, u32[]{:S(2)}) async-start(bf16[4,8,3200]{2,1,0:T(8,128)(2,1)} %bitcast.2), calls=%async_computation | async-start | bytes 409600 | tf_op jit(solution)/shard_map/all_to_all | solution.py:27
  40.7 22.1 %copy-start.9 = (bf16[4,8,3200]{2,1,0:T(8,128)(2,1)}, bf16[4,8,3200]{2,1,0:T(8,128)(2,1)S(1)}, u32[]{:S(2)}) copy-start(bf16[4,8,3200]{2,1,0:T(8,128)(2,1)S(1)} %all-to-all-done) | copy-start | bytes 614404
  42.4 94.3 %all-to-all-start.2 = ((bf16[4,2,1152,128]{3,2,1,0:T(8,128)(2,1)}), bf16[4,2,1152,128]{3,2,1,0:T(8,128)(2,1)S(1)}, u32[]{:S(2)}, u32[]{:S(2)}) async-start(bf16[4,2,1152,128]{3,2,1,0:T(8,128)(2,1)} %broadcast_in_dim.7), calls=%async_computation.2 | async-start | bytes 4718592 | tf_op jit(solution)/shard_map/all_to_all | solution.py:27
  50.3 86.4 %copy-start.2 = (bf16[3200,125]{1,0:T(8,128)(2,1)}, bf16[3200,125]{1,0:T(8,128)(2,1)S(1)}, u32[]{:S(2)}) copy-start(bf16[3200,125]{1,0:T(8,128)(2,1)S(1)} %get-tuple-element.8.refs_9_) | copy-start | bytes 2400004
  50.3 26.1 %collective-permute-start.13 = (bf16[3200,125]{1,0:T(8,128)(2,1)S(1)}, bf16[3200,125]{1,0:T(8,128)(2,1)S(1)}, u32[]{:S(2)}, u32[]{:S(2)}) collective-permute-start(bf16[3200,125]{1,0:T(8,128)(2,1)S(1)} %get-tuple-element.5), channel_id=1, source_target_pairs={{0,256},{128,384},{256,0},{384,128},{1,257},{129,385},{257,1},{385... | collective-permute-start | bytes 2400008 | tf_op jit(solution)/shard_map/ppermute | solution.py:140
  52.8 36.6 %collective-permute-start.9 = (bf16[3200,125]{1,0:T(8,128)(2,1)S(1)}, bf16[3200,125]{1,0:T(8,128)(2,1)S(1)}, u32[]{:S(2)}, u32[]{:S(2)}) collective-permute-start(bf16[3200,125]{1,0:T(8,128)(2,1)S(1)} %get-tuple-element.6), channel_id=1, source_target_pairs={{0,128},{128,256},{256,384},{384,0},{1,129},{129,257},{257,385},{3... | collective-permute-start | bytes 2400008 | tf_op jit(solution)/shard_map/ppermute | solution.py:140
  56.1 35.2 %collective-permute-start.11 = (bf16[3200,125]{1,0:T(8,128)(2,1)S(1)}, bf16[3200,125]{1,0:T(8,128)(2,1)S(1)}, u32[]{:S(2)}, u32[]{:S(2)}) collective-permute-start(bf16[3200,125]{1,0:T(8,128)(2,1)S(1)} %get-tuple-element.7), channel_id=1, source_target_pairs={{0,384},{128,0},{256,128},{384,256},{1,385},{129,1},{257,129},{385... | collective-permute-start | bytes 2400008 | tf_op jit(solution)/shard_map/ppermute | solution.py:140
  59.9 9.8 %collective-permute-start.1 = (bf16[32,3200]{1,0:T(8,128)(2,1)S(1)}, bf16[32,3200]{1,0:T(8,128)(2,1)S(1)}, u32[]{:S(2)}, u32[]{:S(2)}) collective-permute-start(bf16[32,3200]{1,0:T(8,128)(2,1)S(1)} %bitcast.29), channel_id=1, source_target_pairs={{0,16},{32,0},{64,32},{96,64},{112,96},{80,112},{48,80},{16,48},{1... | collective-permute-start | bytes 614408 | tf_op jit(solution)/shard_map/ppermute | solution.py:39
  62.8 11.6 %collective-permute-start = (bf16[32,3200]{1,0:T(8,128)(2,1)S(1)}, bf16[32,3200]{1,0:T(8,128)(2,1)S(1)}, u32[]{:S(2)}, u32[]{:S(2)}) collective-permute-start(bf16[32,3200]{1,0:T(8,128)(2,1)S(1)} %bitcast.30), channel_id=1, source_target_pairs={{0,32},{32,64},{64,96},{96,112},{112,80},{80,48},{48,16},{16,0},{1... | collective-permute-start | bytes 614408 | tf_op jit(solution)/shard_map/ppermute | solution.py:38
  69.7 42.1 %copy-start.12 = (bf16[32,3200]{1,0:T(8,128)(2,1)}, bf16[32,3200]{1,0:T(8,128)(2,1)S(1)}, u32[]{:S(2)}) copy-start(bf16[32,3200]{1,0:T(8,128)(2,1)S(1)} %collective-permute-done.1.refs_2_) | copy-start | bytes 614404
  69.7 24.0 %collective-permute-start.3 = (bf16[32,3200]{1,0:T(8,128)(2,1)S(1)}, bf16[32,3200]{1,0:T(8,128)(2,1)S(1)}, u32[]{:S(2)}, u32[]{:S(2)}) collective-permute-start(bf16[32,3200]{1,0:T(8,128)(2,1)S(1)} %collective-permute-done.1.refs_2_), channel_id=1, source_target_pairs={{0,16},{32,0},{64,32},{96,64},{112,96},{80,112},{48,80},{16,48},{1... | collective-permute-start | bytes 614408 | tf_op jit(solution)/shard_map/ppermute | solution.py:39
  74.4 37.3 %copy-start.13 = (bf16[32,3200]{1,0:T(8,128)(2,1)}, bf16[32,3200]{1,0:T(8,128)(2,1)S(1)}, u32[]{:S(2)}) copy-start(bf16[32,3200]{1,0:T(8,128)(2,1)S(1)} %collective-permute-done.refs_1_) | copy-start | bytes 614404
  74.4 52.9 %collective-permute-start.8 = (bf16[3200,125]{1,0:T(8,128)(2,1)S(1)}, bf16[3200,125]{1,0:T(8,128)(2,1)S(1)}, u32[]{:S(2)}, u32[]{:S(2)}) collective-permute-start(bf16[3200,125]{1,0:T(8,128)(2,1)S(1)} %get-tuple-element.8.refs_9_), channel_id=1, source_target_pairs={{0,8},{8,0},{1,9},{9,1},{2,10},{10,2},{3,11},{11,3},{4,12},{12,4},... | collective-permute-start | bytes 2400008 | tf_op jit(solution)/shard_map/ppermute | solution.py:23
  76.4 58.4 %copy-start.3 = (bf16[3200,125]{1,0:T(8,128)(2,1)}, bf16[3200,125]{1,0:T(8,128)(2,1)S(1)}, u32[]{:S(2)}) copy-start(bf16[3200,125]{1,0:T(8,128)(2,1)S(1)} %collective-permute-done.13.refs_15_) | copy-start | bytes 2400004
  76.4 58.4 %collective-permute-start.14 = (bf16[3200,125]{1,0:T(8,128)(2,1)S(1)}, bf16[3200,125]{1,0:T(8,128)(2,1)S(1)}, u32[]{:S(2)}, u32[]{:S(2)}) collective-permute-start(bf16[3200,125]{1,0:T(8,128)(2,1)S(1)} %collective-permute-done.13.refs_15_), channel_id=1, source_target_pairs={{0,8},{8,0},{1,9},{9,1},{2,10},{10,2},{3,11},{11,3},{4,12},{12,4},... | collective-permute-start | bytes 2400008 | tf_op jit(solution)/shard_map/ppermute | solution.py:23
  89.4 45.5 %copy-start.4 = (bf16[3200,125]{1,0:T(8,128)(2,1)}, bf16[3200,125]{1,0:T(8,128)(2,1)S(1)}, u32[]{:S(2)}) copy-start(bf16[3200,125]{1,0:T(8,128)(2,1)S(1)} %collective-permute-done.9.refs_11_) | copy-start | bytes 2400004
  89.4 45.4 %collective-permute-start.10 = (bf16[3200,125]{1,0:T(8,128)(2,1)S(1)}, bf16[3200,125]{1,0:T(8,128)(2,1)S(1)}, u32[]{:S(2)}, u32[]{:S(2)}) collective-permute-start(bf16[3200,125]{1,0:T(8,128)(2,1)S(1)} %collective-permute-done.9.refs_11_), channel_id=1, source_target_pairs={{0,8},{8,0},{1,9},{9,1},{2,10},{10,2},{3,11},{11,3},{4,12},{12,4},... | collective-permute-start | bytes 2400008 | tf_op jit(solution)/shard_map/ppermute | solution.py:23
  91.3 43.5 %copy-start.5 = (bf16[3200,125]{1,0:T(8,128)(2,1)}, bf16[3200,125]{1,0:T(8,128)(2,1)S(1)}, u32[]{:S(2)}) copy-start(bf16[3200,125]{1,0:T(8,128)(2,1)S(1)} %collective-permute-done.11.refs_13_) | copy-start | bytes 2400004
  91.3 45.3 %collective-permute-start.12 = (bf16[3200,125]{1,0:T(8,128)(2,1)S(1)}, bf16[3200,125]{1,0:T(8,128)(2,1)}, u32[]{:S(2)}, u32[]{:S(2)}) collective-permute-start(bf16[3200,125]{1,0:T(8,128)(2,1)S(1)} %collective-permute-done.11.refs_13_), channel_id=1, source_target_pairs={{0,8},{8,0},{1,9},{9,1},{2,10},{10,2},{3,11},{11,3},{4,12},{12,4},... | collective-permute-start | bytes 2400008 | tf_op jit(solution)/shard_map/ppermute | solution.py:23
  93.7 18.0 %copy-start.14 = (bf16[32,3200]{1,0:T(8,128)(2,1)}, bf16[32,3200]{1,0:T(8,128)(2,1)S(1)}, u32[]{:S(2)}) copy-start(bf16[32,3200]{1,0:T(8,128)(2,1)S(1)} %collective-permute-done.3.refs_4_) | copy-start | bytes 614404
  93.8 9.8 %collective-permute-start.2 = (bf16[32,3200]{1,0:T(8,128)(2,1)S(1)}, bf16[32,3200]{1,0:T(8,128)(2,1)S(1)}, u32[]{:S(2)}, u32[]{:S(2)}) collective-permute-start(bf16[32,3200]{1,0:T(8,128)(2,1)S(1)} %collective-permute-done.refs_1_), channel_id=1, source_target_pairs={{0,32},{32,64},{64,96},{96,112},{112,80},{80,48},{48,16},{16,0},{1... | collective-permute-start | bytes 614408 | tf_op jit(solution)/shard_map/ppermute | solution.py:38
  103.5 31.3 %copy-start.15 = (bf16[32,3200]{1,0:T(8,128)(2,1)}, bf16[32,3200]{1,0:T(8,128)(2,1)S(1)}, u32[]{:S(2)}) copy-start(bf16[32,3200]{1,0:T(8,128)(2,1)S(1)} %collective-permute-done.2.refs_3_) | copy-start | bytes 614404
  103.5 8.2 %collective-permute-start.5 = (bf16[32,3200]{1,0:T(8,128)(2,1)S(1)}, bf16[32,3200]{1,0:T(8,128)(2,1)S(1)}, u32[]{:S(2)}, u32[]{:S(2)}) collective-permute-start(bf16[32,3200]{1,0:T(8,128)(2,1)S(1)} %collective-permute-done.3.refs_4_), channel_id=1, source_target_pairs={{0,16},{32,0},{64,32},{96,64},{112,96},{80,112},{48,80},{16,48},{1... | collective-permute-start | bytes 614408 | tf_op jit(solution)/shard_map/ppermute | solution.py:39
  111.8 24.9 %copy-start.10 = (bf16[32,3200]{1,0:T(8,128)(2,1)}, bf16[32,3200]{1,0:T(8,128)(2,1)S(1)}, u32[]{:S(2)}) copy-start(bf16[32,3200]{1,0:T(8,128)(2,1)S(1)} %collective-permute-done.5.refs_6_) | copy-start | bytes 614404
  111.8 9.1 %collective-permute-start.4 = (bf16[32,3200]{1,0:T(8,128)(2,1)S(1)}, bf16[32,3200]{1,0:T(8,128)(2,1)S(1)}, u32[]{:S(2)}, u32[]{:S(2)}) collective-permute-start(bf16[32,3200]{1,0:T(8,128)(2,1)S(1)} %collective-permute-done.2.refs_3_), channel_id=1, source_target_pairs={{0,32},{32,64},{64,96},{96,112},{112,80},{80,48},{48,16},{16,0},{1... | collective-permute-start | bytes 614408 | tf_op jit(solution)/shard_map/ppermute | solution.py:38
  120.9 14.0 %copy-start.11 = (bf16[32,3200]{1,0:T(8,128)(2,1)}, bf16[32,3200]{1,0:T(8,128)(2,1)S(1)}, u32[]{:S(2)}) copy-start(bf16[32,3200]{1,0:T(8,128)(2,1)S(1)} %collective-permute-done.4.refs_5_) | copy-start | bytes 614404
  120.9 8.7 %collective-permute-start.7 = (bf16[16,3200]{1,0:T(8,128)(2,1)S(1)}, bf16[16,3200]{1,0:T(8,128)(2,1)S(1)}, u32[]{:S(2)}, u32[]{:S(2)}) collective-permute-start(bf16[16,3200]{1,0:T(8,128)(2,1)S(1)} %slice.13), channel_id=1, source_target_pairs={{0,16},{32,0},{64,32},{96,64},{112,96},{80,112},{48,80},{16,48},{1... | collective-permute-start | bytes 307208 | tf_op jit(solution)/shard_map/ppermute | solution.py:43
  127.4 7.5 %copy-start.6 = (bf16[3200,125]{1,0:T(8,128)(2,1)}, bf16[3200,125]{1,0:T(8,128)(2,1)S(1)}, u32[]{:S(2)}) copy-start(bf16[3200,125]{1,0:T(8,128)(2,1)S(1)} %collective-permute-done.8.refs_10_) | copy-start | bytes 2400004
  127.4 7.5 %collective-permute-start.6 = (bf16[16,3200]{1,0:T(8,128)(2,1)S(1)}, bf16[16,3200]{1,0:T(8,128)(2,1)S(1)}, u32[]{:S(2)}, u32[]{:S(2)}) collective-permute-start(bf16[16,3200]{1,0:T(8,128)(2,1)S(1)} %slice.12), channel_id=1, source_target_pairs={{0,32},{32,64},{64,96},{96,112},{112,80},{80,48},{48,16},{16,0},{1... | collective-permute-start | bytes 307208 | tf_op jit(solution)/shard_map/ppermute | solution.py:42
  129.6 7.1 %copy-start.16 = (bf16[16,3200]{1,0:T(8,128)(2,1)}, bf16[16,3200]{1,0:T(8,128)(2,1)S(1)}, u32[]{:S(2)}) copy-start(bf16[16,3200]{1,0:T(8,128)(2,1)S(1)} %collective-permute-done.7.refs_8_) | copy-start | bytes 307204
  134.8 0.6 copy-start.17
  134.8 0.9 copy-start.7
  135.7 0.9 copy-start.8
  136.7 1.4 copy-start
  146.8 43.9 %copy-start.1 = (bf16[4,2,1152,128]{3,2,1,0:T(8,128)(2,1)S(1)}, bf16[4,2,1152,128]{3,2,1,0:T(8,128)(2,1)}, u32[]{:S(2)}) copy-start(bf16[4,2,1152,128]{3,2,1,0:T(8,128)(2,1)} %copy-done) | copy-start | bytes 7077892

commit v2 on v1

v2 whole, which is shorter than its diff:
```python
import jax
import jax.numpy as jnp
from jax import lax
from jax.experimental import pallas as pl
from jax.experimental.pallas import tpu as pltpu
from jax.sharding import Mesh
from jax.sharding import PartitionSpec as P


AXES = ("x", "zl", "c", "y", "zh")
X, ZL, C, Y, ZH = 4, 8, 2, 4, 2
FOLD = (0, 2, 4, 6, 7, 5, 3, 1)
STEPS = (0, -1, 1, -2, 2, -3, 3, 4)
PAIR = [(0, 1), (1, 0), (2, 3), (3, 2)]
CROSS = [(1, 2), (2, 1), (3, 0), (0, 3)]
LANES = 128
BLOCK = 10 * LANES
PIECES = 4


def fold_ring(step):
    return [(FOLD[i], FOLD[(i + step) % ZL]) for i in range(ZL)]


def swap(shard, axis):
    return lax.ppermute(shard, axis, [(0, 1), (1, 0)])


def exchange(shard, axes):
    return lax.all_to_all(shard, axes, split_axis=0, concat_axis=0, tiled=True)


def gathered(shard, axes, count):
    return exchange(jnp.broadcast_to(shard[None], (count,) + shard.shape), axes)


def ring_gather(piece):
    parts = [piece]
    up, down = piece, piece
    for _ in range(1, ZL // 2):
        up = lax.ppermute(up, "zl", fold_ring(1))
        down = lax.ppermute(down, "zl", fold_ring(-1))
        parts += [up, down]
    half = piece.shape[0] // 2
    first = lax.ppermute(up[:half], "zl", fold_ring(1))
    second = lax.ppermute(down[half:], "zl", fold_ring(-1))
    return parts + [first, second]


def ring_source(step):
    here = lax.axis_index("zl")
    place = jnp.where(lax.rem(here, 2) == 0, here // 2, (2 * ZL - 1 - here) // 2)
    place = lax.rem(place + step + ZL, ZL)
    return jnp.where(place < ZL // 2, 2 * place, 2 * ZL - 1 - 2 * place)


def contract_kernel(*refs):
    own, cross, (a, b, c, d, _, out, acc) = refs[: ZL + 1], refs[ZL + 1 : ZL + 4], refs[ZL + 4 :]
    index = pl.program_id(0)
    here = lax.axis_index("x")

    @pl.when(index == 0)
    def _():
        acc[...] = jnp.zeros_like(acc)

    own = jnp.concatenate([part[...] for part in own], axis=0)
    cross = jnp.concatenate([part[...] for part in cross], axis=0)
    low = here < X // 2
    left = jnp.concatenate([jnp.where(low, own, cross), jnp.where(low, cross, own)], axis=0)
    even = lax.rem(here, 2) == 0
    one = jnp.concatenate([a[...], b[...]], axis=1)
    two = jnp.concatenate([c[...], d[...]], axis=1)
    for slot, right in enumerate((jnp.where(even, one, two), jnp.where(even, two, one))):
        both = jnp.dot(left, right, preferred_element_type=jnp.float32)
        acc[2 * slot] += both[:, :LANES]
        acc[2 * slot + 1] += both[:, LANES:]

    @pl.when(index == pl.num_programs(0) - 1)
    def _():
        for piece in range(PIECES):
            for half in range(2):
                for slot in range(ZL):
                    for owner in range(ZH):
                        got = acc[piece, pl.ds((half * ZL + slot) * 16 + owner, 8, stride=2), :]
                        start = half * 512 + (slot * ZH + owner) * PIECES + piece
                        out[pl.ds(start, 8, stride=ZL * ZH * PIECES), :] = got


def contract(own, cross, pieces, ready):
    inner = own[0].shape[1]
    columns = X * ZL * own[0].shape[0] // 2
    lefts = [pl.BlockSpec((part.shape[0], BLOCK), lambda k: (0, k)) for part in own + cross]
    rights = [pl.BlockSpec((BLOCK, LANES), lambda k: (k, 0))] * len(pieces)
    return pl.pallas_call(
        contract_kernel,
        grid=(inner // BLOCK,),
        out_shape=jax.ShapeDtypeStruct((columns * PIECES, LANES), jnp.float32),
        in_specs=lefts + rights + [pl.BlockSpec(memory_space=pl.ANY)],
        out_specs=pl.BlockSpec((columns * PIECES, LANES), lambda k: (0, 0)),
        scratch_shapes=[pltpu.VMEM((PIECES, columns, LANES), jnp.float32)],
        cost_estimate=pl.CostEstimate(
            flops=2 * columns * inner * PIECES * LANES, bytes_accessed=10 << 20, transcendentals=0
        ),
        name="contract",
    )(*own, *cross, *pieces, ready)


def regroup_kernel(got, out):
    for slot in range(ZL):
        target = ring_source(STEPS[slot])
        for pair in range(2):
            total = got[pair * 2 * Y, slot]
            for source in range(pair * 2 * Y + 1, (pair + 1) * 2 * Y):
                total += got[source, slot]
            for owner in range(ZH):
                out[owner, target, pair * PIECES : (pair + 1) * PIECES, :] = total[
                    owner * PIECES : (owner + 1) * PIECES
                ]


def regroup(got):
    return pl.pallas_call(
        regroup_kernel,
        out_shape=jax.ShapeDtypeStruct((ZH, ZL, 2 * X, LANES), jnp.float32),
        cost_estimate=pl.CostEstimate(flops=1 << 17, bytes_accessed=1 << 19, transcendentals=0),
        name="regroup",
    )(got)


def on_device(density, chol_vectors, virt_coef):
    rows, inner = density.shape
    width = chol_vectors.shape[1]
    virt_rows, nao = virt_coef.shape
    here, core, half = lax.axis_index("x"), lax.axis_index("c"), lax.axis_index("zh")
    even = lax.rem(here, 2) == 0
    depth = -(-inner // (2 * BLOCK)) * BLOCK
    pad = 2 * depth - inner
    keep = lax.rem((here + 1) // 2, 2)
    keep, give = keep * depth, (1 - keep) * depth

    vectors = jnp.pad(chol_vectors.T, ((0, 0), (0, pad)))
    mine = lax.dynamic_slice(vectors, (0, keep), (width, depth))
    sent = lax.dynamic_slice(vectors, (0, give), (width, depth))
    got = lax.ppermute(sent, "x", PAIR)
    chunk = jnp.concatenate([jnp.where(even, mine, got), jnp.where(even, got, mine)], axis=0)
    own = ring_gather(chunk)
    cross = [
        lax.ppermute(jnp.concatenate(own[first:last], axis=0), "x", CROSS)
        for first, last in ((0, 3), (3, 5), (5, 9))
    ]

    dens = jnp.pad(density.T, ((0, pad), (0, LANES - rows)))
    kept = lax.dynamic_slice(dens, (keep, 0), (depth, LANES))
    other = lax.ppermute(lax.dynamic_slice(dens, (give, 0), (depth, LANES)), "x", PAIR)
    pieces = [kept, swap(kept, "c"), other, swap(other, "c")]

    coef = virt_coef.T
    part = -(-nao // (X * C * 16)) * 16
    coef = jnp.pad(coef, ((0, X * C * part - nao), (0, LANES - virt_rows)))
    far = lax.dynamic_slice(coef, ((here * C + core) * part, 0), (part, LANES))
    far = swap(far, "zh")
    far = gathered(far, ("x", "c"), X * C).reshape(X * C * part, LANES)
    pair = jnp.where(half == core, jnp.stack([coef, far]), jnp.stack([far, coef]))
    coefs = gathered(pair, "y", Y)

    gamma = contract(own, cross, pieces, coefs[0, 0, :16])
    gamma = exchange(gamma.reshape(X * Y, ZL * ZH * PIECES, LANES), ("x", "y"))
    gamma = regroup(gamma.reshape(X * Y, ZL, ZH * PIECES, LANES))
    gamma = exchange(gamma.reshape(ZH * ZL, 2 * X, LANES), ("zh", "zl"))
    gamma = jnp.sum(gamma.reshape(ZH, 2, ZL // 2, X, 2, LANES), axis=0)
    gamma = gamma.transpose(2, 0, 1, 3, 4).reshape(2 * X, ZL // 2 * 2, LANES)
    out = jnp.einsum(
        "ibr,bnr->in",
        gamma,
        coefs.reshape(2 * Y, X * C * part, LANES).astype(jnp.float32),
        precision=lax.Precision.HIGHEST,
    )
    return out[:, None, :nao]


def solution(mesh):
    split = Mesh(mesh.devices.reshape(X, ZL, C, Y, ZH), AXES)
    return jax.shard_map(
        on_device,
        mesh=split,
        in_specs=(P(("x", "zl", "c"), ("y", "zh")), P(("y", "zh"), ("x", "zl", "c")), P(("y", "zh"), None)),
        out_specs=P(None, AXES, None),
        check_vma=False,
    )
```

time: 195 us -> 178 us (0.913)
  waiting for transfers between devices: 50.4 us -> 35.6 us
  local copies, waits for them, and re-layouts: 13.3 us -> 10.2 us
  other arithmetic: 0.13 us -> 2.97 us
    ppermute x3, waiting for transfers between devices: 12.6 us -> 0.01 us  [ring_gather(): up = lax.ppermute(up, 'zl', fold_ring(1))]
    ppermute x3 -> x5, waiting for transfers between devices: 10.6 us -> 19.8 us  [the longest x3 19.8 us: on_device(): lax.ppermute(jnp.concatenate(own[first:last], axis=0), 'x', CROSS)]
    ppermute x3 -> x5, starting transfers between devices: 9.59 us -> 18.5 us  [the longest x3 12.7 us: on_device(): lax.ppermute(jnp.concatenate(own[first:last], axis=0), 'x', CROSS)]
    all_to_all x3 -> x2, waiting for transfers between devices: 11.4 us -> 3.48 us  [exchange(): return lax.all_to_all(shard, axes, split_axis=0, concat_axis=0, tiled=True)]
    ppermute x5 -> x3, starting transfers between devices: 23.5 us -> 15.7 us  [swap(): return lax.ppermute(shard, axis, [(0, 1), (1, 0)])]
    ppermute x1, waiting for transfers between devices: 5.26 us -> 0.01 us  [ring_gather(): first = lax.ppermute(up[:half], 'zl', fold_ring(1))]
    ppermute x3, starting transfers between devices: 11.9 us -> 16.4 us  [ring_gather(): down = lax.ppermute(down, 'zl', fold_ring(-1))]
    all_to_all x3 -> x2, starting transfers between devices: 12.1 us -> 8.77 us  [exchange(): return lax.all_to_all(shard, axes, split_axis=0, concat_axis=0, tiled=True)]
  transfers between devices with their start and end apart: 19 -> 18, of which waited for: 10 -> 4; matrix products, arithmetic and copies ran while one was open for 3% -> 6% of each run, Pallas kernels for 0% -> 0%
where the time goes in v2:
time: 178 us; the launch traced here: 176 us
  starting transfers between devices  74.4 us (42%)
  blocking collectives  41.9 us (24%)
  waiting for transfers between devices  35.6 us (20%)
  local copies, waits for them, and re-layouts  10.2 us (6%)
  Pallas kernels  9.1 us (5%)
  other arithmetic  2.97 us (2%)
  matrix products  1.92 us (1%)
    all_to_all x2, blocking collectives, exchange(): return lax.all_to_all(shard, axes, split_axis=0, concat_axis=0, tiled=True)  41.9 us
    ppermute x3, waiting for transfers between devices, on_device(): lax.ppermute(jnp.concatenate(own[first:last], axis=0), 'x', CROSS)  19.8 us
    ppermute x3, starting transfers between devices, ring_gather(): down = lax.ppermute(down, 'zl', fold_ring(-1))  16.4 us
    ppermute x3, starting transfers between devices, swap(): return lax.ppermute(shard, axis, [(0, 1), (1, 0)])  15.7 us
    ppermute x3, starting transfers between devices, on_device(): lax.ppermute(jnp.concatenate(own[first:last], axis=0), 'x', CROSS)  12.7 us
    all_to_all x2, starting transfers between devices, exchange(): return lax.all_to_all(shard, axes, split_axis=0, concat_axis=0, tiled=True)  8.77 us
    ppermute x3, starting transfers between devices, ring_gather(): up = lax.ppermute(up, 'zl', fold_ring(1))  7.94 us
    pallas_call x1, Pallas kernels, contract(): pl.pallas_call(contract_kernel, grid=(inner // BLOCK,), out_shape=jax.Sha...  7.39 us
  transfers between devices with their start and end apart: 18, of which 4 were waited for; matrix products, arithmetic and copies ran while one was open for 6% of the time, Pallas kernels for 0%

profile of v2, /device:TPU:32, one launch (start us, length us, event | category | flops | bytes accessed | tf_op | source)
XLA Modules:
  0.0 176.5 jit_solution(18423270857449183056)
XLA Ops:
  0.0 0.9 pad_dynamic-slice_fusion.3
  0.9 3.4 %collective-permute-start = (bf16[8,6400]{1,0:T(8,128)(2,1)S(1)}, bf16[8,6400]{1,0:T(8,128)(2,1)S(1)}, u32[]{:S(2)}, u32[]{:S(2)}) collective-permute-start(bf16[8,6400]{1,0:T(8,128)(2,1)S(1)} %pad_dynamic-slice_fusion.3), channel_id=1, source_target_pairs={{0,128},{128,0},{256,384},{384,256},{1,129},{129,1},{257,385},{385... | collective-permute-start | bytes 307208 | tf_op jit(solution)/shard_map/ppermute | solution.py:144
  4.4 0.0 copy-start.6
  4.4 0.0 copy-start.2
  4.4 5.3 %pad_dynamic-slice_fusion = (bf16[6400,128]{1,0:T(8,128)(2,1)}, bf16[6400,128]{1,0:T(8,128)(2,1)}) fusion(s32[]{:T(128)S(6)} %select_n.43, bf16[12500,125]{1,0:T(8,128)(2,1)} %bitcast.21, s32[]{:T(128)S(6)} %select_n.42), kind=kLoop, calls=%fused_computation | loop fusion | bytes 6401808 | tf_op jit(solution)/shard_map/dynamic_slice | solution.py:154
  9.7 2.4 %collective-permute-start.13 = (bf16[6400,128]{1,0:T(8,128)(2,1)}, bf16[6400,128]{1,0:T(8,128)(2,1)}, u32[]{:S(2)}, u32[]{:S(2)}) collective-permute-start(bf16[6400,128]{1,0:T(8,128)(2,1)} %get-tuple-element.5), channel_id=1, source_target_pairs={{0,128},{128,0},{256,384},{384,256},{1,129},{129,1},{257,385},{385... | collective-permute-start | bytes 4915208 | tf_op jit(solution)/shard_map/ppermute | solution.py:154
  12.1 0.0 collective-permute-done
  12.1 0.0 copy-done.6
  12.1 0.1 broadcast_select_fusion.1
  12.2 5.2 %collective-permute-start.2 = (bf16[16,6400]{1,0:T(8,128)(2,1)S(1)}, bf16[16,6400]{1,0:T(8,128)(2,1)S(1)}, u32[]{:S(2)}, u32[]{:S(2)}) collective-permute-start(bf16[16,6400]{1,0:T(8,128)(2,1)S(1)} %pad_maximum_fusion.3.refs_0_), channel_id=1, source_target_pairs={{0,16},{32,0},{64,32},{96,64},{112,96},{80,112},{48,80},{16,48},{1... | collective-permute-start | bytes 614408 | tf_op jit(solution)/shard_map/ppermute | solution.py:42
  17.4 4.1 %collective-permute-start.1 = (bf16[16,6400]{1,0:T(8,128)(2,1)S(1)}, bf16[16,6400]{1,0:T(8,128)(2,1)S(1)}, u32[]{:S(2)}, u32[]{:S(2)}) collective-permute-start(bf16[16,6400]{1,0:T(8,128)(2,1)S(1)} %pad_maximum_fusion.3.refs_0_), channel_id=1, source_target_pairs={{0,32},{32,64},{64,96},{96,112},{112,80},{80,48},{48,16},{16,0},{1... | collective-permute-start | bytes 614408 | tf_op jit(solution)/shard_map/ppermute | solution.py:41
  21.5 0.0 copy-done.2
  21.6 11.4 %collective-permute-start.15 = (bf16[144,128]{1,0:T(8,128)(2,1)S(1)}, bf16[144,128]{1,0:T(8,128)(2,1)S(1)}, u32[]{:S(2)}, u32[]{:S(2)}) collective-permute-start(bf16[144,128]{1,0:T(8,128)(2,1)S(1)} %pad_dynamic-slice_fusion.2), channel_id=1, source_target_pairs={{0,1},{1,0},{2,3},{3,2},{4,5},{5,4},{6,7},{7,6},{8,9},{9,8},{10,11... | collective-permute-start | bytes 110600 | tf_op jit(solution)/shard_map/ppermute | solution.py:26
  33.0 5.4 %collective-permute-done.15 = bf16[144,128]{1,0:T(8,128)(2,1)S(1)} collective-permute-done((bf16[144,128]{1,0:T(8,128)(2,1)S(1)}, bf16[144,128]{1,0:T(8,128)(2,1)S(1)}, u32[]{:S(2)}, u32[]{:S(2)}) %collective-permute-start.15) | collective-permute-done | bytes 36896 | tf_op jit(solution)/shard_map/ppermute | solution.py:26
  38.4 0.8 broadcast_in_dim.6
  39.1 4.3 %all-to-all-start = ((bf16[8,144,128]{2,1,0:T(8,128)(2,1)}), bf16[8,144,128]{2,1,0:T(8,128)(2,1)S(1)}, u32[]{:S(2)}, u32[]{:S(2)}) async-start(bf16[8,144,128]{2,1,0:T(8,128)(2,1)} %broadcast_in_dim.6), calls=%async_computation | async-start | bytes 589824 | tf_op jit(solution)/shard_map/all_to_all | solution.py:30
  43.4 2.4 %collective-permute-start.12 = (bf16[6400,128]{1,0:T(8,128)(2,1)}, bf16[6400,128]{1,0:T(8,128)(2,1)}, u32[]{:S(2)}, u32[]{:S(2)}) collective-permute-start(bf16[6400,128]{1,0:T(8,128)(2,1)} %get-tuple-element.6.refs_12_), channel_id=1, source_target_pairs={{0,8},{8,0},{1,9},{9,1},{2,10},{10,2},{3,11},{11,3},{4,12},{12,4},... | collective-permute-start | bytes 4915208 | tf_op jit(solution)/shard_map/ppermute | solution.py:26
  45.8 0.0 collective-permute-done.2.refs_2_
  45.9 0.0 copy-start.3
  45.9 5.8 %collective-permute-start.4 = (bf16[16,6400]{1,0:T(8,128)(2,1)S(1)}, bf16[16,6400]{1,0:T(8,128)(2,1)}, u32[]{:S(2)}, u32[]{:S(2)}) collective-permute-start(bf16[16,6400]{1,0:T(8,128)(2,1)S(1)} %collective-permute-done.2.refs_2_), channel_id=1, source_target_pairs={{0,16},{32,0},{64,32},{96,64},{112,96},{80,112},{48,80},{16,48},{1... | collective-permute-start | bytes 614408 | tf_op jit(solution)/shard_map/ppermute | solution.py:42
  51.7 0.0 collective-permute-done.1.refs_1_
  51.7 0.0 copy-done.5
  51.7 0.0 copy-start.4
  51.7 1.9 %collective-permute-start.3 = (bf16[16,6400]{1,0:T(8,128)(2,1)S(1)}, bf16[16,6400]{1,0:T(8,128)(2,1)}, u32[]{:S(2)}, u32[]{:S(2)}) collective-permute-start(bf16[16,6400]{1,0:T(8,128)(2,1)S(1)} %collective-permute-done.1.refs_1_), channel_id=1, source_target_pairs={{0,32},{32,64},{64,96},{96,112},{112,80},{80,48},{48,16},{16,0},{1... | collective-permute-start | bytes 614408 | tf_op jit(solution)/shard_map/ppermute | solution.py:41
  53.6 0.1 pad_bitcast_fusion
  53.7 6.9 %collective-permute-done.4.refs_4_ = bf16[16,6400]{1,0:T(8,128)(2,1)} collective-permute-done((bf16[16,6400]{1,0:T(8,128)(2,1)S(1)}, bf16[16,6400]{1,0:T(8,128)(2,1)}, u32[]{:S(2)}, u32[]{:S(2)}) %collective-permute-start.4) | collective-permute-done | bytes 204832 | tf_op jit(solution)/shard_map/ppermute | solution.py:42
  60.6 5.4 %collective-permute-start.6 = (bf16[16,6400]{1,0:T(8,128)(2,1)}, bf16[16,6400]{1,0:T(8,128)(2,1)S(1)}, u32[]{:S(2)}, u32[]{:S(2)}) collective-permute-start(bf16[16,6400]{1,0:T(8,128)(2,1)} %collective-permute-done.4.refs_4_), channel_id=1, source_target_pairs={{0,16},{32,0},{64,32},{96,64},{112,96},{80,112},{48,80},{16,48},{1... | collective-permute-start | bytes 614408 | tf_op jit(solution)/shard_map/ppermute | solution.py:42
  66.0 0.0 collective-permute-done.3.refs_3_
  66.0 1.9 %collective-permute-start.5 = (bf16[16,6400]{1,0:T(8,128)(2,1)}, bf16[16,6400]{1,0:T(8,128)(2,1)S(1)}, u32[]{:S(2)}, u32[]{:S(2)}) collective-permute-start(bf16[16,6400]{1,0:T(8,128)(2,1)} %collective-permute-done.3.refs_3_), channel_id=1, source_target_pairs={{0,32},{32,64},{64,96},{96,112},{112,80},{80,48},{48,16},{16,0},{1... | collective-permute-start | bytes 614408 | tf_op jit(solution)/shard_map/ppermute | solution.py:41
  68.0 0.0 all-to-all-done
  68.0 0.1 maximum_select_fusion
  68.1 1.7 broadcast_in_dim.7
  69.8 4.5 %all-to-all-start.1 = ((bf16[4,2,1152,128]{3,2,1,0:T(8,128)(2,1)}), bf16[4,2,1152,128]{3,2,1,0:T(8,128)(2,1)S(1)}, u32[]{:S(2)}, u32[]{:S(2)}) async-start(bf16[4,2,1152,128]{3,2,1,0:T(8,128)(2,1)} %broadcast_in_dim.7), calls=%async_computation.1 | async-start | bytes 4718592 | tf_op jit(solution)/shard_map/all_to_all | solution.py:30
  74.3 0.0 collective-permute-done.6.refs_6_
  74.3 5.2 %collective-permute-start.8 = (bf16[8,6400]{1,0:T(8,128)(2,1)S(1)}, bf16[8,6400]{1,0:T(8,128)(2,1)S(1)}, u32[]{:S(2)}, u32[]{:S(2)}) collective-permute-start(bf16[8,6400]{1,0:T(8,128)(2,1)S(1)} %slice.17), channel_id=1, source_target_pairs={{0,16},{32,0},{64,32},{96,64},{112,96},{80,112},{48,80},{16,48},{1... | collective-permute-start | bytes 307208 | tf_op jit(solution)/shard_map/ppermute | solution.py:46
  79.5 0.0 collective-permute-done.5.refs_5_
  79.5 0.0 copy-start.1
  79.5 1.9 %collective-permute-start.7 = (bf16[8,6400]{1,0:T(8,128)(2,1)S(1)}, bf16[8,6400]{1,0:T(8,128)(2,1)S(1)}, u32[]{:S(2)}, u32[]{:S(2)}) collective-permute-start(bf16[8,6400]{1,0:T(8,128)(2,1)S(1)} %slice.16), channel_id=1, source_target_pairs={{0,32},{32,64},{64,96},{96,112},{112,80},{80,48},{48,16},{16,0},{1... | collective-permute-start | bytes 307208 | tf_op jit(solution)/shard_map/ppermute | solution.py:45
  81.5 0.0 copy-done.3
  81.5 0.9 pad_maximum_fusion
  82.4 5.6 %collective-permute-start.9 = (bf16[48,6400]{1,0:T(8,128)(2,1)}, bf16[48,6400]{1,0:T(8,128)(2,1)}, u32[]{:S(2)}, u32[]{:S(2)}) collective-permute-start(bf16[48,6400]{1,0:T(8,128)(2,1)} %pad_maximum_fusion), channel_id=1, source_target_pairs={{128,256},{256,128},{384,0},{0,384},{129,257},{257,129},{385,1},{1... | collective-permute-start | bytes 1843208 | tf_op jit(solution)/shard_map/ppermute | solution.py:148
  88.0 0.0 collective-permute-done.13.refs_14_
  88.0 1.9 %collective-permute-start.14 = (bf16[6400,128]{1,0:T(8,128)(2,1)}, bf16[6400,128]{1,0:T(8,128)(2,1)}, u32[]{:S(2)}, u32[]{:S(2)}) collective-permute-start(bf16[6400,128]{1,0:T(8,128)(2,1)} %collective-permute-done.13.refs_14_), channel_id=1, source_target_pairs={{0,8},{8,0},{1,9},{9,1},{2,10},{10,2},{3,11},{11,3},{4,12},{12,4},... | collective-permute-start | bytes 4915208 | tf_op jit(solution)/shard_map/ppermute | solution.py:26
  89.9 0.0 collective-permute-done.8.refs_8_
  90.0 0.0 copy-start.7
  90.0 0.0 collective-permute-done.7.refs_7_
  90.0 2.6 %collective-permute-start.11 = (bf16[48,6400]{1,0:T(8,128)(2,1)S(1)}, bf16[48,6400]{1,0:T(8,128)(2,1)}, u32[]{:S(2)}, u32[]{:S(2)}) collective-permute-start(bf16[48,6400]{1,0:T(8,128)(2,1)S(1)} %pad_maximum_fusion.1), channel_id=1, source_target_pairs={{128,256},{256,128},{384,0},{0,384},{129,257},{257,129},{385,1},{1... | collective-permute-start | bytes 1843208 | tf_op jit(solution)/shard_map/ppermute | solution.py:148
  92.7 1.8 %pad_maximum_fusion.2 = bf16[32,6400]{1,0:T(8,128)(2,1)} fusion(bf16[16,6400]{1,0:T(8,128)(2,1)} %collective-permute-done.4.refs_4_, bf16[16,6400]{1,0:T(8,128)(2,1)} %collective-permute-done.3.refs_3_), kind=kLoop, calls=%fused_computation.6 | loop fusion | flops 819200 | bytes 819200 | tf_op jit(solution)/shard_map/concatenate | solution.py:148
  94.5 0.0 copy-done
  94.5 0.0 copy-done.8
  94.5 4.4 %collective-permute-start.10 = (bf16[32,6400]{1,0:T(8,128)(2,1)}, bf16[32,6400]{1,0:T(8,128)(2,1)}, u32[]{:S(2)}, u32[]{:S(2)}) collective-permute-start(bf16[32,6400]{1,0:T(8,128)(2,1)} %pad_maximum_fusion.2), channel_id=1, source_target_pairs={{128,256},{256,128},{384,0},{0,384},{129,257},{257,129},{385,1},{1... | collective-permute-start | bytes 1228808 | tf_op jit(solution)/shard_map/ppermute | solution.py:148
  98.9 3.5 %all-to-all-done.1 = bf16[4,2,1152,128]{3,2,1,0:T(8,128)(2,1)S(1)} async-done(((bf16[4,2,1152,128]{3,2,1,0:T(8,128)(2,1)}), bf16[4,2,1152,128]{3,2,1,0:T(8,128)(2,1)S(1)}, u32[]{:S(2)}, u32[]{:S(2)}) %all-to-all-start.1) | async-done | bytes 2359328 | tf_op jit(solution)/shard_map/all_to_all | solution.py:30
  102.4 0.6 slice_bitcast_fusion.1.refs_16_
  103.0 19.8 %collective-permute-done.10.refs_10_ = bf16[32,6400]{1,0:T(8,128)(2,1)} collective-permute-done((bf16[32,6400]{1,0:T(8,128)(2,1)}, bf16[32,6400]{1,0:T(8,128)(2,1)}, u32[]{:S(2)}, u32[]{:S(2)}) %collective-permute-start.10) | collective-permute-done | bytes 409632 | tf_op jit(solution)/shard_map/ppermute | solution.py:148
  122.8 0.0 collective-permute-done.9.refs_9_
  122.8 0.0 collective-permute-done.11.refs_11_
  122.8 0.0 collective-permute-done.12.refs_13_
  122.8 0.0 collective-permute-done.14.refs_15_
  122.8 7.4 %contract.1 = f32[1024,128]{1,0:T(8,128)} custom-call(bf16[16,6400]{1,0:T(8,128)(2,1)} %copy-done.5, bf16[16,6400]{1,0:T(8,128)(2,1)} %copy-done.4, bf16[16,6400]{1,0:T(8,128)(2,1)} %copy-done.3, bf16[16,6400]{1,0:T(8,128)(2,1)} %collective-permute-done.3.refs_3_, bf16[16,6400]{1,0:T(8,128)(2,1)} %collective-permute-done.4.refs_4_, ...), custom_call_target="tpu_custom_call" | custom-call | flops 1677721600 | bytes 10485760 | tf_op jit(solution)/shard_map/contract/pallas_call | solution.py:94
  130.2 17.2 %all_to_all.20 = f32[16,64,128]{2,1,0:T(8,128)} all-to-all(f32[16,64,128]{2,1,0:T(8,128)} %bitcast.22), channel_id=1, replica_groups=mesh['x'=4,'zl'=8,'c'=2,'y'=4,'zh'=2] {'x','y'}, dimensions={0} | all-to-all | bytes 1048576 | tf_op jit(solution)/shard_map/all_to_all | solution.py:30
  147.4 1.7 regroup.1
  149.1 24.7 %all_to_all.21 = f32[16,8,128]{2,1,0:T(8,128)S(1)} all-to-all(f32[16,8,128]{2,1,0:T(8,128)} %bitcast.29), channel_id=1, replica_groups=mesh['x'=4,'zl'=8,'c'=2,'y'=4,'zh'=2] {'zh','zl'}, dimensions={0} | all-to-all | bytes 131072 | tf_op jit(solution)/shard_map/all_to_all | solution.py:30
  173.9 1.9 %convolution_bitcast_fusion = f32[8,1152]{1,0:T(8,128)S(1)} fusion(bf16[8,1152,128]{2,1,0:T(8,128)(2,1)S(1)} %bitcast.20, f32[8,8,128]{2,1,0:T(8,128)S(1)} %bitcast.31), kind=kOutput, calls=%fused_computation.2 | convolution fusion | flops 113246208 | bytes 2428928 | tf_op jit(solution)/shard_map/ibr,bnr->in/dot_general | solution.py:172
  175.8 0.7 copy.8
  (14 shorter events, 0.2 us)
Async XLA Ops:
  0.9 11.2 %collective-permute-start = (bf16[8,6400]{1,0:T(8,128)(2,1)S(1)}, bf16[8,6400]{1,0:T(8,128)(2,1)S(1)}, u32[]{:S(2)}, u32[]{:S(2)}) collective-permute-start(bf16[8,6400]{1,0:T(8,128)(2,1)S(1)} %pad_dynamic-slice_fusion.3), channel_id=1, source_target_pairs={{0,128},{128,0},{256,384},{384,256},{1,129},{129,1},{257,385},{385... | collective-permute-start | bytes 307208 | tf_op jit(solution)/shard_map/ppermute | solution.py:144
  4.4 7.8 %copy-start.6 = (bf16[12500,8]{0,1:T(8,128)(2,1)S(1)}, bf16[12500,8]{0,1:T(8,128)(2,1)}, u32[]{:S(2)}) copy-start(bf16[12500,8]{0,1:T(8,128)(2,1)} %param.4) | copy-start | bytes 600004
  4.4 17.2 %copy-start.2 = (bf16[125,1100]{0,1:T(8,128)(2,1)S(1)}, bf16[125,1100]{0,1:T(8,128)(2,1)}, u32[]{:S(2)}) copy-start(bf16[125,1100]{0,1:T(8,128)(2,1)} %param.5) | copy-start | bytes 825004
  9.7 78.3 %collective-permute-start.13 = (bf16[6400,128]{1,0:T(8,128)(2,1)}, bf16[6400,128]{1,0:T(8,128)(2,1)}, u32[]{:S(2)}, u32[]{:S(2)}) collective-permute-start(bf16[6400,128]{1,0:T(8,128)(2,1)} %get-tuple-element.5), channel_id=1, source_target_pairs={{0,128},{128,0},{256,384},{384,256},{1,129},{129,1},{257,385},{385... | collective-permute-start | bytes 4915208 | tf_op jit(solution)/shard_map/ppermute | solution.py:154
  12.2 39.4 %copy-start.5 = (bf16[16,6400]{1,0:T(8,128)(2,1)}, bf16[16,6400]{1,0:T(8,128)(2,1)S(1)}, u32[]{:S(2)}) copy-start(bf16[16,6400]{1,0:T(8,128)(2,1)S(1)} %pad_maximum_fusion.3.refs_0_) | copy-start | bytes 614404
  12.2 33.6 %collective-permute-start.2 = (bf16[16,6400]{1,0:T(8,128)(2,1)S(1)}, bf16[16,6400]{1,0:T(8,128)(2,1)S(1)}, u32[]{:S(2)}, u32[]{:S(2)}) collective-permute-start(bf16[16,6400]{1,0:T(8,128)(2,1)S(1)} %pad_maximum_fusion.3.refs_0_), channel_id=1, source_target_pairs={{0,16},{32,0},{64,32},{96,64},{112,96},{80,112},{48,80},{16,48},{1... | collective-permute-start | bytes 614408 | tf_op jit(solution)/shard_map/ppermute | solution.py:42
  17.4 34.2 %collective-permute-start.1 = (bf16[16,6400]{1,0:T(8,128)(2,1)S(1)}, bf16[16,6400]{1,0:T(8,128)(2,1)S(1)}, u32[]{:S(2)}, u32[]{:S(2)}) collective-permute-start(bf16[16,6400]{1,0:T(8,128)(2,1)S(1)} %pad_maximum_fusion.3.refs_0_), channel_id=1, source_target_pairs={{0,32},{32,64},{64,96},{96,112},{112,80},{80,48},{48,16},{16,0},{1... | collective-permute-start | bytes 614408 | tf_op jit(solution)/shard_map/ppermute | solution.py:41
  21.6 16.8 %collective-permute-start.15 = (bf16[144,128]{1,0:T(8,128)(2,1)S(1)}, bf16[144,128]{1,0:T(8,128)(2,1)S(1)}, u32[]{:S(2)}, u32[]{:S(2)}) collective-permute-start(bf16[144,128]{1,0:T(8,128)(2,1)S(1)} %pad_dynamic-slice_fusion.2), channel_id=1, source_target_pairs={{0,1},{1,0},{2,3},{3,2},{4,5},{5,4},{6,7},{7,6},{8,9},{9,8},{10,11... | collective-permute-start | bytes 110600 | tf_op jit(solution)/shard_map/ppermute | solution.py:26
  39.1 28.8 %all-to-all-start = ((bf16[8,144,128]{2,1,0:T(8,128)(2,1)}), bf16[8,144,128]{2,1,0:T(8,128)(2,1)S(1)}, u32[]{:S(2)}, u32[]{:S(2)}) async-start(bf16[8,144,128]{2,1,0:T(8,128)(2,1)} %broadcast_in_dim.6), calls=%async_computation | async-start | bytes 589824 | tf_op jit(solution)/shard_map/all_to_all | solution.py:30
  43.4 79.4 %collective-permute-start.12 = (bf16[6400,128]{1,0:T(8,128)(2,1)}, bf16[6400,128]{1,0:T(8,128)(2,1)}, u32[]{:S(2)}, u32[]{:S(2)}) collective-permute-start(bf16[6400,128]{1,0:T(8,128)(2,1)} %get-tuple-element.6.refs_12_), channel_id=1, source_target_pairs={{0,8},{8,0},{1,9},{9,1},{2,10},{10,2},{3,11},{11,3},{4,12},{12,4},... | collective-permute-start | bytes 4915208 | tf_op jit(solution)/shard_map/ppermute | solution.py:26
  45.9 35.6 %copy-start.3 = (bf16[16,6400]{1,0:T(8,128)(2,1)}, bf16[16,6400]{1,0:T(8,128)(2,1)S(1)}, u32[]{:S(2)}) copy-start(bf16[16,6400]{1,0:T(8,128)(2,1)S(1)} %collective-permute-done.2.refs_2_) | copy-start | bytes 614404
  45.9 14.7 %collective-permute-start.4 = (bf16[16,6400]{1,0:T(8,128)(2,1)S(1)}, bf16[16,6400]{1,0:T(8,128)(2,1)}, u32[]{:S(2)}, u32[]{:S(2)}) collective-permute-start(bf16[16,6400]{1,0:T(8,128)(2,1)S(1)} %collective-permute-done.2.refs_2_), channel_id=1, source_target_pairs={{0,16},{32,0},{64,32},{96,64},{112,96},{80,112},{48,80},{16,48},{1... | collective-permute-start | bytes 614408 | tf_op jit(solution)/shard_map/ppermute | solution.py:42
  51.7 29.8 %copy-start.4 = (bf16[16,6400]{1,0:T(8,128)(2,1)}, bf16[16,6400]{1,0:T(8,128)(2,1)S(1)}, u32[]{:S(2)}) copy-start(bf16[16,6400]{1,0:T(8,128)(2,1)S(1)} %collective-permute-done.1.refs_1_) | copy-start | bytes 614404
  51.7 14.3 %collective-permute-start.3 = (bf16[16,6400]{1,0:T(8,128)(2,1)S(1)}, bf16[16,6400]{1,0:T(8,128)(2,1)}, u32[]{:S(2)}, u32[]{:S(2)}) collective-permute-start(bf16[16,6400]{1,0:T(8,128)(2,1)S(1)} %collective-permute-done.1.refs_1_), channel_id=1, source_target_pairs={{0,32},{32,64},{64,96},{96,112},{112,80},{80,48},{48,16},{16,0},{1... | collective-permute-start | bytes 614408 | tf_op jit(solution)/shard_map/ppermute | solution.py:41
  60.6 13.7 %collective-permute-start.6 = (bf16[16,6400]{1,0:T(8,128)(2,1)}, bf16[16,6400]{1,0:T(8,128)(2,1)S(1)}, u32[]{:S(2)}, u32[]{:S(2)}) collective-permute-start(bf16[16,6400]{1,0:T(8,128)(2,1)} %collective-permute-done.4.refs_4_), channel_id=1, source_target_pairs={{0,16},{32,0},{64,32},{96,64},{112,96},{80,112},{48,80},{16,48},{1... | collective-permute-start | bytes 614408 | tf_op jit(solution)/shard_map/ppermute | solution.py:42
  66.0 13.5 %collective-permute-start.5 = (bf16[16,6400]{1,0:T(8,128)(2,1)}, bf16[16,6400]{1,0:T(8,128)(2,1)S(1)}, u32[]{:S(2)}, u32[]{:S(2)}) collective-permute-start(bf16[16,6400]{1,0:T(8,128)(2,1)} %collective-permute-done.3.refs_3_), channel_id=1, source_target_pairs={{0,32},{32,64},{64,96},{96,112},{112,80},{80,48},{48,16},{16,0},{1... | collective-permute-start | bytes 614408 | tf_op jit(solution)/shard_map/ppermute | solution.py:41
  69.8 32.6 %all-to-all-start.1 = ((bf16[4,2,1152,128]{3,2,1,0:T(8,128)(2,1)}), bf16[4,2,1152,128]{3,2,1,0:T(8,128)(2,1)S(1)}, u32[]{:S(2)}, u32[]{:S(2)}) async-start(bf16[4,2,1152,128]{3,2,1,0:T(8,128)(2,1)} %broadcast_in_dim.7), calls=%async_computation.1 | async-start | bytes 4718592 | tf_op jit(solution)/shard_map/all_to_all | solution.py:30
  74.3 20.2 %copy-start = (bf16[16,6400]{1,0:T(8,128)(2,1)}, bf16[16,6400]{1,0:T(8,128)(2,1)S(1)}, u32[]{:S(2)}) copy-start(bf16[16,6400]{1,0:T(8,128)(2,1)S(1)} %collective-permute-done.6.refs_6_) | copy-start | bytes 614404
  74.3 15.6 %collective-permute-start.8 = (bf16[8,6400]{1,0:T(8,128)(2,1)S(1)}, bf16[8,6400]{1,0:T(8,128)(2,1)S(1)}, u32[]{:S(2)}, u32[]{:S(2)}) collective-permute-start(bf16[8,6400]{1,0:T(8,128)(2,1)S(1)} %slice.17), channel_id=1, source_target_pairs={{0,16},{32,0},{64,32},{96,64},{112,96},{80,112},{48,80},{16,48},{1... | collective-permute-start | bytes 307208 | tf_op jit(solution)/shard_map/ppermute | solution.py:46
  79.5 15.0 %copy-start.1 = (bf16[16,6400]{1,0:T(8,128)(2,1)}, bf16[16,6400]{1,0:T(8,128)(2,1)S(1)}, u32[]{:S(2)}) copy-start(bf16[16,6400]{1,0:T(8,128)(2,1)S(1)} %collective-permute-done.5.refs_5_) | copy-start | bytes 614404
  79.5 10.4 %collective-permute-start.7 = (bf16[8,6400]{1,0:T(8,128)(2,1)S(1)}, bf16[8,6400]{1,0:T(8,128)(2,1)S(1)}, u32[]{:S(2)}, u32[]{:S(2)}) collective-permute-start(bf16[8,6400]{1,0:T(8,128)(2,1)S(1)} %slice.16), channel_id=1, source_target_pairs={{0,32},{32,64},{64,96},{96,112},{112,80},{80,48},{48,16},{16,0},{1... | collective-permute-start | bytes 307208 | tf_op jit(solution)/shard_map/ppermute | solution.py:45
  82.4 40.4 %collective-permute-start.9 = (bf16[48,6400]{1,0:T(8,128)(2,1)}, bf16[48,6400]{1,0:T(8,128)(2,1)}, u32[]{:S(2)}, u32[]{:S(2)}) collective-permute-start(bf16[48,6400]{1,0:T(8,128)(2,1)} %pad_maximum_fusion), channel_id=1, source_target_pairs={{128,256},{256,128},{384,0},{0,384},{129,257},{257,129},{385,1},{1... | collective-permute-start | bytes 1843208 | tf_op jit(solution)/shard_map/ppermute | solution.py:148
  88.0 34.8 %collective-permute-start.14 = (bf16[6400,128]{1,0:T(8,128)(2,1)}, bf16[6400,128]{1,0:T(8,128)(2,1)}, u32[]{:S(2)}, u32[]{:S(2)}) collective-permute-start(bf16[6400,128]{1,0:T(8,128)(2,1)} %collective-permute-done.13.refs_14_), channel_id=1, source_target_pairs={{0,8},{8,0},{1,9},{9,1},{2,10},{10,2},{3,11},{11,3},{4,12},{12,4},... | collective-permute-start | bytes 4915208 | tf_op jit(solution)/shard_map/ppermute | solution.py:26
  90.0 32.9 %copy-start.7 = (bf16[8,6400]{1,0:T(8,128)(2,1)}, bf16[8,6400]{1,0:T(8,128)(2,1)S(1)}, u32[]{:S(2)}) copy-start(bf16[8,6400]{1,0:T(8,128)(2,1)S(1)} %collective-permute-done.8.refs_8_) | copy-start | bytes 307204
  90.0 4.5 %copy-start.8 = (bf16[8,6400]{1,0:T(8,128)(2,1)}, bf16[8,6400]{1,0:T(8,128)(2,1)S(1)}, u32[]{:S(2)}) copy-start(bf16[8,6400]{1,0:T(8,128)(2,1)S(1)} %collective-permute-done.7.refs_7_) | copy-start | bytes 307204
  90.0 32.8 %collective-permute-start.11 = (bf16[48,6400]{1,0:T(8,128)(2,1)S(1)}, bf16[48,6400]{1,0:T(8,128)(2,1)}, u32[]{:S(2)}, u32[]{:S(2)}) collective-permute-start(bf16[48,6400]{1,0:T(8,128)(2,1)S(1)} %pad_maximum_fusion.1), channel_id=1, source_target_pairs={{128,256},{256,128},{384,0},{0,384},{129,257},{257,129},{385,1},{1... | collective-permute-start | bytes 1843208 | tf_op jit(solution)/shard_map/ppermute | solution.py:148
  94.5 28.3 %collective-permute-start.10 = (bf16[32,6400]{1,0:T(8,128)(2,1)}, bf16[32,6400]{1,0:T(8,128)(2,1)}, u32[]{:S(2)}, u32[]{:S(2)}) collective-permute-start(bf16[32,6400]{1,0:T(8,128)(2,1)} %pad_maximum_fusion.2), channel_id=1, source_target_pairs={{128,256},{256,128},{384,0},{0,384},{129,257},{257,129},{385,1},{1... | collective-permute-start | bytes 1228808 | tf_op jit(solution)/shard_map/ppermute | solution.py:148

commit v3 on v2

--- a/solution.py
+++ b/solution.py
@@ -41,10 +41,7 @@
         up = lax.ppermute(up, "zl", fold_ring(1))
         down = lax.ppermute(down, "zl", fold_ring(-1))
         parts += [up, down]
-    half = piece.shape[0] // 2
-    first = lax.ppermute(up[:half], "zl", fold_ring(1))
-    second = lax.ppermute(down[half:], "zl", fold_ring(-1))
-    return parts + [first, second]
+    return parts + [lax.ppermute(up, "zl", fold_ring(1))]
 
 
 def ring_source(step):
@@ -55,7 +52,7 @@
 
 
 def contract_kernel(*refs):
-    own, cross, (a, b, c, d, _, out, acc) = refs[: ZL + 1], refs[ZL + 1 : ZL + 4], refs[ZL + 4 :]
+    own, cross, (a, b, c, d, out, acc) = refs[:ZL], refs[ZL : ZL + 4], refs[ZL + 4 :]
     index = pl.program_id(0)
     here = lax.axis_index("x")
 
@@ -86,7 +83,7 @@
                         out[pl.ds(start, 8, stride=ZL * ZH * PIECES), :] = got
 
 
-def contract(own, cross, pieces, ready):
+def contract(own, cross, pieces):
     inner = own[0].shape[1]
     columns = X * ZL * own[0].shape[0] // 2
     lefts = [pl.BlockSpec((part.shape[0], BLOCK), lambda k: (0, k)) for part in own + cross]
@@ -95,14 +92,14 @@
         contract_kernel,
         grid=(inner // BLOCK,),
         out_shape=jax.ShapeDtypeStruct((columns * PIECES, LANES), jnp.float32),
-        in_specs=lefts + rights + [pl.BlockSpec(memory_space=pl.ANY)],
+        in_specs=lefts + rights,
         out_specs=pl.BlockSpec((columns * PIECES, LANES), lambda k: (0, 0)),
         scratch_shapes=[pltpu.VMEM((PIECES, columns, LANES), jnp.float32)],
         cost_estimate=pl.CostEstimate(
             flops=2 * columns * inner * PIECES * LANES, bytes_accessed=10 << 20, transcendentals=0
         ),
         name="contract",
-    )(*own, *cross, *pieces, ready)
+    )(*own, *cross, *pieces)
 
 
 def regroup_kernel(got, out):
@@ -127,6 +124,44 @@
     )(got)
 
 
+def transform_kernel(got, *refs):
+    coefs, out = refs[:Y], refs[Y]
+    nao = out.shape[2]
+    here = lax.axis_index("y")
+    totals = [0.0, 0.0]
+    for coef, shift in zip(coefs, (0, 1, 3, 2)):
+        block = lax.rem(here - shift + Y, Y)
+        tiles = [got[Y * h + block] + got[ZL + Y * h + block] for h in range(2)]
+        rest = jnp.concatenate(tiles, axis=0)
+        terms = []
+        for _ in range(3):
+            terms.append(rest.astype(jnp.bfloat16))
+            rest = rest - terms[-1].astype(jnp.float32)
+        terms = jnp.concatenate(terms, axis=0)
+        for side in range(2):
+            part = lax.dot_general(
+                terms, coef[side], (((1,), (1,)), ((), ())), preferred_element_type=jnp.float32
+            )
+            totals[side] += (part[:16] + part[16:32]) + part[32:]
+    for source in range(X):
+        for h in range(2):
+            row = h * 2 * X + 2 * source
+            line = totals[0][row : row + 1] + totals[1][row + 1 : row + 2]
+            out[2 * source + h] = line[:, :nao]
+
+
+def transform(got, coefs, nao):
+    vmem = pl.BlockSpec(memory_space=pltpu.VMEM)
+    return pl.pallas_call(
+        transform_kernel,
+        out_shape=jax.ShapeDtypeStruct((2 * X, 1, nao), jnp.float32),
+        in_specs=[vmem] * (1 + Y),
+        out_specs=vmem,
+        cost_estimate=pl.CostEstimate(flops=1 << 24, bytes_accessed=3 << 20, transcendentals=0),
+        name="transform",
+    )(got, *coefs)
+
+
 def on_device(density, chol_vectors, virt_coef):
     rows, inner = density.shape
     width = chol_vectors.shape[1]
@@ -146,12 +181,13 @@
     own = ring_gather(chunk)
     cross = [
         lax.ppermute(jnp.concatenate(own[first:last], axis=0), "x", CROSS)
-        for first, last in ((0, 3), (3, 5), (5, 9))
+        for first, last in ((0, 3), (3, 5), (5, 7), (7, 8))
     ]
 
     dens = jnp.pad(density.T, ((0, pad), (0, LANES - rows)))
     kept = lax.dynamic_slice(dens, (keep, 0), (depth, LANES))
-    other = lax.ppermute(lax.dynamic_slice(dens, (give, 0), (depth, LANES)), "x", PAIR)
+    given = lax.dynamic_slice(dens, (give, 0), (depth, LANES))
+    other = lax.ppermute(given, "x", PAIR)
     pieces = [kept, swap(kept, "c"), other, swap(other, "c")]
 
     coef = virt_coef.T
@@ -161,21 +197,15 @@
     far = swap(far, "zh")
     far = gathered(far, ("x", "c"), X * C).reshape(X * C * part, LANES)
     pair = jnp.where(half == core, jnp.stack([coef, far]), jnp.stack([far, coef]))
-    coefs = gathered(pair, "y", Y)
-
-    gamma = contract(own, cross, pieces, coefs[0, 0, :16])
+    coefs = [pair]
+    for shift in (1, 3, 2):
+        coefs.append(lax.ppermute(pair, "y", [(i, (i + shift) % Y) for i in range(Y)]))
+
+    gamma = contract(own, cross, pieces)
     gamma = exchange(gamma.reshape(X * Y, ZL * ZH * PIECES, LANES), ("x", "y"))
     gamma = regroup(gamma.reshape(X * Y, ZL, ZH * PIECES, LANES))
     gamma = exchange(gamma.reshape(ZH * ZL, 2 * X, LANES), ("zh", "zl"))
-    gamma = jnp.sum(gamma.reshape(ZH, 2, ZL // 2, X, 2, LANES), axis=0)
-    gamma = gamma.transpose(2, 0, 1, 3, 4).reshape(2 * X, ZL // 2 * 2, LANES)
-    out = jnp.einsum(
-        "ibr,bnr->in",
-        gamma,
-        coefs.reshape(2 * Y, X * C * part, LANES).astype(jnp.float32),
-        precision=lax.Precision.HIGHEST,
-    )
-    return out[:, None, :nao]
+    return transform(gamma, coefs, nao)
 
 
 def solution(mesh):

time: 178 us -> 165 us (0.927)
  the two profiles are of different devices: /device:TPU:32 before, /device:TPU:96 now
where the time goes in v3:
time: 165 us; the launch traced here: 164 us
  starting transfers between devices  92.2 us (56%)
  waiting for transfers between devices  42.4 us (26%)
  Pallas kernels  12.3 us (7%)
  local copies, waits for them, and re-layouts  11.1 us (7%)
  other arithmetic  5.63 us (3%)
    ppermute x3, starting transfers between devices, ring_gather(): down = lax.ppermute(down, 'zl', fold_ring(-1))  18.2 us
    ppermute x4, waiting for transfers between devices, on_device(): lax.ppermute(jnp.concatenate(own[first:last], axis=0), 'x', CROSS)  17 us
    ppermute x4, starting transfers between devices, on_device(): lax.ppermute(jnp.concatenate(own[first:last], axis=0), 'x', CROSS)  16.7 us
    ppermute x3, starting transfers between devices, swap(): return lax.ppermute(shard, axis, [(0, 1), (1, 0)])  16.5 us
    all_to_all x3, starting transfers between devices, exchange(): return lax.all_to_all(shard, axes, split_axis=0, concat_axis=0, tiled=True)  15.9 us
    ppermute x3, waiting for transfers between devices, on_device(): lax.ppermute(pair, 'y', [(i, (i + shift) % Y) for i in range(Y)])  14.7 us
    ppermute x3, starting transfers between devices, on_device(): lax.ppermute(pair, 'y', [(i, (i + shift) % Y) for i in range(Y)])  11.2 us
    ppermute x3, waiting for transfers between devices, ring_gather(): up = lax.ppermute(up, 'zl', fold_ring(1))  10.8 us
  transfers between devices with their start and end apart: 22, of which 8 were waited for; matrix products, arithmetic and copies ran while one was open for 8% of the time, Pallas kernels for 6%

profile of v3, /device:TPU:96, one launch (start us, length us, event | category | flops | bytes accessed | tf_op | source)
XLA Modules:
  0.0 164.0 jit_solution(4511050829767650110)
XLA Ops:
  0.0 0.9 pad_dynamic-slice_fusion.3
  0.9 3.4 %collective-permute-start = (bf16[8,6400]{1,0:T(8,128)(2,1)S(1)}, bf16[8,6400]{1,0:T(8,128)(2,1)}, u32[]{:S(2)}, u32[]{:S(2)}) collective-permute-start(bf16[8,6400]{1,0:T(8,128)(2,1)S(1)} %pad_dynamic-slice_fusion.3), channel_id=1, source_target_pairs={{0,128},{128,0},{256,384},{384,256},{1,129},{129,1},{257,385},{385... | collective-permute-start | bytes 307208 | tf_op jit(solution)/shard_map/ppermute | solution.py:179
  4.4 4.6 %pad_dynamic-slice_fusion = (bf16[6400,128]{1,0:T(8,128)(2,1)}, bf16[6400,128]{1,0:T(8,128)(2,1)S(1)}) fusion(s32[]{:T(128)S(6)} %select_n.39, bf16[12500,125]{1,0:T(8,128)(2,1)} %bitcast.9, s32[]{:T(128)S(6)} %select_n.38), kind=kLoop, calls=%fused_computation | loop fusion | bytes 6401808 | tf_op jit(solution)/shard_map/dynamic_slice | solution.py:189
  9.0 2.4 %collective-permute-start.13 = (bf16[6400,128]{1,0:T(8,128)(2,1)}, bf16[6400,128]{1,0:T(8,128)(2,1)S(1)}, u32[]{:S(2)}, u32[]{:S(2)}) collective-permute-start(bf16[6400,128]{1,0:T(8,128)(2,1)} %get-tuple-element.5), channel_id=1, source_target_pairs={{0,128},{128,0},{256,384},{384,256},{1,129},{129,1},{257,385},{385... | collective-permute-start | bytes 4915208 | tf_op jit(solution)/shard_map/ppermute | solution.py:190
  11.4 0.0 collective-permute-done
  11.4 1.1 broadcast_select_fusion.1
  12.5 0.7 pad_maximum_fusion.3.refs_0_
  13.2 1.9 %collective-permute-start.1 = (bf16[16,6400]{1,0:T(8,128)(2,1)}, bf16[16,6400]{1,0:T(8,128)(2,1)}, u32[]{:S(2)}, u32[]{:S(2)}) collective-permute-start(bf16[16,6400]{1,0:T(8,128)(2,1)} %pad_maximum_fusion.3.refs_0_), channel_id=1, source_target_pairs={{0,32},{32,64},{64,96},{96,112},{112,80},{80,48},{48,16},{16,0},{1... | collective-permute-start | bytes 614408 | tf_op jit(solution)/shard_map/ppermute | solution.py:41
  15.1 6.4 %collective-permute-start.2 = (bf16[16,6400]{1,0:T(8,128)(2,1)}, bf16[16,6400]{1,0:T(8,128)(2,1)}, u32[]{:S(2)}, u32[]{:S(2)}) collective-permute-start(bf16[16,6400]{1,0:T(8,128)(2,1)} %pad_maximum_fusion.3.refs_0_), channel_id=1, source_target_pairs={{0,16},{32,0},{64,32},{96,64},{112,96},{80,112},{48,80},{16,48},{1... | collective-permute-start | bytes 614408 | tf_op jit(solution)/shard_map/ppermute | solution.py:42
  21.5 1.9 %collective-permute-start.12 = (bf16[6400,128]{1,0:T(8,128)(2,1)S(1)}, bf16[6400,128]{1,0:T(8,128)(2,1)}, u32[]{:S(2)}, u32[]{:S(2)}) collective-permute-start(bf16[6400,128]{1,0:T(8,128)(2,1)S(1)} %get-tuple-element.6.refs_12_), channel_id=1, source_target_pairs={{0,8},{8,0},{1,9},{9,1},{2,10},{10,2},{3,11},{11,3},{4,12},{12,4},... | collective-permute-start | bytes 4915208 | tf_op jit(solution)/shard_map/ppermute | solution.py:26
  23.5 0.8 pad_dynamic-slice_fusion.2
  24.3 12.7 %collective-permute-start.15 = (bf16[144,128]{1,0:T(8,128)(2,1)S(1)}, bf16[144,128]{1,0:T(8,128)(2,1)S(1)}, u32[]{:S(2)}, u32[]{:S(2)}) collective-permute-start(bf16[144,128]{1,0:T(8,128)(2,1)S(1)} %pad_dynamic-slice_fusion.2), channel_id=1, source_target_pairs={{0,1},{1,0},{2,3},{3,2},{4,5},{5,4},{6,7},{7,6},{8,9},{9,8},{10,11... | collective-permute-start | bytes 110600 | tf_op jit(solution)/shard_map/ppermute | solution.py:26
  36.9 0.0 collective-permute-done.1.refs_1_
  37.0 2.1 %collective-permute-start.3 = (bf16[16,6400]{1,0:T(8,128)(2,1)}, bf16[16,6400]{1,0:T(8,128)(2,1)S(1)}, u32[]{:S(2)}, u32[]{:S(2)}) collective-permute-start(bf16[16,6400]{1,0:T(8,128)(2,1)} %collective-permute-done.1.refs_1_), channel_id=1, source_target_pairs={{0,32},{32,64},{64,96},{96,112},{112,80},{80,48},{48,16},{16,0},{1... | collective-permute-start | bytes 614408 | tf_op jit(solution)/shard_map/ppermute | solution.py:41
  39.1 0.0 collective-permute-done.2.refs_2_
  39.1 5.8 %collective-permute-start.4 = (bf16[16,6400]{1,0:T(8,128)(2,1)}, bf16[16,6400]{1,0:T(8,128)(2,1)S(1)}, u32[]{:S(2)}, u32[]{:S(2)}) collective-permute-start(bf16[16,6400]{1,0:T(8,128)(2,1)} %collective-permute-done.2.refs_2_), channel_id=1, source_target_pairs={{0,16},{32,0},{64,32},{96,64},{112,96},{80,112},{48,80},{16,48},{1... | collective-permute-start | bytes 614408 | tf_op jit(solution)/shard_map/ppermute | solution.py:42
  44.9 1.1 pad_maximum_fusion
  46.0 6.8 %collective-permute-done.3.refs_3_ = bf16[16,6400]{1,0:T(8,128)(2,1)S(1)} collective-permute-done((bf16[16,6400]{1,0:T(8,128)(2,1)}, bf16[16,6400]{1,0:T(8,128)(2,1)S(1)}, u32[]{:S(2)}, u32[]{:S(2)}) %collective-permute-start.3) | collective-permute-done | bytes 204832 | tf_op jit(solution)/shard_map/ppermute | solution.py:41
  52.9 1.9 %collective-permute-start.5 = (bf16[16,6400]{1,0:T(8,128)(2,1)S(1)}, bf16[16,6400]{1,0:T(8,128)(2,1)S(1)}, u32[]{:S(2)}, u32[]{:S(2)}) collective-permute-start(bf16[16,6400]{1,0:T(8,128)(2,1)S(1)} %collective-permute-done.3.refs_3_), channel_id=1, source_target_pairs={{0,32},{32,64},{64,96},{96,112},{112,80},{80,48},{48,16},{16,0},{1... | collective-permute-start | bytes 614408 | tf_op jit(solution)/shard_map/ppermute | solution.py:41
  54.8 0.0 collective-permute-done.4.refs_4_
  54.8 6.0 %collective-permute-start.6 = (bf16[16,6400]{1,0:T(8,128)(2,1)S(1)}, bf16[16,6400]{1,0:T(8,128)(2,1)S(1)}, u32[]{:S(2)}, u32[]{:S(2)}) collective-permute-start(bf16[16,6400]{1,0:T(8,128)(2,1)S(1)} %collective-permute-done.4.refs_4_), channel_id=1, source_target_pairs={{0,16},{32,0},{64,32},{96,64},{112,96},{80,112},{48,80},{16,48},{1... | collective-permute-start | bytes 614408 | tf_op jit(solution)/shard_map/ppermute | solution.py:42
  60.8 0.0 collective-permute-done.13.refs_14_
  60.9 1.9 %collective-permute-start.14 = (bf16[6400,128]{1,0:T(8,128)(2,1)S(1)}, bf16[6400,128]{1,0:T(8,128)(2,1)}, u32[]{:S(2)}, u32[]{:S(2)}) collective-permute-start(bf16[6400,128]{1,0:T(8,128)(2,1)S(1)} %collective-permute-done.13.refs_14_), channel_id=1, source_target_pairs={{0,8},{8,0},{1,9},{9,1},{2,10},{10,2},{3,11},{11,3},{4,12},{12,4},... | collective-permute-start | bytes 4915208 | tf_op jit(solution)/shard_map/ppermute | solution.py:26
  62.8 0.8 pad_maximum_fusion.1
  63.6 3.9 %collective-permute-done.5.refs_5_ = bf16[16,6400]{1,0:T(8,128)(2,1)S(1)} collective-permute-done((bf16[16,6400]{1,0:T(8,128)(2,1)S(1)}, bf16[16,6400]{1,0:T(8,128)(2,1)S(1)}, u32[]{:S(2)}, u32[]{:S(2)}) %collective-permute-start.5) | collective-permute-done | bytes 204832 | tf_op jit(solution)/shard_map/ppermute | solution.py:41
  67.5 4.6 %collective-permute-start.8 = (bf16[48,6400]{1,0:T(8,128)(2,1)S(1)}, bf16[48,6400]{1,0:T(8,128)(2,1)}, u32[]{:S(2)}, u32[]{:S(2)}) collective-permute-start(bf16[48,6400]{1,0:T(8,128)(2,1)S(1)} %pad_maximum_fusion), channel_id=1, source_target_pairs={{128,256},{256,128},{384,0},{0,384},{129,257},{257,129},{385,1},{1... | collective-permute-start | bytes 1843208 | tf_op jit(solution)/shard_map/ppermute | solution.py:183
  72.1 0.0 collective-permute-done.6.refs_6_
  72.1 1.9 %collective-permute-start.7 = (bf16[16,6400]{1,0:T(8,128)(2,1)S(1)}, bf16[16,6400]{1,0:T(8,128)(2,1)}, u32[]{:S(2)}, u32[]{:S(2)}) collective-permute-start(bf16[16,6400]{1,0:T(8,128)(2,1)S(1)} %collective-permute-done.5.refs_5_), channel_id=1, source_target_pairs={{0,32},{32,64},{64,96},{96,112},{112,80},{80,48},{48,16},{16,0},{1... | collective-permute-start | bytes 614408 | tf_op jit(solution)/shard_map/ppermute | solution.py:44
  74.1 0.8 pad_maximum_fusion.2
  74.9 0.0 collective-permute-done.15
  74.9 2.4 %collective-permute-start.9 = (bf16[32,6400]{1,0:T(8,128)(2,1)}, bf16[32,6400]{1,0:T(8,128)(2,1)}, u32[]{:S(2)}, u32[]{:S(2)}) collective-permute-start(bf16[32,6400]{1,0:T(8,128)(2,1)} %pad_maximum_fusion.1), channel_id=1, source_target_pairs={{128,256},{256,128},{384,0},{0,384},{129,257},{257,129},{385,1},{1... | collective-permute-start | bytes 1228808 | tf_op jit(solution)/shard_map/ppermute | solution.py:183
  77.3 10.1 %collective-permute-done.8.refs_8_ = bf16[48,6400]{1,0:T(8,128)(2,1)} collective-permute-done((bf16[48,6400]{1,0:T(8,128)(2,1)S(1)}, bf16[48,6400]{1,0:T(8,128)(2,1)}, u32[]{:S(2)}, u32[]{:S(2)}) %collective-permute-start.8) | collective-permute-done | bytes 614432 | tf_op jit(solution)/shard_map/ppermute | solution.py:183
  87.4 4.6 %collective-permute-start.10 = (bf16[32,6400]{1,0:T(8,128)(2,1)}, bf16[32,6400]{1,0:T(8,128)(2,1)}, u32[]{:S(2)}, u32[]{:S(2)}) collective-permute-start(bf16[32,6400]{1,0:T(8,128)(2,1)} %pad_maximum_fusion.2), channel_id=1, source_target_pairs={{128,256},{256,128},{384,0},{0,384},{129,257},{257,129},{385,1},{1... | collective-permute-start | bytes 1228808 | tf_op jit(solution)/shard_map/ppermute | solution.py:183
  92.0 0.8 broadcast_in_dim.2
  92.8 4.0 %all-to-all-start.2 = ((bf16[8,144,128]{2,1,0:T(8,128)(2,1)}), bf16[8,144,128]{2,1,0:T(8,128)(2,1)}, u32[]{:S(2)}, u32[]{:S(2)}) async-start(bf16[8,144,128]{2,1,0:T(8,128)(2,1)} %broadcast_in_dim.2), calls=%async_computation.2 | async-start | bytes 589824 | tf_op jit(solution)/shard_map/all_to_all | solution.py:30
  96.8 0.0 collective-permute-done.7.refs_7_
  96.9 5.0 %collective-permute-start.11 = (bf16[16,6400]{1,0:T(8,128)(2,1)}, bf16[16,6400]{1,0:T(8,128)(2,1)}, u32[]{:S(2)}, u32[]{:S(2)}) collective-permute-start(bf16[16,6400]{1,0:T(8,128)(2,1)} %collective-permute-done.7.refs_7_), channel_id=1, source_target_pairs={{128,256},{256,128},{384,0},{0,384},{129,257},{257,129},{385,1},{1... | collective-permute-start | bytes 614408 | tf_op jit(solution)/shard_map/ppermute | solution.py:183
  101.9 1.7 %pad_bitcast_fusion = bf16[1,1152,128]{2,1,0:T(8,128)(2,1)} fusion(bf16[1100,125]{1,0:T(8,128)(2,1)} %bitcast.13), kind=kLoop, calls=%fused_computation.7 | loop fusion | bytes 569912 | tf_op jit(solution)/shard_map/stack | solution.py:199
  103.6 0.0 collective-permute-done.9.refs_9_
  103.6 2.6 %collective-permute-done.10.refs_10_ = bf16[32,6400]{1,0:T(8,128)(2,1)} collective-permute-done((bf16[32,6400]{1,0:T(8,128)(2,1)}, bf16[32,6400]{1,0:T(8,128)(2,1)}, u32[]{:S(2)}, u32[]{:S(2)}) %collective-permute-start.10) | collective-permute-done | bytes 409632 | tf_op jit(solution)/shard_map/ppermute | solution.py:183
  106.2 4.3 %collective-permute-done.11.refs_11_ = bf16[16,6400]{1,0:T(8,128)(2,1)} collective-permute-done((bf16[16,6400]{1,0:T(8,128)(2,1)}, bf16[16,6400]{1,0:T(8,128)(2,1)}, u32[]{:S(2)}, u32[]{:S(2)}) %collective-permute-start.11) | collective-permute-done | bytes 204832 | tf_op jit(solution)/shard_map/ppermute | solution.py:183
  110.5 0.0 collective-permute-done.12.refs_13_
  110.5 0.0 collective-permute-done.14.refs_15_
  110.5 0.0 copy-done.3
  110.5 0.0 copy-done.7
  110.5 7.4 %contract.1 = f32[1024,128]{1,0:T(8,128)} custom-call(bf16[16,6400]{1,0:T(8,128)(2,1)} %pad_maximum_fusion.3.refs_0_, bf16[16,6400]{1,0:T(8,128)(2,1)} %collective-permute-done.1.refs_1_, bf16[16,6400]{1,0:T(8,128)(2,1)} %collective-permute-done.2.refs_2_, bf16[16,6400]{1,0:T(8,128)(2,1)} %copy-done.5, bf16[16,6400]{1,0:T(8,128)(2,1)} %copy-done.6, ...), custom_call_target="tpu_custom_call" | custom-call | flops 1677721600 | bytes 10485760 | tf_op jit(solution)/shard_map/contract/pallas_call | solution.py:91
  117.9 0.0 all-to-all-done.2
  118.0 6.7 %all-to-all-start = ((f32[16,64,128]{2,1,0:T(8,128)}), f32[16,64,128]{2,1,0:T(8,128)S(1)}, u32[]{:S(2)}, u32[]{:S(2)}) async-start(f32[16,64,128]{2,1,0:T(8,128)} %bitcast.10), calls=%async_computation | async-start | bytes 1048576 | tf_op jit(solution)/shard_map/all_to_all | solution.py:30
  124.7 1.1 maximum_select_fusion.refs_0_
  125.9 3.8 %collective-permute-start.16 = (bf16[2,1152,128]{2,1,0:T(8,128)(2,1)S(1)}, bf16[2,1152,128]{2,1,0:T(8,128)(2,1)S(1)}, u32[]{:S(2)}, u32[]{:S(2)}) collective-permute-start(bf16[2,1152,128]{2,1,0:T(8,128)(2,1)S(1)} %maximum_select_fusion.refs_0_), channel_id=1, source_target_pairs={{0,2},{2,4},{4,6},{6,0},{1,3},{3,5},{5,7},{7,1},{8,10},{10,12},{12... | collective-permute-start | bytes 1769480 | tf_op jit(solution)/shard_map/ppermute | solution.py:202
  129.7 3.2 %collective-permute-start.17 = (bf16[2,1152,128]{2,1,0:T(8,128)(2,1)S(1)}, bf16[2,1152,128]{2,1,0:T(8,128)(2,1)S(1)}, u32[]{:S(2)}, u32[]{:S(2)}) collective-permute-start(bf16[2,1152,128]{2,1,0:T(8,128)(2,1)S(1)} %maximum_select_fusion.refs_0_), channel_id=1, source_target_pairs={{0,6},{2,0},{4,2},{6,4},{1,7},{3,1},{5,3},{7,5},{8,14},{10,8},{12,... | collective-permute-start | bytes 1769480 | tf_op jit(solution)/shard_map/ppermute | solution.py:202
  132.9 4.1 %collective-permute-start.18 = (bf16[2,1152,128]{2,1,0:T(8,128)(2,1)S(1)}, bf16[2,1152,128]{2,1,0:T(8,128)(2,1)S(1)}, u32[]{:S(2)}, u32[]{:S(2)}) collective-permute-start(bf16[2,1152,128]{2,1,0:T(8,128)(2,1)S(1)} %maximum_select_fusion.refs_0_), channel_id=1, source_target_pairs={{0,4},{2,6},{4,0},{6,2},{1,5},{3,7},{5,1},{7,3},{8,12},{10,14},{12... | collective-permute-start | bytes 1769480 | tf_op jit(solution)/shard_map/ppermute | solution.py:202
  137.1 0.0 all-to-all-done
  137.1 0.8 copy-done.2
  137.9 1.7 %regroup.1 = f32[2,8,8,128]{3,2,1,0:T(8,128)} custom-call(f32[16,8,8,128]{3,2,1,0:T(8,128)} %bitcast.11), custom_call_target="tpu_custom_call" | custom-call | flops 131072 | bytes 524288 | tf_op jit(solution)/shard_map/regroup/pallas_call | solution.py:119
  139.6 5.1 %all-to-all-start.1 = ((f32[16,8,128]{2,1,0:T(8,128)}), f32[16,8,128]{2,1,0:T(8,128)S(1)}, u32[]{:S(2)}, u32[]{:S(2)}) async-start(f32[16,8,128]{2,1,0:T(8,128)} %bitcast.16), calls=%async_computation.1 | async-start | bytes 131072 | tf_op jit(solution)/shard_map/all_to_all | solution.py:30
  144.7 1.6 collective-permute-done.16.refs_1_
  146.3 1.5 collective-permute-done.17.refs_2_
  147.8 11.6 %collective-permute-done.18.refs_3_ = bf16[2,1152,128]{2,1,0:T(8,128)(2,1)S(1)} collective-permute-done((bf16[2,1152,128]{2,1,0:T(8,128)(2,1)S(1)}, bf16[2,1152,128]{2,1,0:T(8,128)(2,1)S(1)}, u32[]{:S(2)}, u32[]{:S(2)}) %collective-permute-start.18) | collective-permute-done | bytes 589856 | tf_op jit(solution)/shard_map/ppermute | solution.py:202
  159.4 0.0 all-to-all-done.1.got
  159.4 0.0 copy-done.1
  159.4 0.8 copy-done.11
  160.2 0.6 copy-done.12
  160.8 3.1 %transform.1 = f32[8,1,1100]{2,1,0:T(1,128)} custom-call(f32[16,8,128]{2,1,0:T(8,128)} %copy-done.12, bf16[2,1152,128]{2,1,0:T(8,128)(2,1)} %copy-done.1, bf16[2,1152,128]{2,1,0:T(8,128)(2,1)} %copy-done.9, bf16[2,1152,128]{2,1,0:T(8,128)(2,1)} %copy-done.10, bf16[2,1152,128]{2,1,0:T(8,128)(2,1)} %copy-done.11), custom_call_target="tpu_custom_call" | custom-call | flops 16777216 | bytes 3145728 | tf_op jit(solution)/shard_map/transform/pallas_call | solution.py:155
  (20 shorter events, 0.0 us)
Async XLA Ops:
  0.9 10.5 %collective-permute-start = (bf16[8,6400]{1,0:T(8,128)(2,1)S(1)}, bf16[8,6400]{1,0:T(8,128)(2,1)}, u32[]{:S(2)}, u32[]{:S(2)}) collective-permute-start(bf16[8,6400]{1,0:T(8,128)(2,1)S(1)} %pad_dynamic-slice_fusion.3), channel_id=1, source_target_pairs={{0,128},{128,0},{256,384},{384,256},{1,129},{129,1},{257,385},{385... | collective-permute-start | bytes 307208 | tf_op jit(solution)/shard_map/ppermute | solution.py:179
  9.0 54.6 %copy-start = (bf16[6400,128]{1,0:T(8,128)(2,1)}, bf16[6400,128]{1,0:T(8,128)(2,1)S(1)}, u32[]{:S(2)}) copy-start(bf16[6400,128]{1,0:T(8,128)(2,1)S(1)} %get-tuple-element.6.refs_12_) | copy-start | bytes 4915204
  9.0 51.9 %collective-permute-start.13 = (bf16[6400,128]{1,0:T(8,128)(2,1)}, bf16[6400,128]{1,0:T(8,128)(2,1)S(1)}, u32[]{:S(2)}, u32[]{:S(2)}) collective-permute-start(bf16[6400,128]{1,0:T(8,128)(2,1)} %get-tuple-element.5), channel_id=1, source_target_pairs={{0,128},{128,0},{256,384},{384,256},{1,129},{129,1},{257,385},{385... | collective-permute-start | bytes 4915208 | tf_op jit(solution)/shard_map/ppermute | solution.py:190
  13.2 23.7 %collective-permute-start.1 = (bf16[16,6400]{1,0:T(8,128)(2,1)}, bf16[16,6400]{1,0:T(8,128)(2,1)}, u32[]{:S(2)}, u32[]{:S(2)}) collective-permute-start(bf16[16,6400]{1,0:T(8,128)(2,1)} %pad_maximum_fusion.3.refs_0_), channel_id=1, source_target_pairs={{0,32},{32,64},{64,96},{96,112},{112,80},{80,48},{48,16},{16,0},{1... | collective-permute-start | bytes 614408 | tf_op jit(solution)/shard_map/ppermute | solution.py:41
  15.1 24.0 %collective-permute-start.2 = (bf16[16,6400]{1,0:T(8,128)(2,1)}, bf16[16,6400]{1,0:T(8,128)(2,1)}, u32[]{:S(2)}, u32[]{:S(2)}) collective-permute-start(bf16[16,6400]{1,0:T(8,128)(2,1)} %pad_maximum_fusion.3.refs_0_), channel_id=1, source_target_pairs={{0,16},{32,0},{64,32},{96,64},{112,96},{80,112},{48,80},{16,48},{1... | collective-permute-start | bytes 614408 | tf_op jit(solution)/shard_map/ppermute | solution.py:42
  21.5 89.0 %collective-permute-start.12 = (bf16[6400,128]{1,0:T(8,128)(2,1)S(1)}, bf16[6400,128]{1,0:T(8,128)(2,1)}, u32[]{:S(2)}, u32[]{:S(2)}) collective-permute-start(bf16[6400,128]{1,0:T(8,128)(2,1)S(1)} %get-tuple-element.6.refs_12_), channel_id=1, source_target_pairs={{0,8},{8,0},{1,9},{9,1},{2,10},{10,2},{3,11},{11,3},{4,12},{12,4},... | collective-permute-start | bytes 4915208 | tf_op jit(solution)/shard_map/ppermute | solution.py:26
  24.3 50.6 %collective-permute-start.15 = (bf16[144,128]{1,0:T(8,128)(2,1)S(1)}, bf16[144,128]{1,0:T(8,128)(2,1)S(1)}, u32[]{:S(2)}, u32[]{:S(2)}) collective-permute-start(bf16[144,128]{1,0:T(8,128)(2,1)S(1)} %pad_dynamic-slice_fusion.2), channel_id=1, source_target_pairs={{0,1},{1,0},{2,3},{3,2},{4,5},{5,4},{6,7},{7,6},{8,9},{9,8},{10,11... | collective-permute-start | bytes 110600 | tf_op jit(solution)/shard_map/ppermute | solution.py:26
  37.0 15.9 %collective-permute-start.3 = (bf16[16,6400]{1,0:T(8,128)(2,1)}, bf16[16,6400]{1,0:T(8,128)(2,1)S(1)}, u32[]{:S(2)}, u32[]{:S(2)}) collective-permute-start(bf16[16,6400]{1,0:T(8,128)(2,1)} %collective-permute-done.1.refs_1_), channel_id=1, source_target_pairs={{0,32},{32,64},{64,96},{96,112},{112,80},{80,48},{48,16},{16,0},{1... | collective-permute-start | bytes 614408 | tf_op jit(solution)/shard_map/ppermute | solution.py:41
  39.1 15.7 %collective-permute-start.4 = (bf16[16,6400]{1,0:T(8,128)(2,1)}, bf16[16,6400]{1,0:T(8,128)(2,1)S(1)}, u32[]{:S(2)}, u32[]{:S(2)}) collective-permute-start(bf16[16,6400]{1,0:T(8,128)(2,1)} %collective-permute-done.2.refs_2_), channel_id=1, source_target_pairs={{0,16},{32,0},{64,32},{96,64},{112,96},{80,112},{48,80},{16,48},{1... | collective-permute-start | bytes 614408 | tf_op jit(solution)/shard_map/ppermute | solution.py:42
  52.9 14.6 %copy-start.5 = (bf16[16,6400]{1,0:T(8,128)(2,1)}, bf16[16,6400]{1,0:T(8,128)(2,1)S(1)}, u32[]{:S(2)}) copy-start(bf16[16,6400]{1,0:T(8,128)(2,1)S(1)} %collective-permute-done.3.refs_3_) | copy-start | bytes 614404
  52.9 14.6 %collective-permute-start.5 = (bf16[16,6400]{1,0:T(8,128)(2,1)S(1)}, bf16[16,6400]{1,0:T(8,128)(2,1)S(1)}, u32[]{:S(2)}, u32[]{:S(2)}) collective-permute-start(bf16[16,6400]{1,0:T(8,128)(2,1)S(1)} %collective-permute-done.3.refs_3_), channel_id=1, source_target_pairs={{0,32},{32,64},{64,96},{96,112},{112,80},{80,48},{48,16},{16,0},{1... | collective-permute-start | bytes 614408 | tf_op jit(solution)/shard_map/ppermute | solution.py:41
  54.8 17.3 %copy-start.6 = (bf16[16,6400]{1,0:T(8,128)(2,1)}, bf16[16,6400]{1,0:T(8,128)(2,1)S(1)}, u32[]{:S(2)}) copy-start(bf16[16,6400]{1,0:T(8,128)(2,1)S(1)} %collective-permute-done.4.refs_4_) | copy-start | bytes 614404
  54.8 17.3 %collective-permute-start.6 = (bf16[16,6400]{1,0:T(8,128)(2,1)S(1)}, bf16[16,6400]{1,0:T(8,128)(2,1)S(1)}, u32[]{:S(2)}, u32[]{:S(2)}) collective-permute-start(bf16[16,6400]{1,0:T(8,128)(2,1)S(1)} %collective-permute-done.4.refs_4_), channel_id=1, source_target_pairs={{0,16},{32,0},{64,32},{96,64},{112,96},{80,112},{48,80},{16,48},{1... | collective-permute-start | bytes 614408 | tf_op jit(solution)/shard_map/ppermute | solution.py:42
  60.8 49.7 %copy-start.3 = (bf16[6400,128]{1,0:T(8,128)(2,1)}, bf16[6400,128]{1,0:T(8,128)(2,1)S(1)}, u32[]{:S(2)}) copy-start(bf16[6400,128]{1,0:T(8,128)(2,1)S(1)} %collective-permute-done.13.refs_14_) | copy-start | bytes 4915204
  60.9 49.7 %collective-permute-start.14 = (bf16[6400,128]{1,0:T(8,128)(2,1)S(1)}, bf16[6400,128]{1,0:T(8,128)(2,1)}, u32[]{:S(2)}, u32[]{:S(2)}) collective-permute-start(bf16[6400,128]{1,0:T(8,128)(2,1)S(1)} %collective-permute-done.13.refs_14_), channel_id=1, source_target_pairs={{0,8},{8,0},{1,9},{9,1},{2,10},{10,2},{3,11},{11,3},{4,12},{12,4},... | collective-permute-start | bytes 4915208 | tf_op jit(solution)/shard_map/ppermute | solution.py:26
  67.5 43.1 %copy-start.7 = (bf16[16,6400]{1,0:T(8,128)(2,1)}, bf16[16,6400]{1,0:T(8,128)(2,1)S(1)}, u32[]{:S(2)}) copy-start(bf16[16,6400]{1,0:T(8,128)(2,1)S(1)} %collective-permute-done.5.refs_5_) | copy-start | bytes 614404
  67.5 19.9 %collective-permute-start.8 = (bf16[48,6400]{1,0:T(8,128)(2,1)S(1)}, bf16[48,6400]{1,0:T(8,128)(2,1)}, u32[]{:S(2)}, u32[]{:S(2)}) collective-permute-start(bf16[48,6400]{1,0:T(8,128)(2,1)S(1)} %pad_maximum_fusion), channel_id=1, source_target_pairs={{128,256},{256,128},{384,0},{0,384},{129,257},{257,129},{385,1},{1... | collective-permute-start | bytes 1843208 | tf_op jit(solution)/shard_map/ppermute | solution.py:183
  72.1 1.9 %copy-start.8 = (bf16[16,6400]{1,0:T(8,128)(2,1)}, bf16[16,6400]{1,0:T(8,128)(2,1)S(1)}, u32[]{:S(2)}) copy-start(bf16[16,6400]{1,0:T(8,128)(2,1)S(1)} %collective-permute-done.6.refs_6_) | copy-start | bytes 614404
  72.1 24.7 %collective-permute-start.7 = (bf16[16,6400]{1,0:T(8,128)(2,1)S(1)}, bf16[16,6400]{1,0:T(8,128)(2,1)}, u32[]{:S(2)}, u32[]{:S(2)}) collective-permute-start(bf16[16,6400]{1,0:T(8,128)(2,1)S(1)} %collective-permute-done.5.refs_5_), channel_id=1, source_target_pairs={{0,32},{32,64},{64,96},{96,112},{112,80},{80,48},{48,16},{16,0},{1... | collective-permute-start | bytes 614408 | tf_op jit(solution)/shard_map/ppermute | solution.py:44
  74.9 28.7 %collective-permute-start.9 = (bf16[32,6400]{1,0:T(8,128)(2,1)}, bf16[32,6400]{1,0:T(8,128)(2,1)}, u32[]{:S(2)}, u32[]{:S(2)}) collective-permute-start(bf16[32,6400]{1,0:T(8,128)(2,1)} %pad_maximum_fusion.1), channel_id=1, source_target_pairs={{128,256},{256,128},{384,0},{0,384},{129,257},{257,129},{385,1},{1... | collective-permute-start | bytes 1228808 | tf_op jit(solution)/shard_map/ppermute | solution.py:183
  87.4 18.8 %collective-permute-start.10 = (bf16[32,6400]{1,0:T(8,128)(2,1)}, bf16[32,6400]{1,0:T(8,128)(2,1)}, u32[]{:S(2)}, u32[]{:S(2)}) collective-permute-start(bf16[32,6400]{1,0:T(8,128)(2,1)} %pad_maximum_fusion.2), channel_id=1, source_target_pairs={{128,256},{256,128},{384,0},{0,384},{129,257},{257,129},{385,1},{1... | collective-permute-start | bytes 1228808 | tf_op jit(solution)/shard_map/ppermute | solution.py:183
  92.8 25.2 %all-to-all-start.2 = ((bf16[8,144,128]{2,1,0:T(8,128)(2,1)}), bf16[8,144,128]{2,1,0:T(8,128)(2,1)}, u32[]{:S(2)}, u32[]{:S(2)}) async-start(bf16[8,144,128]{2,1,0:T(8,128)(2,1)} %broadcast_in_dim.2), calls=%async_computation.2 | async-start | bytes 589824 | tf_op jit(solution)/shard_map/all_to_all | solution.py:30
  96.9 13.7 %collective-permute-start.11 = (bf16[16,6400]{1,0:T(8,128)(2,1)}, bf16[16,6400]{1,0:T(8,128)(2,1)}, u32[]{:S(2)}, u32[]{:S(2)}) collective-permute-start(bf16[16,6400]{1,0:T(8,128)(2,1)} %collective-permute-done.7.refs_7_), channel_id=1, source_target_pairs={{128,256},{256,128},{384,0},{0,384},{129,257},{257,129},{385,1},{1... | collective-permute-start | bytes 614408 | tf_op jit(solution)/shard_map/ppermute | solution.py:183
  110.5 14.2 %copy-start.4 = (bf16[1,1152,128]{2,1,0:T(8,128)(2,1)S(1)}, bf16[1,1152,128]{2,1,0:T(8,128)(2,1)}, u32[]{:S(2)}) copy-start(bf16[1,1152,128]{2,1,0:T(8,128)(2,1)} %pad_bitcast_fusion) | copy-start | bytes 884740
  118.0 19.1 %all-to-all-start = ((f32[16,64,128]{2,1,0:T(8,128)}), f32[16,64,128]{2,1,0:T(8,128)S(1)}, u32[]{:S(2)}, u32[]{:S(2)}) async-start(f32[16,64,128]{2,1,0:T(8,128)} %bitcast.10), calls=%async_computation | async-start | bytes 1048576 | tf_op jit(solution)/shard_map/all_to_all | solution.py:30
  125.8 33.5 %copy-start.1 = (bf16[2,1152,128]{2,1,0:T(8,128)(2,1)}, bf16[2,1152,128]{2,1,0:T(8,128)(2,1)S(1)}, u32[]{:S(2)}) copy-start(bf16[2,1152,128]{2,1,0:T(8,128)(2,1)S(1)} %maximum_select_fusion.refs_0_) | copy-start | bytes 1769476
  125.9 20.4 %collective-permute-start.16 = (bf16[2,1152,128]{2,1,0:T(8,128)(2,1)S(1)}, bf16[2,1152,128]{2,1,0:T(8,128)(2,1)S(1)}, u32[]{:S(2)}, u32[]{:S(2)}) collective-permute-start(bf16[2,1152,128]{2,1,0:T(8,128)(2,1)S(1)} %maximum_select_fusion.refs_0_), channel_id=1, source_target_pairs={{0,2},{2,4},{4,6},{6,0},{1,3},{3,5},{5,7},{7,1},{8,10},{10,12},{12... | collective-permute-start | bytes 1769480 | tf_op jit(solution)/shard_map/ppermute | solution.py:202
  129.7 18.1 %collective-permute-start.17 = (bf16[2,1152,128]{2,1,0:T(8,128)(2,1)S(1)}, bf16[2,1152,128]{2,1,0:T(8,128)(2,1)S(1)}, u32[]{:S(2)}, u32[]{:S(2)}) collective-permute-start(bf16[2,1152,128]{2,1,0:T(8,128)(2,1)S(1)} %maximum_select_fusion.refs_0_), channel_id=1, source_target_pairs={{0,6},{2,0},{4,2},{6,4},{1,7},{3,1},{5,3},{7,5},{8,14},{10,8},{12,... | collective-permute-start | bytes 1769480 | tf_op jit(solution)/shard_map/ppermute | solution.py:202
  132.9 26.5 %collective-permute-start.18 = (bf16[2,1152,128]{2,1,0:T(8,128)(2,1)S(1)}, bf16[2,1152,128]{2,1,0:T(8,128)(2,1)S(1)}, u32[]{:S(2)}, u32[]{:S(2)}) collective-permute-start(bf16[2,1152,128]{2,1,0:T(8,128)(2,1)S(1)} %maximum_select_fusion.refs_0_), channel_id=1, source_target_pairs={{0,4},{2,6},{4,0},{6,2},{1,5},{3,7},{5,1},{7,3},{8,12},{10,14},{12... | collective-permute-start | bytes 1769480 | tf_op jit(solution)/shard_map/ppermute | solution.py:202
  137.1 0.8 copy-start.2
  139.6 19.8 %all-to-all-start.1 = ((f32[16,8,128]{2,1,0:T(8,128)}), f32[16,8,128]{2,1,0:T(8,128)S(1)}, u32[]{:S(2)}, u32[]{:S(2)}) async-start(f32[16,8,128]{2,1,0:T(8,128)} %bitcast.16), calls=%async_computation.1 | async-start | bytes 131072 | tf_op jit(solution)/shard_map/all_to_all | solution.py:30
  146.3 13.1 %copy-start.9 = (bf16[2,1152,128]{2,1,0:T(8,128)(2,1)}, bf16[2,1152,128]{2,1,0:T(8,128)(2,1)S(1)}, u32[]{:S(2)}) copy-start(bf16[2,1152,128]{2,1,0:T(8,128)(2,1)S(1)} %collective-permute-done.16.refs_1_) | copy-start | bytes 1769476
  147.8 11.6 %copy-start.10 = (bf16[2,1152,128]{2,1,0:T(8,128)(2,1)}, bf16[2,1152,128]{2,1,0:T(8,128)(2,1)S(1)}, u32[]{:S(2)}) copy-start(bf16[2,1152,128]{2,1,0:T(8,128)(2,1)S(1)} %collective-permute-done.17.refs_2_) | copy-start | bytes 1769476
  159.4 0.8 copy-start.11
  160.2 0.6 copy-start.12

commit v4 on v3

--- a/solution.py
+++ b/solution.py
@@ -28,10 +28,6 @@
 
 def exchange(shard, axes):
     return lax.all_to_all(shard, axes, split_axis=0, concat_axis=0, tiled=True)
-
-
-def gathered(shard, axes, count):
-    return exchange(jnp.broadcast_to(shard[None], (count,) + shard.shape), axes)
 
 
 def ring_gather(piece):
@@ -116,20 +112,23 @@
 
 
 def regroup(got):
+    vmem = pl.BlockSpec(memory_space=pltpu.VMEM)
     return pl.pallas_call(
         regroup_kernel,
+        in_specs=[vmem],
+        out_specs=vmem,
         out_shape=jax.ShapeDtypeStruct((ZH, ZL, 2 * X, LANES), jnp.float32),
         cost_estimate=pl.CostEstimate(flops=1 << 17, bytes_accessed=1 << 19, transcendentals=0),
+        compiler_params=pltpu.CompilerParams(vmem_limit_bytes=8 << 20),
         name="regroup",
     )(got)
 
 
-def transform_kernel(got, *refs):
-    coefs, out = refs[:Y], refs[Y]
+def transform_kernel(got, near, other, out):
     nao = out.shape[2]
-    here = lax.axis_index("y")
-    totals = [0.0, 0.0]
-    for coef, shift in zip(coefs, (0, 1, 3, 2)):
+    here, core = lax.axis_index("y"), lax.axis_index("c")
+    totals = [[0.0, 0.0], [0.0, 0.0]]
+    for slot, shift in enumerate((0, 1, 3, 2)):
         block = lax.rem(here - shift + Y, Y)
         tiles = [got[Y * h + block] + got[ZL + Y * h + block] for h in range(2)]
         rest = jnp.concatenate(tiles, axis=0)
@@ -139,27 +138,35 @@
             rest = rest - terms[-1].astype(jnp.float32)
         terms = jnp.concatenate(terms, axis=0)
         for side in range(2):
-            part = lax.dot_general(
-                terms, coef[side], (((1,), (1,)), ((), ())), preferred_element_type=jnp.float32
-            )
-            totals[side] += (part[:16] + part[16:32]) + part[32:]
+            source = core if side == 0 else 1 - core
+            for index, coef in enumerate((near, other)):
+                got_part = lax.dot_general(
+                    terms, coef[slot, source], (((1,), (1,)), ((), ())), preferred_element_type=jnp.float32
+                )
+                totals[index][side] += (got_part[:16] + got_part[16:32]) + got_part[32:]
+    first = core == 0
+    both = []
+    for side in range(2):
+        low = jnp.where(first, totals[0][side], totals[1][side])
+        high = jnp.where(first, totals[1][side], totals[0][side])
+        both.append(jnp.concatenate([low, high], axis=1))
     for source in range(X):
         for h in range(2):
             row = h * 2 * X + 2 * source
-            line = totals[0][row : row + 1] + totals[1][row + 1 : row + 2]
-            out[2 * source + h] = line[:, :nao]
-
-
-def transform(got, coefs, nao):
+            out[2 * source + h] = (both[0][row : row + 1] + both[1][row + 1 : row + 2])[:, :nao]
+
+
+def transform(got, near, other, nao):
     vmem = pl.BlockSpec(memory_space=pltpu.VMEM)
     return pl.pallas_call(
         transform_kernel,
         out_shape=jax.ShapeDtypeStruct((2 * X, 1, nao), jnp.float32),
-        in_specs=[vmem] * (1 + Y),
+        in_specs=[vmem] * 3,
         out_specs=vmem,
         cost_estimate=pl.CostEstimate(flops=1 << 24, bytes_accessed=3 << 20, transcendentals=0),
+        compiler_params=pltpu.CompilerParams(vmem_limit_bytes=16 << 20),
         name="transform",
-    )(got, *coefs)
+    )(got, near, other)
 
 
 def on_device(density, chol_vectors, virt_coef):
@@ -190,22 +197,22 @@
     other = lax.ppermute(given, "x", PAIR)
     pieces = [kept, swap(kept, "c"), other, swap(other, "c")]
 
-    coef = virt_coef.T
-    part = -(-nao // (X * C * 16)) * 16
-    coef = jnp.pad(coef, ((0, X * C * part - nao), (0, LANES - virt_rows)))
-    far = lax.dynamic_slice(coef, ((here * C + core) * part, 0), (part, LANES))
-    far = swap(far, "zh")
-    far = gathered(far, ("x", "c"), X * C).reshape(X * C * part, LANES)
-    pair = jnp.where(half == core, jnp.stack([coef, far]), jnp.stack([far, coef]))
+    part = -(-nao // (C * LANES)) * LANES
+    coef = jnp.pad(virt_coef.T, ((0, C * part - nao), (0, LANES - virt_rows)))
+    mine = lax.dynamic_slice(coef, (core * part, 0), (part, LANES))
+    far = swap(mine, "zh")
+    pair = jnp.where(half == 0, jnp.stack([mine, far]), jnp.stack([far, mine]))
     coefs = [pair]
     for shift in (1, 3, 2):
         coefs.append(lax.ppermute(pair, "y", [(i, (i + shift) % Y) for i in range(Y)]))
+    coefs = jnp.stack(coefs)
+    coefs = [coefs, swap(coefs, "c")]
 
     gamma = contract(own, cross, pieces)
     gamma = exchange(gamma.reshape(X * Y, ZL * ZH * PIECES, LANES), ("x", "y"))
     gamma = regroup(gamma.reshape(X * Y, ZL, ZH * PIECES, LANES))
     gamma = exchange(gamma.reshape(ZH * ZL, 2 * X, LANES), ("zh", "zl"))
-    return transform(gamma, coefs, nao)
+    return transform(gamma, *coefs, nao)
 
 
 def solution(mesh):

time: 165 us -> 185 us (1.12)
  the two profiles are of different devices: /device:TPU:96 before, /device:TPU:32 now
where the time goes in v4:
time: 185 us; the launch traced here: 184 us
  starting transfers between devices  94.7 us (51%)
  waiting for transfers between devices  59.5 us (32%)
  blocking collectives  13.6 us (7%)
  Pallas kernels  9.66 us (5%)
  local copies, waits for them, and re-layouts  5.82 us (3%)
    ppermute x1, waiting for transfers between devices, on_device(): got = lax.ppermute(sent, 'x', PAIR)  20.6 us
    ppermute x4, starting transfers between devices, swap(): return lax.ppermute(shard, axis, [(0, 1), (1, 0)])  20.6 us
    all_to_all x1, starting transfers between devices, exchange(): return lax.all_to_all(shard, axes, split_axis=0, concat_axis=0, tiled=True)  16.4 us
    ppermute x4, waiting for transfers between devices, on_device(): lax.ppermute(jnp.concatenate(own[first:last], axis=0), 'x', CROSS)  14.8 us
    ppermute x4, starting transfers between devices, on_device(): lax.ppermute(jnp.concatenate(own[first:last], axis=0), 'x', CROSS)  14.1 us
    ppermute x3, starting transfers between devices, ring_gather(): down = lax.ppermute(down, 'zl', fold_ring(-1))  13.7 us
    all_to_all x1, blocking collectives, exchange(): return lax.all_to_all(shard, axes, split_axis=0, concat_axis=0, tiled=True)  13.6 us
    all_to_all x1, waiting for transfers between devices, exchange(): return lax.all_to_all(shard, axes, split_axis=0, concat_axis=0, tiled=True)  11.8 us
  transfers between devices with their start and end apart: 21, of which 7 were waited for; matrix products, arithmetic and copies ran while one was open for 0% of the time, Pallas kernels for 4%

profile of v4, /device:TPU:32, one launch (start us, length us, event | category | flops | bytes accessed | tf_op | source)
XLA Modules:
  0.0 184.2 jit_solution(10477005014282828327)
XLA Ops:
  0.0 4.7 %pad_dynamic-slice_fusion = (bf16[6400,128]{1,0:T(8,128)(2,1)S(1)}, bf16[6400,128]{1,0:T(8,128)(2,1)}) fusion(s32[]{:T(128)S(6)} %select_n.50, bf16[12500,125]{1,0:T(8,128)(2,1)} %bitcast.16, s32[]{:T(128)S(6)} %select_n.49), kind=kLoop, calls=%fused_computation | loop fusion | bytes 6401808 | tf_op jit(solution)/shard_map/dynamic_slice | solution.py:196
  4.7 3.4 %collective-permute-start.13 = (bf16[6400,128]{1,0:T(8,128)(2,1)S(1)}, bf16[6400,128]{1,0:T(8,128)(2,1)}, u32[]{:S(2)}, u32[]{:S(2)}) collective-permute-start(bf16[6400,128]{1,0:T(8,128)(2,1)S(1)} %get-tuple-element.5), channel_id=1, source_target_pairs={{0,128},{128,0},{256,384},{384,256},{1,129},{129,1},{257,385},{385... | collective-permute-start | bytes 4915208 | tf_op jit(solution)/shard_map/ppermute | solution.py:197
  8.1 0.0 copy-done.8
  8.1 2.4 %collective-permute-start = (bf16[8,6400]{1,0:T(8,128)(2,1)S(1)}, bf16[8,6400]{1,0:T(8,128)(2,1)S(1)}, u32[]{:S(2)}, u32[]{:S(2)}) collective-permute-start(bf16[8,6400]{1,0:T(8,128)(2,1)S(1)} %pad_dynamic-slice_fusion.3), channel_id=1, source_target_pairs={{0,128},{128,0},{256,384},{384,256},{1,129},{129,1},{257,385},{385... | collective-permute-start | bytes 307208 | tf_op jit(solution)/shard_map/ppermute | solution.py:186
  10.6 0.0 copy-done
  10.6 0.1 pad_dynamic-slice_fusion.2
  10.7 14.8 %collective-permute-start.15 = (bf16[640,128]{1,0:T(8,128)(2,1)S(1)}, bf16[640,128]{1,0:T(8,128)(2,1)S(1)}, u32[]{:S(2)}, u32[]{:S(2)}) collective-permute-start(bf16[640,128]{1,0:T(8,128)(2,1)S(1)} %pad_dynamic-slice_fusion.2), channel_id=1, source_target_pairs={{0,1},{1,0},{2,3},{3,2},{4,5},{5,4},{6,7},{7,6},{8,9},{9,8},{10,11... | collective-permute-start | bytes 491528 | tf_op jit(solution)/shard_map/ppermute | solution.py:26
  25.6 0.1 fusion.1
  25.7 20.6 %collective-permute-done = bf16[8,6400]{1,0:T(8,128)(2,1)S(1)} collective-permute-done((bf16[8,6400]{1,0:T(8,128)(2,1)S(1)}, bf16[8,6400]{1,0:T(8,128)(2,1)S(1)}, u32[]{:S(2)}, u32[]{:S(2)}) %collective-permute-start) | collective-permute-done | bytes 102432 | tf_op jit(solution)/shard_map/ppermute | solution.py:186
  46.3 0.1 broadcast_select_fusion.1
  46.4 0.0 collective-permute-done.15
  46.4 3.5 %collective-permute-start.16 = (bf16[2,640,128]{2,1,0:T(8,128)(2,1)S(1)}, bf16[2,640,128]{2,1,0:T(8,128)(2,1)S(1)}, u32[]{:S(2)}, u32[]{:S(2)}) collective-permute-start(bf16[2,640,128]{2,1,0:T(8,128)(2,1)S(1)} %maximum_select_fusion.1), channel_id=1, source_target_pairs={{0,2},{2,4},{4,6},{6,0},{1,3},{3,5},{5,7},{7,1},{8,10},{10,12},{12... | collective-permute-start | bytes 983048 | tf_op jit(solution)/shard_map/ppermute | solution.py:207
  49.9 2.0 %collective-permute-start.1 = (bf16[16,6400]{1,0:T(8,128)(2,1)S(1)}, bf16[16,6400]{1,0:T(8,128)(2,1)S(1)}, u32[]{:S(2)}, u32[]{:S(2)}) collective-permute-start(bf16[16,6400]{1,0:T(8,128)(2,1)S(1)} %pad_maximum_fusion.4.refs_0_), channel_id=1, source_target_pairs={{0,32},{32,64},{64,96},{96,112},{112,80},{80,48},{48,16},{16,0},{1... | collective-permute-start | bytes 614408 | tf_op jit(solution)/shard_map/ppermute | solution.py:37
  52.0 5.1 %collective-permute-start.2 = (bf16[16,6400]{1,0:T(8,128)(2,1)S(1)}, bf16[16,6400]{1,0:T(8,128)(2,1)S(1)}, u32[]{:S(2)}, u32[]{:S(2)}) collective-permute-start(bf16[16,6400]{1,0:T(8,128)(2,1)S(1)} %pad_maximum_fusion.4.refs_0_), channel_id=1, source_target_pairs={{0,16},{32,0},{64,32},{96,64},{112,96},{80,112},{48,80},{16,48},{1... | collective-permute-start | bytes 614408 | tf_op jit(solution)/shard_map/ppermute | solution.py:38
  57.1 0.1 fusion
  57.2 3.6 %collective-permute-start.17 = (bf16[2,640,128]{2,1,0:T(8,128)(2,1)S(1)}, bf16[2,640,128]{2,1,0:T(8,128)(2,1)S(1)}, u32[]{:S(2)}, u32[]{:S(2)}) collective-permute-start(bf16[2,640,128]{2,1,0:T(8,128)(2,1)S(1)} %maximum_select_fusion.1), channel_id=1, source_target_pairs={{0,6},{2,0},{4,2},{6,4},{1,7},{3,1},{5,3},{7,5},{8,14},{10,8},{12,... | collective-permute-start | bytes 983048 | tf_op jit(solution)/shard_map/ppermute | solution.py:207
  60.8 0.0 collective-permute-done.1.refs_1_
  60.8 0.0 copy-start.1
  60.8 3.9 %collective-permute-start.18 = (bf16[2,640,128]{2,1,0:T(8,128)(2,1)S(1)}, bf16[2,640,128]{2,1,0:T(8,128)(2,1)S(1)}, u32[]{:S(2)}, u32[]{:S(2)}) collective-permute-start(bf16[2,640,128]{2,1,0:T(8,128)(2,1)S(1)} %maximum_select_fusion.1), channel_id=1, source_target_pairs={{0,4},{2,6},{4,0},{6,2},{1,5},{3,7},{5,1},{7,3},{8,12},{10,14},{12... | collective-permute-start | bytes 983048 | tf_op jit(solution)/shard_map/ppermute | solution.py:207
  64.7 0.0 collective-permute-done.2.refs_2_
  64.7 2.7 %collective-permute-start.3 = (bf16[16,6400]{1,0:T(8,128)(2,1)S(1)}, bf16[16,6400]{1,0:T(8,128)(2,1)S(1)}, u32[]{:S(2)}, u32[]{:S(2)}) collective-permute-start(bf16[16,6400]{1,0:T(8,128)(2,1)S(1)} %collective-permute-done.1.refs_1_), channel_id=1, source_target_pairs={{0,32},{32,64},{64,96},{96,112},{112,80},{80,48},{48,16},{16,0},{1... | collective-permute-start | bytes 614408 | tf_op jit(solution)/shard_map/ppermute | solution.py:37
  67.4 0.0 collective-permute-done.16
  67.4 5.6 %collective-permute-start.4 = (bf16[16,6400]{1,0:T(8,128)(2,1)S(1)}, bf16[16,6400]{1,0:T(8,128)(2,1)S(1)}, u32[]{:S(2)}, u32[]{:S(2)}) collective-permute-start(bf16[16,6400]{1,0:T(8,128)(2,1)S(1)} %collective-permute-done.2.refs_2_), channel_id=1, source_target_pairs={{0,16},{32,0},{64,32},{96,64},{112,96},{80,112},{48,80},{16,48},{1... | collective-permute-start | bytes 614408 | tf_op jit(solution)/shard_map/ppermute | solution.py:38
  73.1 0.1 pad_maximum_fusion.1
  73.1 0.0 collective-permute-done.17
  73.2 1.9 %collective-permute-start.12 = (bf16[6400,128]{1,0:T(8,128)(2,1)}, bf16[6400,128]{1,0:T(8,128)(2,1)}, u32[]{:S(2)}, u32[]{:S(2)}) collective-permute-start(bf16[6400,128]{1,0:T(8,128)(2,1)} %get-tuple-element.6.refs_12_), channel_id=1, source_target_pairs={{0,8},{8,0},{1,9},{9,1},{2,10},{10,2},{3,11},{11,3},{4,12},{12,4},... | collective-permute-start | bytes 4915208 | tf_op jit(solution)/shard_map/ppermute | solution.py:26
  75.1 0.0 collective-permute-done.18
  75.1 4.7 %collective-permute-start.8 = (bf16[48,6400]{1,0:T(8,128)(2,1)S(1)}, bf16[48,6400]{1,0:T(8,128)(2,1)S(1)}, u32[]{:S(2)}, u32[]{:S(2)}) collective-permute-start(bf16[48,6400]{1,0:T(8,128)(2,1)S(1)} %pad_maximum_fusion.1), channel_id=1, source_target_pairs={{128,256},{256,128},{384,0},{0,384},{129,257},{257,129},{385,1},{1... | collective-permute-start | bytes 1843208 | tf_op jit(solution)/shard_map/ppermute | solution.py:190
  79.8 0.2 pad_maximum_fusion.near
  80.0 0.0 collective-permute-done.3.refs_3_
  80.0 0.0 copy-start.4
  80.0 4.9 %collective-permute-start.5 = (bf16[16,6400]{1,0:T(8,128)(2,1)S(1)}, bf16[16,6400]{1,0:T(8,128)(2,1)S(1)}, u32[]{:S(2)}, u32[]{:S(2)}) collective-permute-start(bf16[16,6400]{1,0:T(8,128)(2,1)S(1)} %collective-permute-done.3.refs_3_), channel_id=1, source_target_pairs={{0,32},{32,64},{64,96},{96,112},{112,80},{80,48},{48,16},{16,0},{1... | collective-permute-start | bytes 614408 | tf_op jit(solution)/shard_map/ppermute | solution.py:37
  84.9 0.0 collective-permute-done.4.refs_4_
  85.0 3.0 %collective-permute-start.6 = (bf16[16,6400]{1,0:T(8,128)(2,1)S(1)}, bf16[16,6400]{1,0:T(8,128)(2,1)S(1)}, u32[]{:S(2)}, u32[]{:S(2)}) collective-permute-start(bf16[16,6400]{1,0:T(8,128)(2,1)S(1)} %collective-permute-done.4.refs_4_), channel_id=1, source_target_pairs={{0,16},{32,0},{64,32},{96,64},{112,96},{80,112},{48,80},{16,48},{1... | collective-permute-start | bytes 614408 | tf_op jit(solution)/shard_map/ppermute | solution.py:38
  88.0 0.0 collective-permute-done.13.refs_14_
  88.0 1.9 %collective-permute-start.14 = (bf16[6400,128]{1,0:T(8,128)(2,1)}, bf16[6400,128]{1,0:T(8,128)(2,1)}, u32[]{:S(2)}, u32[]{:S(2)}) collective-permute-start(bf16[6400,128]{1,0:T(8,128)(2,1)} %collective-permute-done.13.refs_14_), channel_id=1, source_target_pairs={{0,8},{8,0},{1,9},{9,1},{2,10},{10,2},{3,11},{11,3},{4,12},{12,4},... | collective-permute-start | bytes 4915208 | tf_op jit(solution)/shard_map/ppermute | solution.py:26
  90.0 0.0 copy-done.4
  90.0 1.5 collective-permute-done.5.refs_5_
  91.5 0.0 copy-done.5
  91.5 1.9 %collective-permute-start.19 = (bf16[4,2,640,128]{3,2,1,0:T(8,128)(2,1)S(1)}, bf16[4,2,640,128]{3,2,1,0:T(8,128)(2,1)S(1)}, u32[]{:S(2)}, u32[]{:S(2)}) collective-permute-start(bf16[4,2,640,128]{3,2,1,0:T(8,128)(2,1)S(1)} %pad_maximum_fusion.near), channel_id=1, source_target_pairs={{0,8},{8,0},{1,9},{9,1},{2,10},{10,2},{3,11},{11,3},{4,12},{12,4},... | collective-permute-start | bytes 3932168 | tf_op jit(solution)/shard_map/ppermute | solution.py:26
  93.4 5.8 %collective-permute-done.6.refs_6_ = bf16[16,6400]{1,0:T(8,128)(2,1)S(1)} collective-permute-done((bf16[16,6400]{1,0:T(8,128)(2,1)S(1)}, bf16[16,6400]{1,0:T(8,128)(2,1)S(1)}, u32[]{:S(2)}, u32[]{:S(2)}) %collective-permute-start.6) | collective-permute-done | bytes 204832 | tf_op jit(solution)/shard_map/ppermute | solution.py:38
  99.2 2.4 %collective-permute-start.9 = (bf16[32,6400]{1,0:T(8,128)(2,1)S(1)}, bf16[32,6400]{1,0:T(8,128)(2,1)S(1)}, u32[]{:S(2)}, u32[]{:S(2)}) collective-permute-start(bf16[32,6400]{1,0:T(8,128)(2,1)S(1)} %pad_maximum_fusion.2), channel_id=1, source_target_pairs={{128,256},{256,128},{384,0},{0,384},{129,257},{257,129},{385,1},{1... | collective-permute-start | bytes 1228808 | tf_op jit(solution)/shard_map/ppermute | solution.py:190
  101.6 0.0 collective-permute-done.8.refs_8_
  101.6 0.0 copy-start.9
  101.6 4.7 %collective-permute-start.10 = (bf16[32,6400]{1,0:T(8,128)(2,1)S(1)}, bf16[32,6400]{1,0:T(8,128)(2,1)S(1)}, u32[]{:S(2)}, u32[]{:S(2)}) collective-permute-start(bf16[32,6400]{1,0:T(8,128)(2,1)S(1)} %pad_maximum_fusion.3), channel_id=1, source_target_pairs={{128,256},{256,128},{384,0},{0,384},{129,257},{257,129},{385,1},{1... | collective-permute-start | bytes 1228808 | tf_op jit(solution)/shard_map/ppermute | solution.py:190
  106.3 8.3 %collective-permute-done.9.refs_9_ = bf16[32,6400]{1,0:T(8,128)(2,1)S(1)} collective-permute-done((bf16[32,6400]{1,0:T(8,128)(2,1)S(1)}, bf16[32,6400]{1,0:T(8,128)(2,1)S(1)}, u32[]{:S(2)}, u32[]{:S(2)}) %collective-permute-start.9) | collective-permute-done | bytes 409632 | tf_op jit(solution)/shard_map/ppermute | solution.py:190
  114.6 3.5 %collective-permute-start.7 = (bf16[16,6400]{1,0:T(8,128)(2,1)S(1)}, bf16[16,6400]{1,0:T(8,128)(2,1)S(1)}, u32[]{:S(2)}, u32[]{:S(2)}) collective-permute-start(bf16[16,6400]{1,0:T(8,128)(2,1)S(1)} %collective-permute-done.5.refs_5_), channel_id=1, source_target_pairs={{0,32},{32,64},{64,96},{96,112},{112,80},{80,48},{48,16},{16,0},{1... | collective-permute-start | bytes 614408 | tf_op jit(solution)/shard_map/ppermute | solution.py:40
  118.1 5.0 %collective-permute-done.7.refs_7_ = bf16[16,6400]{1,0:T(8,128)(2,1)S(1)} collective-permute-done((bf16[16,6400]{1,0:T(8,128)(2,1)S(1)}, bf16[16,6400]{1,0:T(8,128)(2,1)S(1)}, u32[]{:S(2)}, u32[]{:S(2)}) %collective-permute-start.7) | collective-permute-done | bytes 204832 | tf_op jit(solution)/shard_map/ppermute | solution.py:40
  123.1 2.4 %collective-permute-start.11 = (bf16[16,6400]{1,0:T(8,128)(2,1)S(1)}, bf16[16,6400]{1,0:T(8,128)(2,1)S(1)}, u32[]{:S(2)}, u32[]{:S(2)}) collective-permute-start(bf16[16,6400]{1,0:T(8,128)(2,1)S(1)} %collective-permute-done.7.refs_7_), channel_id=1, source_target_pairs={{128,256},{256,128},{384,0},{0,384},{129,257},{257,129},{385,1},{1... | collective-permute-start | bytes 614408 | tf_op jit(solution)/shard_map/ppermute | solution.py:190
  125.5 0.0 collective-permute-done.10.refs_10_
  125.5 0.0 copy-done.10
  125.6 0.0 copy-start.11
  125.6 6.4 %collective-permute-done.11.refs_11_ = bf16[16,6400]{1,0:T(8,128)(2,1)S(1)} collective-permute-done((bf16[16,6400]{1,0:T(8,128)(2,1)S(1)}, bf16[16,6400]{1,0:T(8,128)(2,1)S(1)}, u32[]{:S(2)}, u32[]{:S(2)}) %collective-permute-start.11) | collective-permute-done | bytes 204832 | tf_op jit(solution)/shard_map/ppermute | solution.py:190
  132.0 0.0 collective-permute-done.12.refs_13_
  132.0 0.7 copy-done.13
  132.7 0.0 collective-permute-done.14.refs_15_
  132.7 0.0 copy-done.12
  132.7 7.4 %contract.1 = f32[1024,128]{1,0:T(8,128)} custom-call(bf16[16,6400]{1,0:T(8,128)(2,1)} %copy-done.3, bf16[16,6400]{1,0:T(8,128)(2,1)} %copy-done.1, bf16[16,6400]{1,0:T(8,128)(2,1)} %copy-done.2, bf16[16,6400]{1,0:T(8,128)(2,1)} %copy-done.4, bf16[16,6400]{1,0:T(8,128)(2,1)} %copy-done.5, bf16[16,6400]{1,0:T(8,128)(2,1)} %copy-done.6, ...), custom_call_target="tpu_custom_call" | custom-call | flops 1677721600 | bytes 10485760 | tf_op jit(solution)/shard_map/contract/pallas_call | solution.py:87
  140.1 13.6 %all_to_all.10 = f32[16,64,128]{2,1,0:T(8,128)S(1)} all-to-all(f32[16,64,128]{2,1,0:T(8,128)} %bitcast.20), channel_id=1, replica_groups=mesh['x'=4,'zl'=8,'c'=2,'y'=4,'zh'=2] {'x','y'}, dimensions={0} | all-to-all | bytes 1048576 | tf_op jit(solution)/shard_map/all_to_all | solution.py:30
  153.7 0.7 regroup.1
  154.4 16.4 %all-to-all-start.1 = ((f32[16,8,128]{2,1,0:T(8,128)}), f32[16,8,128]{2,1,0:T(8,128)S(1)}, u32[]{:S(2)}, u32[]{:S(2)}) async-start(f32[16,8,128]{2,1,0:T(8,128)} %bitcast.4), calls=%async_computation.1 | async-start | bytes 131072 | tf_op jit(solution)/shard_map/all_to_all | solution.py:30
  170.8 0.0 collective-permute-done.19.other
  170.8 11.8 %all-to-all-done.1.got = f32[16,8,128]{2,1,0:T(8,128)S(1)} async-done(((f32[16,8,128]{2,1,0:T(8,128)}), f32[16,8,128]{2,1,0:T(8,128)S(1)}, u32[]{:S(2)}, u32[]{:S(2)}) %all-to-all-start.1) | async-done | bytes 65568 | tf_op jit(solution)/shard_map/all_to_all | solution.py:30
  182.6 1.6 transform.1
  (23 shorter events, 0.2 us)
Async XLA Ops:
  0.0 8.1 %copy-start.8 = (bf16[12500,8]{0,1:T(8,128)(2,1)S(1)}, bf16[12500,8]{0,1:T(8,128)(2,1)}, u32[]{:S(2)}) copy-start(bf16[12500,8]{0,1:T(8,128)(2,1)} %param.4) | copy-start | bytes 600004
  0.0 10.6 %copy-start = (bf16[125,1100]{0,1:T(8,128)(2,1)S(1)}, bf16[125,1100]{0,1:T(8,128)(2,1)}, u32[]{:S(2)}) copy-start(bf16[125,1100]{0,1:T(8,128)(2,1)} %param.5) | copy-start | bytes 825004
  4.7 83.3 %collective-permute-start.13 = (bf16[6400,128]{1,0:T(8,128)(2,1)S(1)}, bf16[6400,128]{1,0:T(8,128)(2,1)}, u32[]{:S(2)}, u32[]{:S(2)}) collective-permute-start(bf16[6400,128]{1,0:T(8,128)(2,1)S(1)} %get-tuple-element.5), channel_id=1, source_target_pairs={{0,128},{128,0},{256,384},{384,256},{1,129},{129,1},{257,385},{385... | collective-permute-start | bytes 4915208 | tf_op jit(solution)/shard_map/ppermute | solution.py:197
  8.1 38.2 %collective-permute-start = (bf16[8,6400]{1,0:T(8,128)(2,1)S(1)}, bf16[8,6400]{1,0:T(8,128)(2,1)S(1)}, u32[]{:S(2)}, u32[]{:S(2)}) collective-permute-start(bf16[8,6400]{1,0:T(8,128)(2,1)S(1)} %pad_dynamic-slice_fusion.3), channel_id=1, source_target_pairs={{0,128},{128,0},{256,384},{384,256},{1,129},{129,1},{257,385},{385... | collective-permute-start | bytes 307208 | tf_op jit(solution)/shard_map/ppermute | solution.py:186
  10.7 35.6 %collective-permute-start.15 = (bf16[640,128]{1,0:T(8,128)(2,1)S(1)}, bf16[640,128]{1,0:T(8,128)(2,1)S(1)}, u32[]{:S(2)}, u32[]{:S(2)}) collective-permute-start(bf16[640,128]{1,0:T(8,128)(2,1)S(1)} %pad_dynamic-slice_fusion.2), channel_id=1, source_target_pairs={{0,1},{1,0},{2,3},{3,2},{4,5},{5,4},{6,7},{7,6},{8,9},{9,8},{10,11... | collective-permute-start | bytes 491528 | tf_op jit(solution)/shard_map/ppermute | solution.py:26
  46.4 21.0 %collective-permute-start.16 = (bf16[2,640,128]{2,1,0:T(8,128)(2,1)S(1)}, bf16[2,640,128]{2,1,0:T(8,128)(2,1)S(1)}, u32[]{:S(2)}, u32[]{:S(2)}) collective-permute-start(bf16[2,640,128]{2,1,0:T(8,128)(2,1)S(1)} %maximum_select_fusion.1), channel_id=1, source_target_pairs={{0,2},{2,4},{4,6},{6,0},{1,3},{3,5},{5,7},{7,1},{8,10},{10,12},{12... | collective-permute-start | bytes 983048 | tf_op jit(solution)/shard_map/ppermute | solution.py:207
  49.9 29.8 %copy-start.3 = (bf16[16,6400]{1,0:T(8,128)(2,1)}, bf16[16,6400]{1,0:T(8,128)(2,1)S(1)}, u32[]{:S(2)}) copy-start(bf16[16,6400]{1,0:T(8,128)(2,1)S(1)} %pad_maximum_fusion.4.refs_0_) | copy-start | bytes 614404
  49.9 10.9 %collective-permute-start.1 = (bf16[16,6400]{1,0:T(8,128)(2,1)S(1)}, bf16[16,6400]{1,0:T(8,128)(2,1)S(1)}, u32[]{:S(2)}, u32[]{:S(2)}) collective-permute-start(bf16[16,6400]{1,0:T(8,128)(2,1)S(1)} %pad_maximum_fusion.4.refs_0_), channel_id=1, source_target_pairs={{0,32},{32,64},{64,96},{96,112},{112,80},{80,48},{48,16},{16,0},{1... | collective-permute-start | bytes 614408 | tf_op jit(solution)/shard_map/ppermute | solution.py:37
  52.0 12.8 %collective-permute-start.2 = (bf16[16,6400]{1,0:T(8,128)(2,1)S(1)}, bf16[16,6400]{1,0:T(8,128)(2,1)S(1)}, u32[]{:S(2)}, u32[]{:S(2)}) collective-permute-start(bf16[16,6400]{1,0:T(8,128)(2,1)S(1)} %pad_maximum_fusion.4.refs_0_), channel_id=1, source_target_pairs={{0,16},{32,0},{64,32},{96,64},{112,96},{80,112},{48,80},{16,48},{1... | collective-permute-start | bytes 614408 | tf_op jit(solution)/shard_map/ppermute | solution.py:38
  57.2 16.0 %collective-permute-start.17 = (bf16[2,640,128]{2,1,0:T(8,128)(2,1)S(1)}, bf16[2,640,128]{2,1,0:T(8,128)(2,1)S(1)}, u32[]{:S(2)}, u32[]{:S(2)}) collective-permute-start(bf16[2,640,128]{2,1,0:T(8,128)(2,1)S(1)} %maximum_select_fusion.1), channel_id=1, source_target_pairs={{0,6},{2,0},{4,2},{6,4},{1,7},{3,1},{5,3},{7,5},{8,14},{10,8},{12,... | collective-permute-start | bytes 983048 | tf_op jit(solution)/shard_map/ppermute | solution.py:207
  60.8 19.1 %copy-start.1 = (bf16[16,6400]{1,0:T(8,128)(2,1)}, bf16[16,6400]{1,0:T(8,128)(2,1)S(1)}, u32[]{:S(2)}) copy-start(bf16[16,6400]{1,0:T(8,128)(2,1)S(1)} %collective-permute-done.1.refs_1_) | copy-start | bytes 614404
  60.8 14.3 %collective-permute-start.18 = (bf16[2,640,128]{2,1,0:T(8,128)(2,1)S(1)}, bf16[2,640,128]{2,1,0:T(8,128)(2,1)S(1)}, u32[]{:S(2)}, u32[]{:S(2)}) collective-permute-start(bf16[2,640,128]{2,1,0:T(8,128)(2,1)S(1)} %maximum_select_fusion.1), channel_id=1, source_target_pairs={{0,4},{2,6},{4,0},{6,2},{1,5},{3,7},{5,1},{7,3},{8,12},{10,14},{12... | collective-permute-start | bytes 983048 | tf_op jit(solution)/shard_map/ppermute | solution.py:207
  64.7 15.2 %copy-start.2 = (bf16[16,6400]{1,0:T(8,128)(2,1)}, bf16[16,6400]{1,0:T(8,128)(2,1)S(1)}, u32[]{:S(2)}) copy-start(bf16[16,6400]{1,0:T(8,128)(2,1)S(1)} %collective-permute-done.2.refs_2_) | copy-start | bytes 614404
  64.7 15.2 %collective-permute-start.3 = (bf16[16,6400]{1,0:T(8,128)(2,1)S(1)}, bf16[16,6400]{1,0:T(8,128)(2,1)S(1)}, u32[]{:S(2)}, u32[]{:S(2)}) collective-permute-start(bf16[16,6400]{1,0:T(8,128)(2,1)S(1)} %collective-permute-done.1.refs_1_), channel_id=1, source_target_pairs={{0,32},{32,64},{64,96},{96,112},{112,80},{80,48},{48,16},{16,0},{1... | collective-permute-start | bytes 614408 | tf_op jit(solution)/shard_map/ppermute | solution.py:37
  67.4 17.5 %collective-permute-start.4 = (bf16[16,6400]{1,0:T(8,128)(2,1)S(1)}, bf16[16,6400]{1,0:T(8,128)(2,1)S(1)}, u32[]{:S(2)}, u32[]{:S(2)}) collective-permute-start(bf16[16,6400]{1,0:T(8,128)(2,1)S(1)} %collective-permute-done.2.refs_2_), channel_id=1, source_target_pairs={{0,16},{32,0},{64,32},{96,64},{112,96},{80,112},{48,80},{16,48},{1... | collective-permute-start | bytes 614408 | tf_op jit(solution)/shard_map/ppermute | solution.py:38
  73.2 58.9 %collective-permute-start.12 = (bf16[6400,128]{1,0:T(8,128)(2,1)}, bf16[6400,128]{1,0:T(8,128)(2,1)}, u32[]{:S(2)}, u32[]{:S(2)}) collective-permute-start(bf16[6400,128]{1,0:T(8,128)(2,1)} %get-tuple-element.6.refs_12_), channel_id=1, source_target_pairs={{0,8},{8,0},{1,9},{9,1},{2,10},{10,2},{3,11},{11,3},{4,12},{12,4},... | collective-permute-start | bytes 4915208 | tf_op jit(solution)/shard_map/ppermute | solution.py:26
  75.1 26.5 %collective-permute-start.8 = (bf16[48,6400]{1,0:T(8,128)(2,1)S(1)}, bf16[48,6400]{1,0:T(8,128)(2,1)S(1)}, u32[]{:S(2)}, u32[]{:S(2)}) collective-permute-start(bf16[48,6400]{1,0:T(8,128)(2,1)S(1)} %pad_maximum_fusion.1), channel_id=1, source_target_pairs={{128,256},{256,128},{384,0},{0,384},{129,257},{257,129},{385,1},{1... | collective-permute-start | bytes 1843208 | tf_op jit(solution)/shard_map/ppermute | solution.py:190
  80.0 10.0 %copy-start.4 = (bf16[16,6400]{1,0:T(8,128)(2,1)}, bf16[16,6400]{1,0:T(8,128)(2,1)S(1)}, u32[]{:S(2)}) copy-start(bf16[16,6400]{1,0:T(8,128)(2,1)S(1)} %collective-permute-done.3.refs_3_) | copy-start | bytes 614404
  80.0 11.5 %collective-permute-start.5 = (bf16[16,6400]{1,0:T(8,128)(2,1)S(1)}, bf16[16,6400]{1,0:T(8,128)(2,1)S(1)}, u32[]{:S(2)}, u32[]{:S(2)}) collective-permute-start(bf16[16,6400]{1,0:T(8,128)(2,1)S(1)} %collective-permute-done.3.refs_3_), channel_id=1, source_target_pairs={{0,32},{32,64},{64,96},{96,112},{112,80},{80,48},{48,16},{16,0},{1... | collective-permute-start | bytes 614408 | tf_op jit(solution)/shard_map/ppermute | solution.py:37
  84.9 6.5 %copy-start.5 = (bf16[16,6400]{1,0:T(8,128)(2,1)}, bf16[16,6400]{1,0:T(8,128)(2,1)S(1)}, u32[]{:S(2)}) copy-start(bf16[16,6400]{1,0:T(8,128)(2,1)S(1)} %collective-permute-done.4.refs_4_) | copy-start | bytes 614404
  85.0 14.2 %collective-permute-start.6 = (bf16[16,6400]{1,0:T(8,128)(2,1)S(1)}, bf16[16,6400]{1,0:T(8,128)(2,1)S(1)}, u32[]{:S(2)}, u32[]{:S(2)}) collective-permute-start(bf16[16,6400]{1,0:T(8,128)(2,1)S(1)} %collective-permute-done.4.refs_4_), channel_id=1, source_target_pairs={{0,16},{32,0},{64,32},{96,64},{112,96},{80,112},{48,80},{16,48},{1... | collective-permute-start | bytes 614408 | tf_op jit(solution)/shard_map/ppermute | solution.py:38
  88.0 44.7 %collective-permute-start.14 = (bf16[6400,128]{1,0:T(8,128)(2,1)}, bf16[6400,128]{1,0:T(8,128)(2,1)}, u32[]{:S(2)}, u32[]{:S(2)}) collective-permute-start(bf16[6400,128]{1,0:T(8,128)(2,1)} %collective-permute-done.13.refs_14_), channel_id=1, source_target_pairs={{0,8},{8,0},{1,9},{9,1},{2,10},{10,2},{3,11},{11,3},{4,12},{12,4},... | collective-permute-start | bytes 4915208 | tf_op jit(solution)/shard_map/ppermute | solution.py:26
  91.5 41.2 %copy-start.6 = (bf16[16,6400]{1,0:T(8,128)(2,1)}, bf16[16,6400]{1,0:T(8,128)(2,1)S(1)}, u32[]{:S(2)}) copy-start(bf16[16,6400]{1,0:T(8,128)(2,1)S(1)} %collective-permute-done.5.refs_5_) | copy-start | bytes 614404
  91.5 79.3 %collective-permute-start.19 = (bf16[4,2,640,128]{3,2,1,0:T(8,128)(2,1)S(1)}, bf16[4,2,640,128]{3,2,1,0:T(8,128)(2,1)S(1)}, u32[]{:S(2)}, u32[]{:S(2)}) collective-permute-start(bf16[4,2,640,128]{3,2,1,0:T(8,128)(2,1)S(1)} %pad_maximum_fusion.near), channel_id=1, source_target_pairs={{0,8},{8,0},{1,9},{9,1},{2,10},{10,2},{3,11},{11,3},{4,12},{12,4},... | collective-permute-start | bytes 3932168 | tf_op jit(solution)/shard_map/ppermute | solution.py:26
  99.2 33.5 %copy-start.7 = (bf16[16,6400]{1,0:T(8,128)(2,1)}, bf16[16,6400]{1,0:T(8,128)(2,1)S(1)}, u32[]{:S(2)}) copy-start(bf16[16,6400]{1,0:T(8,128)(2,1)S(1)} %collective-permute-done.6.refs_6_) | copy-start | bytes 614404
  99.2 15.4 %collective-permute-start.9 = (bf16[32,6400]{1,0:T(8,128)(2,1)S(1)}, bf16[32,6400]{1,0:T(8,128)(2,1)S(1)}, u32[]{:S(2)}, u32[]{:S(2)}) collective-permute-start(bf16[32,6400]{1,0:T(8,128)(2,1)S(1)} %pad_maximum_fusion.2), channel_id=1, source_target_pairs={{128,256},{256,128},{384,0},{0,384},{129,257},{257,129},{385,1},{1... | collective-permute-start | bytes 1228808 | tf_op jit(solution)/shard_map/ppermute | solution.py:190
  101.6 21.5 %copy-start.9 = (bf16[48,6400]{1,0:T(8,128)(2,1)}, bf16[48,6400]{1,0:T(8,128)(2,1)S(1)}, u32[]{:S(2)}) copy-start(bf16[48,6400]{1,0:T(8,128)(2,1)S(1)} %collective-permute-done.8.refs_8_) | copy-start | bytes 1843204
  101.6 23.9 %collective-permute-start.10 = (bf16[32,6400]{1,0:T(8,128)(2,1)S(1)}, bf16[32,6400]{1,0:T(8,128)(2,1)S(1)}, u32[]{:S(2)}, u32[]{:S(2)}) collective-permute-start(bf16[32,6400]{1,0:T(8,128)(2,1)S(1)} %pad_maximum_fusion.3), channel_id=1, source_target_pairs={{128,256},{256,128},{384,0},{0,384},{129,257},{257,129},{385,1},{1... | collective-permute-start | bytes 1228808 | tf_op jit(solution)/shard_map/ppermute | solution.py:190
  114.6 10.9 %copy-start.10 = (bf16[32,6400]{1,0:T(8,128)(2,1)}, bf16[32,6400]{1,0:T(8,128)(2,1)S(1)}, u32[]{:S(2)}) copy-start(bf16[32,6400]{1,0:T(8,128)(2,1)S(1)} %collective-permute-done.9.refs_9_) | copy-start | bytes 1228804
  114.6 8.5 %collective-permute-start.7 = (bf16[16,6400]{1,0:T(8,128)(2,1)S(1)}, bf16[16,6400]{1,0:T(8,128)(2,1)S(1)}, u32[]{:S(2)}, u32[]{:S(2)}) collective-permute-start(bf16[16,6400]{1,0:T(8,128)(2,1)S(1)} %collective-permute-done.5.refs_5_), channel_id=1, source_target_pairs={{0,32},{32,64},{64,96},{96,112},{112,80},{80,48},{48,16},{16,0},{1... | collective-permute-start | bytes 614408 | tf_op jit(solution)/shard_map/ppermute | solution.py:40
  123.1 9.6 %copy-start.12 = (bf16[16,6400]{1,0:T(8,128)(2,1)}, bf16[16,6400]{1,0:T(8,128)(2,1)S(1)}, u32[]{:S(2)}) copy-start(bf16[16,6400]{1,0:T(8,128)(2,1)S(1)} %collective-permute-done.7.refs_7_) | copy-start | bytes 614404
  123.1 8.9 %collective-permute-start.11 = (bf16[16,6400]{1,0:T(8,128)(2,1)S(1)}, bf16[16,6400]{1,0:T(8,128)(2,1)S(1)}, u32[]{:S(2)}, u32[]{:S(2)}) collective-permute-start(bf16[16,6400]{1,0:T(8,128)(2,1)S(1)} %collective-permute-done.7.refs_7_), channel_id=1, source_target_pairs={{128,256},{256,128},{384,0},{0,384},{129,257},{257,129},{385,1},{1... | collective-permute-start | bytes 614408 | tf_op jit(solution)/shard_map/ppermute | solution.py:190
  125.6 6.5 %copy-start.11 = (bf16[32,6400]{1,0:T(8,128)(2,1)}, bf16[32,6400]{1,0:T(8,128)(2,1)S(1)}, u32[]{:S(2)}) copy-start(bf16[32,6400]{1,0:T(8,128)(2,1)S(1)} %collective-permute-done.10.refs_10_) | copy-start | bytes 1228804
  132.0 0.7 copy-start.13
  154.4 28.2 %all-to-all-start.1 = ((f32[16,8,128]{2,1,0:T(8,128)}), f32[16,8,128]{2,1,0:T(8,128)S(1)}, u32[]{:S(2)}, u32[]{:S(2)}) async-start(f32[16,8,128]{2,1,0:T(8,128)} %bitcast.4), calls=%async_computation.1 | async-start | bytes 131072 | tf_op jit(solution)/shard_map/all_to_all | solution.py:30

commit v5 on v4

--- a/solution.py
+++ b/solution.py
@@ -126,10 +126,10 @@
 
 def transform_kernel(got, near, other, out):
     nao = out.shape[2]
-    here, core = lax.axis_index("y"), lax.axis_index("c")
+    core = lax.axis_index("c")
+    source = jnp.where(core == lax.axis_index("zh"), 0, 1)
     totals = [[0.0, 0.0], [0.0, 0.0]]
-    for slot, shift in enumerate((0, 1, 3, 2)):
-        block = lax.rem(here - shift + Y, Y)
+    for block in range(Y):
         tiles = [got[Y * h + block] + got[ZL + Y * h + block] for h in range(2)]
         rest = jnp.concatenate(tiles, axis=0)
         terms = []
@@ -138,10 +138,9 @@
             rest = rest - terms[-1].astype(jnp.float32)
         terms = jnp.concatenate(terms, axis=0)
         for side in range(2):
-            source = core if side == 0 else 1 - core
             for index, coef in enumerate((near, other)):
                 got_part = lax.dot_general(
-                    terms, coef[slot, source], (((1,), (1,)), ((), ())), preferred_element_type=jnp.float32
+                    terms, coef[block, source if side == 0 else 1 - source], (((1,), (1,)), ((), ())), preferred_element_type=jnp.float32
                 )
                 totals[index][side] += (got_part[:16] + got_part[16:32]) + got_part[32:]
     first = core == 0
@@ -173,7 +172,7 @@
     rows, inner = density.shape
     width = chol_vectors.shape[1]
     virt_rows, nao = virt_coef.shape
-    here, core, half = lax.axis_index("x"), lax.axis_index("c"), lax.axis_index("zh")
+    here, core = lax.axis_index("x"), lax.axis_index("c")
     even = lax.rem(here, 2) == 0
     depth = -(-inner // (2 * BLOCK)) * BLOCK
     pad = 2 * depth - inner
@@ -201,12 +200,9 @@
     coef = jnp.pad(virt_coef.T, ((0, C * part - nao), (0, LANES - virt_rows)))
     mine = lax.dynamic_slice(coef, (core * part, 0), (part, LANES))
     far = swap(mine, "zh")
-    pair = jnp.where(half == 0, jnp.stack([mine, far]), jnp.stack([far, mine]))
-    coefs = [pair]
-    for shift in (1, 3, 2):
-        coefs.append(lax.ppermute(pair, "y", [(i, (i + shift) % Y) for i in range(Y)]))
-    coefs = jnp.stack(coefs)
-    coefs = [coefs, swap(coefs, "c")]
+    pair = jnp.broadcast_to(jnp.stack([mine, far])[None], (Y, ZH, part, LANES))
+    coefs = exchange(pair, "y")
+    coefs = [coefs.reshape(Y, ZH, part, LANES), swap(coefs, "c").reshape(Y, ZH, part, LANES)]
 
     gamma = contract(own, cross, pieces)
     gamma = exchange(gamma.reshape(X * Y, ZL * ZH * PIECES, LANES), ("x", "y"))

time: 185 us -> 174 us (0.941)
  waiting for transfers between devices: 59.5 us -> 48.1 us
  starting transfers between devices: 94.7 us -> 87.1 us
  other arithmetic: 0.45 us -> 4.41 us
  blocking collectives: 13.6 us -> 15.5 us
  local copies, waits for them, and re-layouts: 5.82 us -> 7.71 us
    ppermute x3 -> x0, starting transfers between devices: 10.9 us -> none  [on_device(): lax.ppermute(pair, 'y', [(i, (i + shift) % Y) for i in range(Y)])]
    ppermute x4, waiting for transfers between devices: 14.8 us -> 9.17 us  [on_device(): lax.ppermute(jnp.concatenate(own[first:last], axis=0), 'x', CROSS)]
    ppermute x3, waiting for transfers between devices: 5.78 us -> 1.15 us  [ring_gather(): down = lax.ppermute(down, 'zl', fold_ring(-1))]
    concatenate x3, other arithmetic: 0.11 us -> 3.61 us  [on_device(): jnp.concatenate(own[first:last], axis=0)]
    ppermute x3, starting transfers between devices: 9.62 us -> 6.42 us  [ring_gather(): up = lax.ppermute(up, 'zl', fold_ring(1))]
    ppermute x3, starting transfers between devices: 13.7 us -> 16.9 us  [ring_gather(): down = lax.ppermute(down, 'zl', fold_ring(-1))]
    all_to_all x1 -> x2, starting transfers between devices: 16.4 us -> 19 us  [exchange(): return lax.all_to_all(shard, axes, split_axis=0, concat_axis=0, tiled=True)]
    ppermute x1, waiting for transfers between devices: 5 us -> 7.18 us  [ring_gather(): return parts + [lax.ppermute(up, 'zl', fold_ring(1))]]
  transfers between devices with their start and end apart: 21 -> 19, of which waited for: 7 -> 6; matrix products, arithmetic and copies ran while one was open for 0% -> 3% of each run, Pallas kernels for 4% -> 5%
where the time goes in v5:
time: 174 us; the launch traced here: 173 us
  starting transfers between devices  87.1 us (50%)
  waiting for transfers between devices  48.1 us (28%)
  blocking collectives  15.5 us (9%)
  Pallas kernels  9.67 us (6%)
  local copies, waits for them, and re-layouts  7.71 us (4%)
  other arithmetic  4.41 us (3%)
    ppermute x4, starting transfers between devices, swap(): return lax.ppermute(shard, axis, [(0, 1), (1, 0)])  20.6 us
    all_to_all x2, starting transfers between devices, exchange(): return lax.all_to_all(shard, axes, split_axis=0, concat_axis=0, tiled=True)  19 us
    ppermute x1, waiting for transfers between devices, on_device(): got = lax.ppermute(sent, 'x', PAIR)  18.8 us
    ppermute x3, starting transfers between devices, ring_gather(): down = lax.ppermute(down, 'zl', fold_ring(-1))  16.9 us
    all_to_all x1, blocking collectives, exchange(): return lax.all_to_all(shard, axes, split_axis=0, concat_axis=0, tiled=True)  15.5 us
    ppermute x4, starting transfers between devices, on_device(): lax.ppermute(jnp.concatenate(own[first:last], axis=0), 'x', CROSS)  15.2 us
    all_to_all x2, waiting for transfers between devices, exchange(): return lax.all_to_all(shard, axes, split_axis=0, concat_axis=0, tiled=True)  11.8 us
    ppermute x4, waiting for transfers between devices, on_device(): lax.ppermute(jnp.concatenate(own[first:last], axis=0), 'x', CROSS)  9.17 us
  transfers between devices with their start and end apart: 19, of which 6 were waited for; matrix products, arithmetic and copies ran while one was open for 3% of the time, Pallas kernels for 5%

profile of v5, /device:TPU:32, one launch (start us, length us, event | category | flops | bytes accessed | tf_op | source)
XLA Modules:
  0.0 172.9 jit_solution(1136703901918592759)
XLA Ops:
  0.0 0.0 copy-start.5
  0.0 4.7 %pad_dynamic-slice_fusion = (bf16[6400,128]{1,0:T(8,128)(2,1)S(1)}, bf16[6400,128]{1,0:T(8,128)(2,1)}) fusion(s32[]{:T(128)S(6)} %select_n.31, bf16[12500,125]{1,0:T(8,128)(2,1)} %bitcast.10, s32[]{:T(128)S(6)} %select_n.30), kind=kLoop, calls=%fused_computation | loop fusion | bytes 6401808 | tf_op jit(solution)/shard_map/dynamic_slice | solution.py:195
  4.7 3.4 %collective-permute-start.13 = (bf16[6400,128]{1,0:T(8,128)(2,1)S(1)}, bf16[6400,128]{1,0:T(8,128)(2,1)}, u32[]{:S(2)}, u32[]{:S(2)}) collective-permute-start(bf16[6400,128]{1,0:T(8,128)(2,1)S(1)} %get-tuple-element.5), channel_id=1, source_target_pairs={{0,128},{128,0},{256,384},{384,256},{1,129},{129,1},{257,385},{385... | collective-permute-start | bytes 4915208 | tf_op jit(solution)/shard_map/ppermute | solution.py:196
  8.1 1.9 %collective-permute-start.12 = (bf16[6400,128]{1,0:T(8,128)(2,1)}, bf16[6400,128]{1,0:T(8,128)(2,1)}, u32[]{:S(2)}, u32[]{:S(2)}) collective-permute-start(bf16[6400,128]{1,0:T(8,128)(2,1)} %get-tuple-element.6.refs_12_), channel_id=1, source_target_pairs={{0,8},{8,0},{1,9},{9,1},{2,10},{10,2},{3,11},{11,3},{4,12},{12,4},... | collective-permute-start | bytes 4915208 | tf_op jit(solution)/shard_map/ppermute | solution.py:26
  10.0 0.0 copy-done.5
  10.1 2.4 %collective-permute-start = (bf16[8,6400]{1,0:T(8,128)(2,1)S(1)}, bf16[8,6400]{1,0:T(8,128)(2,1)S(1)}, u32[]{:S(2)}, u32[]{:S(2)}) collective-permute-start(bf16[8,6400]{1,0:T(8,128)(2,1)S(1)} %pad_dynamic-slice_fusion.3), channel_id=1, source_target_pairs={{0,128},{128,0},{256,384},{384,256},{1,129},{129,1},{257,385},{385... | collective-permute-start | bytes 307208 | tf_op jit(solution)/shard_map/ppermute | solution.py:185
  12.5 0.0 copy-done
  12.5 0.1 pad_dynamic-slice_fusion.2
  12.7 14.8 %collective-permute-start.15 = (bf16[640,128]{1,0:T(8,128)(2,1)S(1)}, bf16[640,128]{1,0:T(8,128)(2,1)S(1)}, u32[]{:S(2)}, u32[]{:S(2)}) collective-permute-start(bf16[640,128]{1,0:T(8,128)(2,1)S(1)} %pad_dynamic-slice_fusion.2), channel_id=1, source_target_pairs={{0,1},{1,0},{2,3},{3,2},{4,5},{5,4},{6,7},{7,6},{8,9},{9,8},{10,11... | collective-permute-start | bytes 491528 | tf_op jit(solution)/shard_map/ppermute | solution.py:26
  27.5 18.8 %collective-permute-done = bf16[8,6400]{1,0:T(8,128)(2,1)S(1)} collective-permute-done((bf16[8,6400]{1,0:T(8,128)(2,1)S(1)}, bf16[8,6400]{1,0:T(8,128)(2,1)S(1)}, u32[]{:S(2)}, u32[]{:S(2)}) %collective-permute-start) | collective-permute-done | bytes 102432 | tf_op jit(solution)/shard_map/ppermute | solution.py:185
  46.3 0.1 broadcast_select_fusion.1
  46.3 0.7 pad_maximum_fusion.4.refs_0_
  47.1 1.9 %collective-permute-start.1 = (bf16[16,6400]{1,0:T(8,128)(2,1)}, bf16[16,6400]{1,0:T(8,128)(2,1)S(1)}, u32[]{:S(2)}, u32[]{:S(2)}) collective-permute-start(bf16[16,6400]{1,0:T(8,128)(2,1)} %pad_maximum_fusion.4.refs_0_), channel_id=1, source_target_pairs={{0,32},{32,64},{64,96},{96,112},{112,80},{80,48},{48,16},{16,0},{1... | collective-permute-start | bytes 614408 | tf_op jit(solution)/shard_map/ppermute | solution.py:37
  49.0 5.2 %collective-permute-start.2 = (bf16[16,6400]{1,0:T(8,128)(2,1)}, bf16[16,6400]{1,0:T(8,128)(2,1)}, u32[]{:S(2)}, u32[]{:S(2)}) collective-permute-start(bf16[16,6400]{1,0:T(8,128)(2,1)} %pad_maximum_fusion.4.refs_0_), channel_id=1, source_target_pairs={{0,16},{32,0},{64,32},{96,64},{112,96},{80,112},{48,80},{16,48},{1... | collective-permute-start | bytes 614408 | tf_op jit(solution)/shard_map/ppermute | solution.py:38
  54.2 0.1 fusion
  54.3 0.0 collective-permute-done.15
  54.3 1.2 broadcast_in_dim.2
  55.6 4.5 %all-to-all-start.2 = ((bf16[4,2,640,128]{3,2,1,0:T(8,128)(2,1)}), bf16[4,2,640,128]{3,2,1,0:T(8,128)(2,1)S(1)}, u32[]{:S(2)}, u32[]{:S(2)}) async-start(bf16[4,2,640,128]{3,2,1,0:T(8,128)(2,1)} %broadcast_in_dim.2), calls=%async_computation.2 | async-start | bytes 2621440 | tf_op jit(solution)/shard_map/all_to_all | solution.py:30
  60.0 0.0 collective-permute-done.1.refs_1_
  60.1 2.0 %collective-permute-start.3 = (bf16[16,6400]{1,0:T(8,128)(2,1)S(1)}, bf16[16,6400]{1,0:T(8,128)(2,1)S(1)}, u32[]{:S(2)}, u32[]{:S(2)}) collective-permute-start(bf16[16,6400]{1,0:T(8,128)(2,1)S(1)} %collective-permute-done.1.refs_1_), channel_id=1, source_target_pairs={{0,32},{32,64},{64,96},{96,112},{112,80},{80,48},{48,16},{16,0},{1... | collective-permute-start | bytes 614408 | tf_op jit(solution)/shard_map/ppermute | solution.py:37
  62.1 0.0 collective-permute-done.2.refs_2_
  62.1 6.3 %collective-permute-start.4 = (bf16[16,6400]{1,0:T(8,128)(2,1)}, bf16[16,6400]{1,0:T(8,128)(2,1)S(1)}, u32[]{:S(2)}, u32[]{:S(2)}) collective-permute-start(bf16[16,6400]{1,0:T(8,128)(2,1)} %collective-permute-done.2.refs_2_), channel_id=1, source_target_pairs={{0,16},{32,0},{64,32},{96,64},{112,96},{80,112},{48,80},{16,48},{1... | collective-permute-start | bytes 614408 | tf_op jit(solution)/shard_map/ppermute | solution.py:38
  68.4 1.9 %pad_maximum_fusion = bf16[48,6400]{1,0:T(8,128)(2,1)} fusion(bf16[16,6400]{1,0:T(8,128)(2,1)} %collective-permute-done.2.refs_2_, bf16[16,6400]{1,0:T(8,128)(2,1)S(1)} %collective-permute-done.1.refs_1_, bf16[8,6400]{1,0:T(8,128)(2,1)S(1)} %get-tuple-element.8, bf16[8,6400]{1,0:T(8,128)(2,1)S(1)} %get-tuple-element.7), kind=kLoop, calls=%fused_computation.2 | loop fusion | flops 2457600 | bytes 1228800 | tf_op jit(solution)/shard_map/concatenate | solution.py:189
  70.3 4.7 %collective-permute-start.8 = (bf16[48,6400]{1,0:T(8,128)(2,1)}, bf16[48,6400]{1,0:T(8,128)(2,1)}, u32[]{:S(2)}, u32[]{:S(2)}) collective-permute-start(bf16[48,6400]{1,0:T(8,128)(2,1)} %pad_maximum_fusion), channel_id=1, source_target_pairs={{128,256},{256,128},{384,0},{0,384},{129,257},{257,129},{385,1},{1... | collective-permute-start | bytes 1843208 | tf_op jit(solution)/shard_map/ppermute | solution.py:189
  74.9 0.0 collective-permute-done.3.refs_3_
  74.9 0.0 copy-start.2
  74.9 2.5 %collective-permute-start.5 = (bf16[16,6400]{1,0:T(8,128)(2,1)S(1)}, bf16[16,6400]{1,0:T(8,128)(2,1)S(1)}, u32[]{:S(2)}, u32[]{:S(2)}) collective-permute-start(bf16[16,6400]{1,0:T(8,128)(2,1)S(1)} %collective-permute-done.3.refs_3_), channel_id=1, source_target_pairs={{0,32},{32,64},{64,96},{96,112},{112,80},{80,48},{48,16},{16,0},{1... | collective-permute-start | bytes 614408 | tf_op jit(solution)/shard_map/ppermute | solution.py:37
  77.4 0.0 collective-permute-done.4.refs_4_
  77.5 0.0 copy-start.3
  77.5 5.5 %collective-permute-start.6 = (bf16[16,6400]{1,0:T(8,128)(2,1)S(1)}, bf16[16,6400]{1,0:T(8,128)(2,1)}, u32[]{:S(2)}, u32[]{:S(2)}) collective-permute-start(bf16[16,6400]{1,0:T(8,128)(2,1)S(1)} %collective-permute-done.4.refs_4_), channel_id=1, source_target_pairs={{0,16},{32,0},{64,32},{96,64},{112,96},{80,112},{48,80},{16,48},{1... | collective-permute-start | bytes 614408 | tf_op jit(solution)/shard_map/ppermute | solution.py:38
  82.9 0.0 collective-permute-done.13.refs_14_
  82.9 1.9 %collective-permute-start.14 = (bf16[6400,128]{1,0:T(8,128)(2,1)}, bf16[6400,128]{1,0:T(8,128)(2,1)}, u32[]{:S(2)}, u32[]{:S(2)}) collective-permute-start(bf16[6400,128]{1,0:T(8,128)(2,1)} %collective-permute-done.13.refs_14_), channel_id=1, source_target_pairs={{0,8},{8,0},{1,9},{9,1},{2,10},{10,2},{3,11},{11,3},{4,12},{12,4},... | collective-permute-start | bytes 4915208 | tf_op jit(solution)/shard_map/ppermute | solution.py:26
  84.9 0.8 pad_maximum_fusion.1
  85.6 0.0 collective-permute-done.5.refs_5_
  85.7 2.9 %collective-permute-start.9 = (bf16[32,6400]{1,0:T(8,128)(2,1)}, bf16[32,6400]{1,0:T(8,128)(2,1)}, u32[]{:S(2)}, u32[]{:S(2)}) collective-permute-start(bf16[32,6400]{1,0:T(8,128)(2,1)} %pad_maximum_fusion.1), channel_id=1, source_target_pairs={{128,256},{256,128},{384,0},{0,384},{129,257},{257,129},{385,1},{1... | collective-permute-start | bytes 1228808 | tf_op jit(solution)/shard_map/ppermute | solution.py:189
  88.6 0.0 copy-done.2
  88.6 0.0 copy-done.3
  88.6 1.1 collective-permute-done.6.refs_6_
  89.7 0.0 all-to-all-done.2.near
  89.7 1.9 %collective-permute-start.16 = (bf16[4,2,640,128]{3,2,1,0:T(8,128)(2,1)S(1)}, bf16[4,2,640,128]{3,2,1,0:T(8,128)(2,1)S(1)}, u32[]{:S(2)}, u32[]{:S(2)}) collective-permute-start(bf16[4,2,640,128]{3,2,1,0:T(8,128)(2,1)S(1)} %all-to-all-done.2.near), channel_id=1, source_target_pairs={{0,8},{8,0},{1,9},{9,1},{2,10},{10,2},{3,11},{11,3},{4,12},{12,4},... | collective-permute-start | bytes 3932168 | tf_op jit(solution)/shard_map/ppermute | solution.py:26
  91.7 1.0 pad_maximum_fusion.2
  92.6 0.0 collective-permute-done.8.refs_8_
  92.6 4.4 %collective-permute-start.10 = (bf16[32,6400]{1,0:T(8,128)(2,1)S(1)}, bf16[32,6400]{1,0:T(8,128)(2,1)S(1)}, u32[]{:S(2)}, u32[]{:S(2)}) collective-permute-start(bf16[32,6400]{1,0:T(8,128)(2,1)S(1)} %pad_maximum_fusion.2), channel_id=1, source_target_pairs={{128,256},{256,128},{384,0},{0,384},{129,257},{257,129},{385,1},{1... | collective-permute-start | bytes 1228808 | tf_op jit(solution)/shard_map/ppermute | solution.py:189
  97.0 4.4 %collective-permute-done.9.refs_9_ = bf16[32,6400]{1,0:T(8,128)(2,1)} collective-permute-done((bf16[32,6400]{1,0:T(8,128)(2,1)}, bf16[32,6400]{1,0:T(8,128)(2,1)}, u32[]{:S(2)}, u32[]{:S(2)}) %collective-permute-start.9) | collective-permute-done | bytes 409632 | tf_op jit(solution)/shard_map/ppermute | solution.py:189
  101.4 3.2 %collective-permute-start.7 = (bf16[16,6400]{1,0:T(8,128)(2,1)S(1)}, bf16[16,6400]{1,0:T(8,128)(2,1)S(1)}, u32[]{:S(2)}, u32[]{:S(2)}) collective-permute-start(bf16[16,6400]{1,0:T(8,128)(2,1)S(1)} %collective-permute-done.5.refs_5_), channel_id=1, source_target_pairs={{0,32},{32,64},{64,96},{96,112},{112,80},{80,48},{48,16},{16,0},{1... | collective-permute-start | bytes 614408 | tf_op jit(solution)/shard_map/ppermute | solution.py:40
  104.6 7.2 %collective-permute-done.7.refs_7_ = bf16[16,6400]{1,0:T(8,128)(2,1)S(1)} collective-permute-done((bf16[16,6400]{1,0:T(8,128)(2,1)S(1)}, bf16[16,6400]{1,0:T(8,128)(2,1)S(1)}, u32[]{:S(2)}, u32[]{:S(2)}) %collective-permute-start.7) | collective-permute-done | bytes 204832 | tf_op jit(solution)/shard_map/ppermute | solution.py:40
  111.8 3.2 %collective-permute-start.11 = (bf16[16,6400]{1,0:T(8,128)(2,1)S(1)}, bf16[16,6400]{1,0:T(8,128)(2,1)S(1)}, u32[]{:S(2)}, u32[]{:S(2)}) collective-permute-start(bf16[16,6400]{1,0:T(8,128)(2,1)S(1)} %collective-permute-done.7.refs_7_), channel_id=1, source_target_pairs={{128,256},{256,128},{384,0},{0,384},{129,257},{257,129},{385,1},{1... | collective-permute-start | bytes 614408 | tf_op jit(solution)/shard_map/ppermute | solution.py:189
  115.1 0.0 collective-permute-done.10.refs_10_
  115.1 0.0 copy-start.6
  115.1 0.8 copy-done.6
  115.9 4.8 %collective-permute-done.11.refs_11_ = bf16[16,6400]{1,0:T(8,128)(2,1)S(1)} collective-permute-done((bf16[16,6400]{1,0:T(8,128)(2,1)S(1)}, bf16[16,6400]{1,0:T(8,128)(2,1)S(1)}, u32[]{:S(2)}, u32[]{:S(2)}) %collective-permute-start.11) | collective-permute-done | bytes 204832 | tf_op jit(solution)/shard_map/ppermute | solution.py:189
  120.7 0.7 copy-done.8
  121.4 0.0 collective-permute-done.12.refs_13_
  121.4 0.0 collective-permute-done.14.refs_15_
  121.4 0.0 copy-done.1
  121.4 0.0 copy-done.4
  121.4 0.0 copy-done.7
  121.4 7.4 %contract.1 = f32[1024,128]{1,0:T(8,128)} custom-call(bf16[16,6400]{1,0:T(8,128)(2,1)} %pad_maximum_fusion.4.refs_0_, bf16[16,6400]{1,0:T(8,128)(2,1)} %copy-done.1, bf16[16,6400]{1,0:T(8,128)(2,1)} %collective-permute-done.2.refs_2_, bf16[16,6400]{1,0:T(8,128)(2,1)} %copy-done.2, bf16[16,6400]{1,0:T(8,128)(2,1)} %copy-done.3, bf16[16,6400]{1,0:T(8,128)(2,1)} %copy-done.4, ...), custom_call_target="tpu_custom_call" | custom-call | flops 1677721600 | bytes 10485760 | tf_op jit(solution)/shard_map/contract/pallas_call | solution.py:87
  128.8 15.5 %all_to_all.15 = f32[16,64,128]{2,1,0:T(8,128)S(1)} all-to-all(f32[16,64,128]{2,1,0:T(8,128)} %bitcast.11), channel_id=1, replica_groups=mesh['x'=4,'zl'=8,'c'=2,'y'=4,'zh'=2] {'x','y'}, dimensions={0} | all-to-all | bytes 1048576 | tf_op jit(solution)/shard_map/all_to_all | solution.py:30
  144.2 0.7 regroup.1
  144.9 14.5 %all-to-all-start.1 = ((f32[16,8,128]{2,1,0:T(8,128)}), f32[16,8,128]{2,1,0:T(8,128)S(1)}, u32[]{:S(2)}, u32[]{:S(2)}) async-start(f32[16,8,128]{2,1,0:T(8,128)} %bitcast.4), calls=%async_computation.1 | async-start | bytes 131072 | tf_op jit(solution)/shard_map/all_to_all | solution.py:30
  159.4 0.0 collective-permute-done.16.other
  159.4 11.8 %all-to-all-done.1.got = f32[16,8,128]{2,1,0:T(8,128)S(1)} async-done(((f32[16,8,128]{2,1,0:T(8,128)}), f32[16,8,128]{2,1,0:T(8,128)S(1)}, u32[]{:S(2)}, u32[]{:S(2)}) %all-to-all-start.1) | async-done | bytes 65568 | tf_op jit(solution)/shard_map/all_to_all | solution.py:30
  171.2 1.7 transform.1
  (7 shorter events, 0.1 us)
Async XLA Ops:
  0.0 10.0 %copy-start.5 = (bf16[12500,8]{0,1:T(8,128)(2,1)S(1)}, bf16[12500,8]{0,1:T(8,128)(2,1)}, u32[]{:S(2)}) copy-start(bf16[12500,8]{0,1:T(8,128)(2,1)} %param.4) | copy-start | bytes 600004
  0.0 12.5 %copy-start = (bf16[125,1100]{0,1:T(8,128)(2,1)S(1)}, bf16[125,1100]{0,1:T(8,128)(2,1)}, u32[]{:S(2)}) copy-start(bf16[125,1100]{0,1:T(8,128)(2,1)} %param.5) | copy-start | bytes 825004
  4.7 78.3 %collective-permute-start.13 = (bf16[6400,128]{1,0:T(8,128)(2,1)S(1)}, bf16[6400,128]{1,0:T(8,128)(2,1)}, u32[]{:S(2)}, u32[]{:S(2)}) collective-permute-start(bf16[6400,128]{1,0:T(8,128)(2,1)S(1)} %get-tuple-element.5), channel_id=1, source_target_pairs={{0,128},{128,0},{256,384},{384,256},{1,129},{129,1},{257,385},{385... | collective-permute-start | bytes 4915208 | tf_op jit(solution)/shard_map/ppermute | solution.py:196
  8.1 113.3 %collective-permute-start.12 = (bf16[6400,128]{1,0:T(8,128)(2,1)}, bf16[6400,128]{1,0:T(8,128)(2,1)}, u32[]{:S(2)}, u32[]{:S(2)}) collective-permute-start(bf16[6400,128]{1,0:T(8,128)(2,1)} %get-tuple-element.6.refs_12_), channel_id=1, source_target_pairs={{0,8},{8,0},{1,9},{9,1},{2,10},{10,2},{3,11},{11,3},{4,12},{12,4},... | collective-permute-start | bytes 4915208 | tf_op jit(solution)/shard_map/ppermute | solution.py:26
  10.1 36.2 %collective-permute-start = (bf16[8,6400]{1,0:T(8,128)(2,1)S(1)}, bf16[8,6400]{1,0:T(8,128)(2,1)S(1)}, u32[]{:S(2)}, u32[]{:S(2)}) collective-permute-start(bf16[8,6400]{1,0:T(8,128)(2,1)S(1)} %pad_dynamic-slice_fusion.3), channel_id=1, source_target_pairs={{0,128},{128,0},{256,384},{384,256},{1,129},{129,1},{257,385},{385... | collective-permute-start | bytes 307208 | tf_op jit(solution)/shard_map/ppermute | solution.py:185
  12.7 41.6 %collective-permute-start.15 = (bf16[640,128]{1,0:T(8,128)(2,1)S(1)}, bf16[640,128]{1,0:T(8,128)(2,1)S(1)}, u32[]{:S(2)}, u32[]{:S(2)}) collective-permute-start(bf16[640,128]{1,0:T(8,128)(2,1)S(1)} %pad_dynamic-slice_fusion.2), channel_id=1, source_target_pairs={{0,1},{1,0},{2,3},{3,2},{4,5},{5,4},{6,7},{7,6},{8,9},{9,8},{10,11... | collective-permute-start | bytes 491528 | tf_op jit(solution)/shard_map/ppermute | solution.py:26
  47.1 13.0 %collective-permute-start.1 = (bf16[16,6400]{1,0:T(8,128)(2,1)}, bf16[16,6400]{1,0:T(8,128)(2,1)S(1)}, u32[]{:S(2)}, u32[]{:S(2)}) collective-permute-start(bf16[16,6400]{1,0:T(8,128)(2,1)} %pad_maximum_fusion.4.refs_0_), channel_id=1, source_target_pairs={{0,32},{32,64},{64,96},{96,112},{112,80},{80,48},{48,16},{16,0},{1... | collective-permute-start | bytes 614408 | tf_op jit(solution)/shard_map/ppermute | solution.py:37
  49.0 13.1 %collective-permute-start.2 = (bf16[16,6400]{1,0:T(8,128)(2,1)}, bf16[16,6400]{1,0:T(8,128)(2,1)}, u32[]{:S(2)}, u32[]{:S(2)}) collective-permute-start(bf16[16,6400]{1,0:T(8,128)(2,1)} %pad_maximum_fusion.4.refs_0_), channel_id=1, source_target_pairs={{0,16},{32,0},{64,32},{96,64},{112,96},{80,112},{48,80},{16,48},{1... | collective-permute-start | bytes 614408 | tf_op jit(solution)/shard_map/ppermute | solution.py:38
  55.6 34.2 %all-to-all-start.2 = ((bf16[4,2,640,128]{3,2,1,0:T(8,128)(2,1)}), bf16[4,2,640,128]{3,2,1,0:T(8,128)(2,1)S(1)}, u32[]{:S(2)}, u32[]{:S(2)}) async-start(bf16[4,2,640,128]{3,2,1,0:T(8,128)(2,1)} %broadcast_in_dim.2), calls=%async_computation.2 | async-start | bytes 2621440 | tf_op jit(solution)/shard_map/all_to_all | solution.py:30
  60.0 61.3 %copy-start.1 = (bf16[16,6400]{1,0:T(8,128)(2,1)}, bf16[16,6400]{1,0:T(8,128)(2,1)S(1)}, u32[]{:S(2)}) copy-start(bf16[16,6400]{1,0:T(8,128)(2,1)S(1)} %collective-permute-done.1.refs_1_) | copy-start | bytes 614404
  60.1 14.9 %collective-permute-start.3 = (bf16[16,6400]{1,0:T(8,128)(2,1)S(1)}, bf16[16,6400]{1,0:T(8,128)(2,1)S(1)}, u32[]{:S(2)}, u32[]{:S(2)}) collective-permute-start(bf16[16,6400]{1,0:T(8,128)(2,1)S(1)} %collective-permute-done.1.refs_1_), channel_id=1, source_target_pairs={{0,32},{32,64},{64,96},{96,112},{112,80},{80,48},{48,16},{16,0},{1... | collective-permute-start | bytes 614408 | tf_op jit(solution)/shard_map/ppermute | solution.py:37
  62.1 15.4 %collective-permute-start.4 = (bf16[16,6400]{1,0:T(8,128)(2,1)}, bf16[16,6400]{1,0:T(8,128)(2,1)S(1)}, u32[]{:S(2)}, u32[]{:S(2)}) collective-permute-start(bf16[16,6400]{1,0:T(8,128)(2,1)} %collective-permute-done.2.refs_2_), channel_id=1, source_target_pairs={{0,16},{32,0},{64,32},{96,64},{112,96},{80,112},{48,80},{16,48},{1... | collective-permute-start | bytes 614408 | tf_op jit(solution)/shard_map/ppermute | solution.py:38
  70.3 22.4 %collective-permute-start.8 = (bf16[48,6400]{1,0:T(8,128)(2,1)}, bf16[48,6400]{1,0:T(8,128)(2,1)}, u32[]{:S(2)}, u32[]{:S(2)}) collective-permute-start(bf16[48,6400]{1,0:T(8,128)(2,1)} %pad_maximum_fusion), channel_id=1, source_target_pairs={{128,256},{256,128},{384,0},{0,384},{129,257},{257,129},{385,1},{1... | collective-permute-start | bytes 1843208 | tf_op jit(solution)/shard_map/ppermute | solution.py:189
  74.9 13.6 %copy-start.2 = (bf16[16,6400]{1,0:T(8,128)(2,1)}, bf16[16,6400]{1,0:T(8,128)(2,1)S(1)}, u32[]{:S(2)}) copy-start(bf16[16,6400]{1,0:T(8,128)(2,1)S(1)} %collective-permute-done.3.refs_3_) | copy-start | bytes 614404
  74.9 10.7 %collective-permute-start.5 = (bf16[16,6400]{1,0:T(8,128)(2,1)S(1)}, bf16[16,6400]{1,0:T(8,128)(2,1)S(1)}, u32[]{:S(2)}, u32[]{:S(2)}) collective-permute-start(bf16[16,6400]{1,0:T(8,128)(2,1)S(1)} %collective-permute-done.3.refs_3_), channel_id=1, source_target_pairs={{0,32},{32,64},{64,96},{96,112},{112,80},{80,48},{48,16},{16,0},{1... | collective-permute-start | bytes 614408 | tf_op jit(solution)/shard_map/ppermute | solution.py:37
  77.5 11.1 %copy-start.3 = (bf16[16,6400]{1,0:T(8,128)(2,1)}, bf16[16,6400]{1,0:T(8,128)(2,1)S(1)}, u32[]{:S(2)}) copy-start(bf16[16,6400]{1,0:T(8,128)(2,1)S(1)} %collective-permute-done.4.refs_4_) | copy-start | bytes 614404
  77.5 12.3 %collective-permute-start.6 = (bf16[16,6400]{1,0:T(8,128)(2,1)S(1)}, bf16[16,6400]{1,0:T(8,128)(2,1)}, u32[]{:S(2)}, u32[]{:S(2)}) collective-permute-start(bf16[16,6400]{1,0:T(8,128)(2,1)S(1)} %collective-permute-done.4.refs_4_), channel_id=1, source_target_pairs={{0,16},{32,0},{64,32},{96,64},{112,96},{80,112},{48,80},{16,48},{1... | collective-permute-start | bytes 614408 | tf_op jit(solution)/shard_map/ppermute | solution.py:38
  82.9 38.4 %collective-permute-start.14 = (bf16[6400,128]{1,0:T(8,128)(2,1)}, bf16[6400,128]{1,0:T(8,128)(2,1)}, u32[]{:S(2)}, u32[]{:S(2)}) collective-permute-start(bf16[6400,128]{1,0:T(8,128)(2,1)} %collective-permute-done.13.refs_14_), channel_id=1, source_target_pairs={{0,8},{8,0},{1,9},{9,1},{2,10},{10,2},{3,11},{11,3},{4,12},{12,4},... | collective-permute-start | bytes 4915208 | tf_op jit(solution)/shard_map/ppermute | solution.py:26
  85.6 35.7 %copy-start.4 = (bf16[16,6400]{1,0:T(8,128)(2,1)}, bf16[16,6400]{1,0:T(8,128)(2,1)S(1)}, u32[]{:S(2)}) copy-start(bf16[16,6400]{1,0:T(8,128)(2,1)S(1)} %collective-permute-done.5.refs_5_) | copy-start | bytes 614404
  85.7 15.8 %collective-permute-start.9 = (bf16[32,6400]{1,0:T(8,128)(2,1)}, bf16[32,6400]{1,0:T(8,128)(2,1)}, u32[]{:S(2)}, u32[]{:S(2)}) collective-permute-start(bf16[32,6400]{1,0:T(8,128)(2,1)} %pad_maximum_fusion.1), channel_id=1, source_target_pairs={{128,256},{256,128},{384,0},{0,384},{129,257},{257,129},{385,1},{1... | collective-permute-start | bytes 1228808 | tf_op jit(solution)/shard_map/ppermute | solution.py:189
  89.7 69.7 %collective-permute-start.16 = (bf16[4,2,640,128]{3,2,1,0:T(8,128)(2,1)S(1)}, bf16[4,2,640,128]{3,2,1,0:T(8,128)(2,1)S(1)}, u32[]{:S(2)}, u32[]{:S(2)}) collective-permute-start(bf16[4,2,640,128]{3,2,1,0:T(8,128)(2,1)S(1)} %all-to-all-done.2.near), channel_id=1, source_target_pairs={{0,8},{8,0},{1,9},{9,1},{2,10},{10,2},{3,11},{11,3},{4,12},{12,4},... | collective-permute-start | bytes 3932168 | tf_op jit(solution)/shard_map/ppermute | solution.py:26
  92.6 22.4 %collective-permute-start.10 = (bf16[32,6400]{1,0:T(8,128)(2,1)S(1)}, bf16[32,6400]{1,0:T(8,128)(2,1)S(1)}, u32[]{:S(2)}, u32[]{:S(2)}) collective-permute-start(bf16[32,6400]{1,0:T(8,128)(2,1)S(1)} %pad_maximum_fusion.2), channel_id=1, source_target_pairs={{128,256},{256,128},{384,0},{0,384},{129,257},{257,129},{385,1},{1... | collective-permute-start | bytes 1228808 | tf_op jit(solution)/shard_map/ppermute | solution.py:189
  101.4 10.4 %collective-permute-start.7 = (bf16[16,6400]{1,0:T(8,128)(2,1)S(1)}, bf16[16,6400]{1,0:T(8,128)(2,1)S(1)}, u32[]{:S(2)}, u32[]{:S(2)}) collective-permute-start(bf16[16,6400]{1,0:T(8,128)(2,1)S(1)} %collective-permute-done.5.refs_5_), channel_id=1, source_target_pairs={{0,32},{32,64},{64,96},{96,112},{112,80},{80,48},{48,16},{16,0},{1... | collective-permute-start | bytes 614408 | tf_op jit(solution)/shard_map/ppermute | solution.py:40
  111.8 9.6 %copy-start.7 = (bf16[16,6400]{1,0:T(8,128)(2,1)}, bf16[16,6400]{1,0:T(8,128)(2,1)S(1)}, u32[]{:S(2)}) copy-start(bf16[16,6400]{1,0:T(8,128)(2,1)S(1)} %collective-permute-done.7.refs_7_) | copy-start | bytes 614404
  111.8 8.9 %collective-permute-start.11 = (bf16[16,6400]{1,0:T(8,128)(2,1)S(1)}, bf16[16,6400]{1,0:T(8,128)(2,1)S(1)}, u32[]{:S(2)}, u32[]{:S(2)}) collective-permute-start(bf16[16,6400]{1,0:T(8,128)(2,1)S(1)} %collective-permute-done.7.refs_7_), channel_id=1, source_target_pairs={{128,256},{256,128},{384,0},{0,384},{129,257},{257,129},{385,1},{1... | collective-permute-start | bytes 614408 | tf_op jit(solution)/shard_map/ppermute | solution.py:189
  115.1 0.8 copy-start.6
  120.7 0.7 copy-start.8
  144.9 26.3 %all-to-all-start.1 = ((f32[16,8,128]{2,1,0:T(8,128)}), f32[16,8,128]{2,1,0:T(8,128)S(1)}, u32[]{:S(2)}, u32[]{:S(2)}) async-start(f32[16,8,128]{2,1,0:T(8,128)} %bitcast.4), calls=%async_computation.1 | async-start | bytes 131072 | tf_op jit(solution)/shard_map/all_to_all | solution.py:30

commit v6 on v5

--- a/solution.py
+++ b/solution.py
@@ -14,7 +14,7 @@
 PAIR = [(0, 1), (1, 0), (2, 3), (3, 2)]
 CROSS = [(1, 2), (2, 1), (3, 0), (0, 3)]
 LANES = 128
-BLOCK = 10 * LANES
+BLOCK = 25 * LANES
 PIECES = 4
 
 
@@ -199,7 +199,8 @@
     part = -(-nao // (C * LANES)) * LANES
     coef = jnp.pad(virt_coef.T, ((0, C * part - nao), (0, LANES - virt_rows)))
     mine = lax.dynamic_slice(coef, (core * part, 0), (part, LANES))
-    far = swap(mine, "zh")
+    mirror = [(z * ZH + h, (ZL - 1 - z) * ZH + 1 - h) for z in range(ZL) for h in range(ZH)]
+    far = lax.ppermute(mine, ("zl", "zh"), mirror)
     pair = jnp.broadcast_to(jnp.stack([mine, far])[None], (Y, ZH, part, LANES))
     coefs = exchange(pair, "y")
     coefs = [coefs.reshape(Y, ZH, part, LANES), swap(coefs, "c").reshape(Y, ZH, part, LANES)]

time: 174 us -> 173 us (level)
  waiting for transfers between devices: 48.1 us -> 51.6 us
  starting transfers between devices: 87.1 us -> 83.7 us
    ppermute x4 -> x3, starting transfers between devices: 20.6 us -> 5.75 us  [swap(): return lax.ppermute(shard, axis, [(0, 1), (1, 0)])]
    ppermute x0 -> x1, starting transfers between devices: none -> 11.4 us  [on_device(): far = lax.ppermute(mine, ('zl', 'zh'), mirror)]
    ppermute x1, waiting for transfers between devices: 18.8 us -> 22.2 us  [on_device(): got = lax.ppermute(sent, 'x', PAIR)]
  transfers between devices with their start and end apart: 19 -> 19, of which waited for: 6 -> 6; matrix products, arithmetic and copies ran while one was open for 3% -> 3% of each run, Pallas kernels for 5% -> 4%
where the time goes in v6:
time: 173 us; the launch traced here: 172 us
  starting transfers between devices  83.7 us (48%)
  waiting for transfers between devices  51.6 us (30%)
  blocking collectives  15.5 us (9%)
  Pallas kernels  8.42 us (5%)
  local copies, waits for them, and re-layouts  7.71 us (4%)
  other arithmetic  4.41 us (3%)
    ppermute x1, waiting for transfers between devices, on_device(): got = lax.ppermute(sent, 'x', PAIR)  22.2 us
    all_to_all x2, starting transfers between devices, exchange(): return lax.all_to_all(shard, axes, split_axis=0, concat_axis=0, tiled=True)  19 us
    ppermute x3, starting transfers between devices, ring_gather(): down = lax.ppermute(down, 'zl', fold_ring(-1))  16.9 us
    all_to_all x1, blocking collectives, exchange(): return lax.all_to_all(shard, axes, split_axis=0, concat_axis=0, tiled=True)  15.5 us
    ppermute x4, starting transfers between devices, on_device(): lax.ppermute(jnp.concatenate(own[first:last], axis=0), 'x', CROSS)  15.2 us
    all_to_all x2, waiting for transfers between devices, exchange(): return lax.all_to_all(shard, axes, split_axis=0, concat_axis=0, tiled=True)  11.8 us
    ppermute x1, starting transfers between devices, on_device(): far = lax.ppermute(mine, ('zl', 'zh'), mirror)  11.4 us
    ppermute x4, waiting for transfers between devices, on_device(): lax.ppermute(jnp.concatenate(own[first:last], axis=0), 'x', CROSS)  9.17 us
  transfers between devices with their start and end apart: 19, of which 6 were waited for; matrix products, arithmetic and copies ran while one was open for 3% of the time, Pallas kernels for 4%

profile of v6, /device:TPU:32, one launch (start us, length us, event | category | flops | bytes accessed | tf_op | source)
XLA Modules:
  0.0 171.6 jit_solution(11718032980835355950)
XLA Ops:
  0.0 0.0 copy-start.5
  0.0 4.7 %pad_dynamic-slice_fusion = (bf16[6400,128]{1,0:T(8,128)(2,1)S(1)}, bf16[6400,128]{1,0:T(8,128)(2,1)}) fusion(s32[]{:T(128)S(6)} %select_n.31, bf16[12500,125]{1,0:T(8,128)(2,1)} %bitcast.10, s32[]{:T(128)S(6)} %select_n.30), kind=kLoop, calls=%fused_computation | loop fusion | bytes 6401808 | tf_op jit(solution)/shard_map/dynamic_slice | solution.py:195
  4.7 3.4 %collective-permute-start.13 = (bf16[6400,128]{1,0:T(8,128)(2,1)S(1)}, bf16[6400,128]{1,0:T(8,128)(2,1)}, u32[]{:S(2)}, u32[]{:S(2)}) collective-permute-start(bf16[6400,128]{1,0:T(8,128)(2,1)S(1)} %get-tuple-element.5), channel_id=1, source_target_pairs={{0,128},{128,0},{256,384},{384,256},{1,129},{129,1},{257,385},{385... | collective-permute-start | bytes 4915208 | tf_op jit(solution)/shard_map/ppermute | solution.py:196
  8.1 1.9 %collective-permute-start.12 = (bf16[6400,128]{1,0:T(8,128)(2,1)}, bf16[6400,128]{1,0:T(8,128)(2,1)}, u32[]{:S(2)}, u32[]{:S(2)}) collective-permute-start(bf16[6400,128]{1,0:T(8,128)(2,1)} %get-tuple-element.6.refs_12_), channel_id=1, source_target_pairs={{0,8},{8,0},{1,9},{9,1},{2,10},{10,2},{3,11},{11,3},{4,12},{12,4},... | collective-permute-start | bytes 4915208 | tf_op jit(solution)/shard_map/ppermute | solution.py:26
  10.0 0.0 copy-done.5
  10.1 2.4 %collective-permute-start = (bf16[8,6400]{1,0:T(8,128)(2,1)S(1)}, bf16[8,6400]{1,0:T(8,128)(2,1)S(1)}, u32[]{:S(2)}, u32[]{:S(2)}) collective-permute-start(bf16[8,6400]{1,0:T(8,128)(2,1)S(1)} %pad_dynamic-slice_fusion.3), channel_id=1, source_target_pairs={{0,128},{128,0},{256,384},{384,256},{1,129},{129,1},{257,385},{385... | collective-permute-start | bytes 307208 | tf_op jit(solution)/shard_map/ppermute | solution.py:185
  12.5 0.0 copy-done
  12.5 0.1 pad_dynamic-slice_fusion.2
  12.7 11.4 %collective-permute-start.15 = (bf16[640,128]{1,0:T(8,128)(2,1)S(1)}, bf16[640,128]{1,0:T(8,128)(2,1)S(1)}, u32[]{:S(2)}, u32[]{:S(2)}) collective-permute-start(bf16[640,128]{1,0:T(8,128)(2,1)S(1)} %pad_dynamic-slice_fusion.2), channel_id=1, source_target_pairs={{0,113},{1,112},{16,97},{17,96},{32,81},{33,80},{48,65},{49,64},{6... | collective-permute-start | bytes 491528 | tf_op jit(solution)/shard_map/ppermute | solution.py:203
  24.1 22.2 %collective-permute-done = bf16[8,6400]{1,0:T(8,128)(2,1)S(1)} collective-permute-done((bf16[8,6400]{1,0:T(8,128)(2,1)S(1)}, bf16[8,6400]{1,0:T(8,128)(2,1)S(1)}, u32[]{:S(2)}, u32[]{:S(2)}) %collective-permute-start) | collective-permute-done | bytes 102432 | tf_op jit(solution)/shard_map/ppermute | solution.py:185
  46.3 0.1 broadcast_select_fusion.1
  46.3 0.7 pad_maximum_fusion.4.refs_0_
  47.1 1.9 %collective-permute-start.1 = (bf16[16,6400]{1,0:T(8,128)(2,1)}, bf16[16,6400]{1,0:T(8,128)(2,1)S(1)}, u32[]{:S(2)}, u32[]{:S(2)}) collective-permute-start(bf16[16,6400]{1,0:T(8,128)(2,1)} %pad_maximum_fusion.4.refs_0_), channel_id=1, source_target_pairs={{0,32},{32,64},{64,96},{96,112},{112,80},{80,48},{48,16},{16,0},{1... | collective-permute-start | bytes 614408 | tf_op jit(solution)/shard_map/ppermute | solution.py:37
  49.0 5.2 %collective-permute-start.2 = (bf16[16,6400]{1,0:T(8,128)(2,1)}, bf16[16,6400]{1,0:T(8,128)(2,1)}, u32[]{:S(2)}, u32[]{:S(2)}) collective-permute-start(bf16[16,6400]{1,0:T(8,128)(2,1)} %pad_maximum_fusion.4.refs_0_), channel_id=1, source_target_pairs={{0,16},{32,0},{64,32},{96,64},{112,96},{80,112},{48,80},{16,48},{1... | collective-permute-start | bytes 614408 | tf_op jit(solution)/shard_map/ppermute | solution.py:38
  54.2 0.1 fusion
  54.3 0.0 collective-permute-done.15
  54.3 1.2 broadcast_in_dim.2
  55.6 4.5 %all-to-all-start.2 = ((bf16[4,2,640,128]{3,2,1,0:T(8,128)(2,1)}), bf16[4,2,640,128]{3,2,1,0:T(8,128)(2,1)S(1)}, u32[]{:S(2)}, u32[]{:S(2)}) async-start(bf16[4,2,640,128]{3,2,1,0:T(8,128)(2,1)} %broadcast_in_dim.2), calls=%async_computation.2 | async-start | bytes 2621440 | tf_op jit(solution)/shard_map/all_to_all | solution.py:30
  60.0 0.0 collective-permute-done.1.refs_1_
  60.1 2.0 %collective-permute-start.3 = (bf16[16,6400]{1,0:T(8,128)(2,1)S(1)}, bf16[16,6400]{1,0:T(8,128)(2,1)S(1)}, u32[]{:S(2)}, u32[]{:S(2)}) collective-permute-start(bf16[16,6400]{1,0:T(8,128)(2,1)S(1)} %collective-permute-done.1.refs_1_), channel_id=1, source_target_pairs={{0,32},{32,64},{64,96},{96,112},{112,80},{80,48},{48,16},{16,0},{1... | collective-permute-start | bytes 614408 | tf_op jit(solution)/shard_map/ppermute | solution.py:37
  62.1 0.0 collective-permute-done.2.refs_2_
  62.1 6.3 %collective-permute-start.4 = (bf16[16,6400]{1,0:T(8,128)(2,1)}, bf16[16,6400]{1,0:T(8,128)(2,1)S(1)}, u32[]{:S(2)}, u32[]{:S(2)}) collective-permute-start(bf16[16,6400]{1,0:T(8,128)(2,1)} %collective-permute-done.2.refs_2_), channel_id=1, source_target_pairs={{0,16},{32,0},{64,32},{96,64},{112,96},{80,112},{48,80},{16,48},{1... | collective-permute-start | bytes 614408 | tf_op jit(solution)/shard_map/ppermute | solution.py:38
  68.4 1.9 %pad_maximum_fusion = bf16[48,6400]{1,0:T(8,128)(2,1)} fusion(bf16[16,6400]{1,0:T(8,128)(2,1)} %collective-permute-done.2.refs_2_, bf16[16,6400]{1,0:T(8,128)(2,1)S(1)} %collective-permute-done.1.refs_1_, bf16[8,6400]{1,0:T(8,128)(2,1)S(1)} %get-tuple-element.8, bf16[8,6400]{1,0:T(8,128)(2,1)S(1)} %get-tuple-element.7), kind=kLoop, calls=%fused_computation.2 | loop fusion | flops 2457600 | bytes 1228800 | tf_op jit(solution)/shard_map/concatenate | solution.py:189
  70.3 4.7 %collective-permute-start.8 = (bf16[48,6400]{1,0:T(8,128)(2,1)}, bf16[48,6400]{1,0:T(8,128)(2,1)}, u32[]{:S(2)}, u32[]{:S(2)}) collective-permute-start(bf16[48,6400]{1,0:T(8,128)(2,1)} %pad_maximum_fusion), channel_id=1, source_target_pairs={{128,256},{256,128},{384,0},{0,384},{129,257},{257,129},{385,1},{1... | collective-permute-start | bytes 1843208 | tf_op jit(solution)/shard_map/ppermute | solution.py:189
  74.9 0.0 collective-permute-done.3.refs_3_
  74.9 0.0 copy-start.2
  74.9 2.5 %collective-permute-start.5 = (bf16[16,6400]{1,0:T(8,128)(2,1)S(1)}, bf16[16,6400]{1,0:T(8,128)(2,1)S(1)}, u32[]{:S(2)}, u32[]{:S(2)}) collective-permute-start(bf16[16,6400]{1,0:T(8,128)(2,1)S(1)} %collective-permute-done.3.refs_3_), channel_id=1, source_target_pairs={{0,32},{32,64},{64,96},{96,112},{112,80},{80,48},{48,16},{16,0},{1... | collective-permute-start | bytes 614408 | tf_op jit(solution)/shard_map/ppermute | solution.py:37
  77.4 0.0 collective-permute-done.4.refs_4_
  77.5 0.0 copy-start.3
  77.5 5.5 %collective-permute-start.6 = (bf16[16,6400]{1,0:T(8,128)(2,1)S(1)}, bf16[16,6400]{1,0:T(8,128)(2,1)}, u32[]{:S(2)}, u32[]{:S(2)}) collective-permute-start(bf16[16,6400]{1,0:T(8,128)(2,1)S(1)} %collective-permute-done.4.refs_4_), channel_id=1, source_target_pairs={{0,16},{32,0},{64,32},{96,64},{112,96},{80,112},{48,80},{16,48},{1... | collective-permute-start | bytes 614408 | tf_op jit(solution)/shard_map/ppermute | solution.py:38
  82.9 0.0 collective-permute-done.13.refs_14_
  82.9 1.9 %collective-permute-start.14 = (bf16[6400,128]{1,0:T(8,128)(2,1)}, bf16[6400,128]{1,0:T(8,128)(2,1)}, u32[]{:S(2)}, u32[]{:S(2)}) collective-permute-start(bf16[6400,128]{1,0:T(8,128)(2,1)} %collective-permute-done.13.refs_14_), channel_id=1, source_target_pairs={{0,8},{8,0},{1,9},{9,1},{2,10},{10,2},{3,11},{11,3},{4,12},{12,4},... | collective-permute-start | bytes 4915208 | tf_op jit(solution)/shard_map/ppermute | solution.py:26
  84.9 0.8 pad_maximum_fusion.1
  85.6 0.0 collective-permute-done.5.refs_5_
  85.7 2.9 %collective-permute-start.9 = (bf16[32,6400]{1,0:T(8,128)(2,1)}, bf16[32,6400]{1,0:T(8,128)(2,1)}, u32[]{:S(2)}, u32[]{:S(2)}) collective-permute-start(bf16[32,6400]{1,0:T(8,128)(2,1)} %pad_maximum_fusion.1), channel_id=1, source_target_pairs={{128,256},{256,128},{384,0},{0,384},{129,257},{257,129},{385,1},{1... | collective-permute-start | bytes 1228808 | tf_op jit(solution)/shard_map/ppermute | solution.py:189
  88.6 0.0 copy-done.2
  88.6 0.0 copy-done.3
  88.6 1.1 collective-permute-done.6.refs_6_
  89.7 0.0 all-to-all-done.2.near
  89.7 1.9 %collective-permute-start.16 = (bf16[4,2,640,128]{3,2,1,0:T(8,128)(2,1)S(1)}, bf16[4,2,640,128]{3,2,1,0:T(8,128)(2,1)S(1)}, u32[]{:S(2)}, u32[]{:S(2)}) collective-permute-start(bf16[4,2,640,128]{3,2,1,0:T(8,128)(2,1)S(1)} %all-to-all-done.2.near), channel_id=1, source_target_pairs={{0,8},{8,0},{1,9},{9,1},{2,10},{10,2},{3,11},{11,3},{4,12},{12,4},... | collective-permute-start | bytes 3932168 | tf_op jit(solution)/shard_map/ppermute | solution.py:26
  91.7 1.0 pad_maximum_fusion.2
  92.6 0.0 collective-permute-done.8.refs_8_
  92.6 4.4 %collective-permute-start.10 = (bf16[32,6400]{1,0:T(8,128)(2,1)S(1)}, bf16[32,6400]{1,0:T(8,128)(2,1)S(1)}, u32[]{:S(2)}, u32[]{:S(2)}) collective-permute-start(bf16[32,6400]{1,0:T(8,128)(2,1)S(1)} %pad_maximum_fusion.2), channel_id=1, source_target_pairs={{128,256},{256,128},{384,0},{0,384},{129,257},{257,129},{385,1},{1... | collective-permute-start | bytes 1228808 | tf_op jit(solution)/shard_map/ppermute | solution.py:189
  97.0 4.4 %collective-permute-done.9.refs_9_ = bf16[32,6400]{1,0:T(8,128)(2,1)} collective-permute-done((bf16[32,6400]{1,0:T(8,128)(2,1)}, bf16[32,6400]{1,0:T(8,128)(2,1)}, u32[]{:S(2)}, u32[]{:S(2)}) %collective-permute-start.9) | collective-permute-done | bytes 409632 | tf_op jit(solution)/shard_map/ppermute | solution.py:189
  101.4 3.2 %collective-permute-start.7 = (bf16[16,6400]{1,0:T(8,128)(2,1)S(1)}, bf16[16,6400]{1,0:T(8,128)(2,1)S(1)}, u32[]{:S(2)}, u32[]{:S(2)}) collective-permute-start(bf16[16,6400]{1,0:T(8,128)(2,1)S(1)} %collective-permute-done.5.refs_5_), channel_id=1, source_target_pairs={{0,32},{32,64},{64,96},{96,112},{112,80},{80,48},{48,16},{16,0},{1... | collective-permute-start | bytes 614408 | tf_op jit(solution)/shard_map/ppermute | solution.py:40
  104.6 7.2 %collective-permute-done.7.refs_7_ = bf16[16,6400]{1,0:T(8,128)(2,1)S(1)} collective-permute-done((bf16[16,6400]{1,0:T(8,128)(2,1)S(1)}, bf16[16,6400]{1,0:T(8,128)(2,1)S(1)}, u32[]{:S(2)}, u32[]{:S(2)}) %collective-permute-start.7) | collective-permute-done | bytes 204832 | tf_op jit(solution)/shard_map/ppermute | solution.py:40
  111.8 3.2 %collective-permute-start.11 = (bf16[16,6400]{1,0:T(8,128)(2,1)S(1)}, bf16[16,6400]{1,0:T(8,128)(2,1)S(1)}, u32[]{:S(2)}, u32[]{:S(2)}) collective-permute-start(bf16[16,6400]{1,0:T(8,128)(2,1)S(1)} %collective-permute-done.7.refs_7_), channel_id=1, source_target_pairs={{128,256},{256,128},{384,0},{0,384},{129,257},{257,129},{385,1},{1... | collective-permute-start | bytes 614408 | tf_op jit(solution)/shard_map/ppermute | solution.py:189
  115.1 0.0 collective-permute-done.10.refs_10_
  115.1 0.0 copy-start.6
  115.1 0.8 copy-done.6
  115.9 4.8 %collective-permute-done.11.refs_11_ = bf16[16,6400]{1,0:T(8,128)(2,1)S(1)} collective-permute-done((bf16[16,6400]{1,0:T(8,128)(2,1)S(1)}, bf16[16,6400]{1,0:T(8,128)(2,1)S(1)}, u32[]{:S(2)}, u32[]{:S(2)}) %collective-permute-start.11) | collective-permute-done | bytes 204832 | tf_op jit(solution)/shard_map/ppermute | solution.py:189
  120.7 0.7 copy-done.8
  121.4 0.0 collective-permute-done.12.refs_13_
  121.4 0.0 collective-permute-done.14.refs_15_
  121.4 0.0 copy-done.1
  121.4 0.0 copy-done.4
  121.4 0.0 copy-done.7
  121.4 6.1 %contract.1 = f32[1024,128]{1,0:T(8,128)} custom-call(bf16[16,6400]{1,0:T(8,128)(2,1)} %pad_maximum_fusion.4.refs_0_, bf16[16,6400]{1,0:T(8,128)(2,1)} %copy-done.1, bf16[16,6400]{1,0:T(8,128)(2,1)} %collective-permute-done.2.refs_2_, bf16[16,6400]{1,0:T(8,128)(2,1)} %copy-done.2, bf16[16,6400]{1,0:T(8,128)(2,1)} %copy-done.3, bf16[16,6400]{1,0:T(8,128)(2,1)} %copy-done.4, ...), custom_call_target="tpu_custom_call" | custom-call | flops 1677721600 | bytes 10485760 | tf_op jit(solution)/shard_map/contract/pallas_call | solution.py:87
  127.5 15.5 %all_to_all.15 = f32[16,64,128]{2,1,0:T(8,128)S(1)} all-to-all(f32[16,64,128]{2,1,0:T(8,128)} %bitcast.11), channel_id=1, replica_groups=mesh['x'=4,'zl'=8,'c'=2,'y'=4,'zh'=2] {'x','y'}, dimensions={0} | all-to-all | bytes 1048576 | tf_op jit(solution)/shard_map/all_to_all | solution.py:30
  143.0 0.7 regroup.1
  143.7 14.5 %all-to-all-start.1 = ((f32[16,8,128]{2,1,0:T(8,128)}), f32[16,8,128]{2,1,0:T(8,128)S(1)}, u32[]{:S(2)}, u32[]{:S(2)}) async-start(f32[16,8,128]{2,1,0:T(8,128)} %bitcast.4), calls=%async_computation.1 | async-start | bytes 131072 | tf_op jit(solution)/shard_map/all_to_all | solution.py:30
  158.2 0.0 collective-permute-done.16.other
  158.2 11.8 %all-to-all-done.1.got = f32[16,8,128]{2,1,0:T(8,128)S(1)} async-done(((f32[16,8,128]{2,1,0:T(8,128)}), f32[16,8,128]{2,1,0:T(8,128)S(1)}, u32[]{:S(2)}, u32[]{:S(2)}) %all-to-all-start.1) | async-done | bytes 65568 | tf_op jit(solution)/shard_map/all_to_all | solution.py:30
  170.0 1.7 transform.1
  (7 shorter events, 0.1 us)
Async XLA Ops:
  0.0 10.0 %copy-start.5 = (bf16[12500,8]{0,1:T(8,128)(2,1)S(1)}, bf16[12500,8]{0,1:T(8,128)(2,1)}, u32[]{:S(2)}) copy-start(bf16[12500,8]{0,1:T(8,128)(2,1)} %param.4) | copy-start | bytes 600004
  0.0 12.5 %copy-start = (bf16[125,1100]{0,1:T(8,128)(2,1)S(1)}, bf16[125,1100]{0,1:T(8,128)(2,1)}, u32[]{:S(2)}) copy-start(bf16[125,1100]{0,1:T(8,128)(2,1)} %param.5) | copy-start | bytes 825004
  4.7 78.3 %collective-permute-start.13 = (bf16[6400,128]{1,0:T(8,128)(2,1)S(1)}, bf16[6400,128]{1,0:T(8,128)(2,1)}, u32[]{:S(2)}, u32[]{:S(2)}) collective-permute-start(bf16[6400,128]{1,0:T(8,128)(2,1)S(1)} %get-tuple-element.5), channel_id=1, source_target_pairs={{0,128},{128,0},{256,384},{384,256},{1,129},{129,1},{257,385},{385... | collective-permute-start | bytes 4915208 | tf_op jit(solution)/shard_map/ppermute | solution.py:196
  8.1 113.3 %collective-permute-start.12 = (bf16[6400,128]{1,0:T(8,128)(2,1)}, bf16[6400,128]{1,0:T(8,128)(2,1)}, u32[]{:S(2)}, u32[]{:S(2)}) collective-permute-start(bf16[6400,128]{1,0:T(8,128)(2,1)} %get-tuple-element.6.refs_12_), channel_id=1, source_target_pairs={{0,8},{8,0},{1,9},{9,1},{2,10},{10,2},{3,11},{11,3},{4,12},{12,4},... | collective-permute-start | bytes 4915208 | tf_op jit(solution)/shard_map/ppermute | solution.py:26
  10.1 36.2 %collective-permute-start = (bf16[8,6400]{1,0:T(8,128)(2,1)S(1)}, bf16[8,6400]{1,0:T(8,128)(2,1)S(1)}, u32[]{:S(2)}, u32[]{:S(2)}) collective-permute-start(bf16[8,6400]{1,0:T(8,128)(2,1)S(1)} %pad_dynamic-slice_fusion.3), channel_id=1, source_target_pairs={{0,128},{128,0},{256,384},{384,256},{1,129},{129,1},{257,385},{385... | collective-permute-start | bytes 307208 | tf_op jit(solution)/shard_map/ppermute | solution.py:185
  12.7 41.6 %collective-permute-start.15 = (bf16[640,128]{1,0:T(8,128)(2,1)S(1)}, bf16[640,128]{1,0:T(8,128)(2,1)S(1)}, u32[]{:S(2)}, u32[]{:S(2)}) collective-permute-start(bf16[640,128]{1,0:T(8,128)(2,1)S(1)} %pad_dynamic-slice_fusion.2), channel_id=1, source_target_pairs={{0,113},{1,112},{16,97},{17,96},{32,81},{33,80},{48,65},{49,64},{6... | collective-permute-start | bytes 491528 | tf_op jit(solution)/shard_map/ppermute | solution.py:203
  47.1 13.0 %collective-permute-start.1 = (bf16[16,6400]{1,0:T(8,128)(2,1)}, bf16[16,6400]{1,0:T(8,128)(2,1)S(1)}, u32[]{:S(2)}, u32[]{:S(2)}) collective-permute-start(bf16[16,6400]{1,0:T(8,128)(2,1)} %pad_maximum_fusion.4.refs_0_), channel_id=1, source_target_pairs={{0,32},{32,64},{64,96},{96,112},{112,80},{80,48},{48,16},{16,0},{1... | collective-permute-start | bytes 614408 | tf_op jit(solution)/shard_map/ppermute | solution.py:37
  49.0 13.1 %collective-permute-start.2 = (bf16[16,6400]{1,0:T(8,128)(2,1)}, bf16[16,6400]{1,0:T(8,128)(2,1)}, u32[]{:S(2)}, u32[]{:S(2)}) collective-permute-start(bf16[16,6400]{1,0:T(8,128)(2,1)} %pad_maximum_fusion.4.refs_0_), channel_id=1, source_target_pairs={{0,16},{32,0},{64,32},{96,64},{112,96},{80,112},{48,80},{16,48},{1... | collective-permute-start | bytes 614408 | tf_op jit(solution)/shard_map/ppermute | solution.py:38
  55.6 34.2 %all-to-all-start.2 = ((bf16[4,2,640,128]{3,2,1,0:T(8,128)(2,1)}), bf16[4,2,640,128]{3,2,1,0:T(8,128)(2,1)S(1)}, u32[]{:S(2)}, u32[]{:S(2)}) async-start(bf16[4,2,640,128]{3,2,1,0:T(8,128)(2,1)} %broadcast_in_dim.2), calls=%async_computation.2 | async-start | bytes 2621440 | tf_op jit(solution)/shard_map/all_to_all | solution.py:30
  60.0 61.3 %copy-start.1 = (bf16[16,6400]{1,0:T(8,128)(2,1)}, bf16[16,6400]{1,0:T(8,128)(2,1)S(1)}, u32[]{:S(2)}) copy-start(bf16[16,6400]{1,0:T(8,128)(2,1)S(1)} %collective-permute-done.1.refs_1_) | copy-start | bytes 614404
  60.1 14.9 %collective-permute-start.3 = (bf16[16,6400]{1,0:T(8,128)(2,1)S(1)}, bf16[16,6400]{1,0:T(8,128)(2,1)S(1)}, u32[]{:S(2)}, u32[]{:S(2)}) collective-permute-start(bf16[16,6400]{1,0:T(8,128)(2,1)S(1)} %collective-permute-done.1.refs_1_), channel_id=1, source_target_pairs={{0,32},{32,64},{64,96},{96,112},{112,80},{80,48},{48,16},{16,0},{1... | collective-permute-start | bytes 614408 | tf_op jit(solution)/shard_map/ppermute | solution.py:37
  62.1 15.4 %collective-permute-start.4 = (bf16[16,6400]{1,0:T(8,128)(2,1)}, bf16[16,6400]{1,0:T(8,128)(2,1)S(1)}, u32[]{:S(2)}, u32[]{:S(2)}) collective-permute-start(bf16[16,6400]{1,0:T(8,128)(2,1)} %collective-permute-done.2.refs_2_), channel_id=1, source_target_pairs={{0,16},{32,0},{64,32},{96,64},{112,96},{80,112},{48,80},{16,48},{1... | collective-permute-start | bytes 614408 | tf_op jit(solution)/shard_map/ppermute | solution.py:38
  70.3 22.4 %collective-permute-start.8 = (bf16[48,6400]{1,0:T(8,128)(2,1)}, bf16[48,6400]{1,0:T(8,128)(2,1)}, u32[]{:S(2)}, u32[]{:S(2)}) collective-permute-start(bf16[48,6400]{1,0:T(8,128)(2,1)} %pad_maximum_fusion), channel_id=1, source_target_pairs={{128,256},{256,128},{384,0},{0,384},{129,257},{257,129},{385,1},{1... | collective-permute-start | bytes 1843208 | tf_op jit(solution)/shard_map/ppermute | solution.py:189
  74.9 13.6 %copy-start.2 = (bf16[16,6400]{1,0:T(8,128)(2,1)}, bf16[16,6400]{1,0:T(8,128)(2,1)S(1)}, u32[]{:S(2)}) copy-start(bf16[16,6400]{1,0:T(8,128)(2,1)S(1)} %collective-permute-done.3.refs_3_) | copy-start | bytes 614404
  74.9 10.7 %collective-permute-start.5 = (bf16[16,6400]{1,0:T(8,128)(2,1)S(1)}, bf16[16,6400]{1,0:T(8,128)(2,1)S(1)}, u32[]{:S(2)}, u32[]{:S(2)}) collective-permute-start(bf16[16,6400]{1,0:T(8,128)(2,1)S(1)} %collective-permute-done.3.refs_3_), channel_id=1, source_target_pairs={{0,32},{32,64},{64,96},{96,112},{112,80},{80,48},{48,16},{16,0},{1... | collective-permute-start | bytes 614408 | tf_op jit(solution)/shard_map/ppermute | solution.py:37
  77.5 11.1 %copy-start.3 = (bf16[16,6400]{1,0:T(8,128)(2,1)}, bf16[16,6400]{1,0:T(8,128)(2,1)S(1)}, u32[]{:S(2)}) copy-start(bf16[16,6400]{1,0:T(8,128)(2,1)S(1)} %collective-permute-done.4.refs_4_) | copy-start | bytes 614404
  77.5 12.3 %collective-permute-start.6 = (bf16[16,6400]{1,0:T(8,128)(2,1)S(1)}, bf16[16,6400]{1,0:T(8,128)(2,1)}, u32[]{:S(2)}, u32[]{:S(2)}) collective-permute-start(bf16[16,6400]{1,0:T(8,128)(2,1)S(1)} %collective-permute-done.4.refs_4_), channel_id=1, source_target_pairs={{0,16},{32,0},{64,32},{96,64},{112,96},{80,112},{48,80},{16,48},{1... | collective-permute-start | bytes 614408 | tf_op jit(solution)/shard_map/ppermute | solution.py:38
  82.9 38.4 %collective-permute-start.14 = (bf16[6400,128]{1,0:T(8,128)(2,1)}, bf16[6400,128]{1,0:T(8,128)(2,1)}, u32[]{:S(2)}, u32[]{:S(2)}) collective-permute-start(bf16[6400,128]{1,0:T(8,128)(2,1)} %collective-permute-done.13.refs_14_), channel_id=1, source_target_pairs={{0,8},{8,0},{1,9},{9,1},{2,10},{10,2},{3,11},{11,3},{4,12},{12,4},... | collective-permute-start | bytes 4915208 | tf_op jit(solution)/shard_map/ppermute | solution.py:26
  85.6 35.7 %copy-start.4 = (bf16[16,6400]{1,0:T(8,128)(2,1)}, bf16[16,6400]{1,0:T(8,128)(2,1)S(1)}, u32[]{:S(2)}) copy-start(bf16[16,6400]{1,0:T(8,128)(2,1)S(1)} %collective-permute-done.5.refs_5_) | copy-start | bytes 614404
  85.7 15.8 %collective-permute-start.9 = (bf16[32,6400]{1,0:T(8,128)(2,1)}, bf16[32,6400]{1,0:T(8,128)(2,1)}, u32[]{:S(2)}, u32[]{:S(2)}) collective-permute-start(bf16[32,6400]{1,0:T(8,128)(2,1)} %pad_maximum_fusion.1), channel_id=1, source_target_pairs={{128,256},{256,128},{384,0},{0,384},{129,257},{257,129},{385,1},{1... | collective-permute-start | bytes 1228808 | tf_op jit(solution)/shard_map/ppermute | solution.py:189
  89.7 68.4 %collective-permute-start.16 = (bf16[4,2,640,128]{3,2,1,0:T(8,128)(2,1)S(1)}, bf16[4,2,640,128]{3,2,1,0:T(8,128)(2,1)S(1)}, u32[]{:S(2)}, u32[]{:S(2)}) collective-permute-start(bf16[4,2,640,128]{3,2,1,0:T(8,128)(2,1)S(1)} %all-to-all-done.2.near), channel_id=1, source_target_pairs={{0,8},{8,0},{1,9},{9,1},{2,10},{10,2},{3,11},{11,3},{4,12},{12,4},... | collective-permute-start | bytes 3932168 | tf_op jit(solution)/shard_map/ppermute | solution.py:26
  92.6 22.4 %collective-permute-start.10 = (bf16[32,6400]{1,0:T(8,128)(2,1)S(1)}, bf16[32,6400]{1,0:T(8,128)(2,1)S(1)}, u32[]{:S(2)}, u32[]{:S(2)}) collective-permute-start(bf16[32,6400]{1,0:T(8,128)(2,1)S(1)} %pad_maximum_fusion.2), channel_id=1, source_target_pairs={{128,256},{256,128},{384,0},{0,384},{129,257},{257,129},{385,1},{1... | collective-permute-start | bytes 1228808 | tf_op jit(solution)/shard_map/ppermute | solution.py:189
  101.4 10.4 %collective-permute-start.7 = (bf16[16,6400]{1,0:T(8,128)(2,1)S(1)}, bf16[16,6400]{1,0:T(8,128)(2,1)S(1)}, u32[]{:S(2)}, u32[]{:S(2)}) collective-permute-start(bf16[16,6400]{1,0:T(8,128)(2,1)S(1)} %collective-permute-done.5.refs_5_), channel_id=1, source_target_pairs={{0,32},{32,64},{64,96},{96,112},{112,80},{80,48},{48,16},{16,0},{1... | collective-permute-start | bytes 614408 | tf_op jit(solution)/shard_map/ppermute | solution.py:40
  111.8 9.6 %copy-start.7 = (bf16[16,6400]{1,0:T(8,128)(2,1)}, bf16[16,6400]{1,0:T(8,128)(2,1)S(1)}, u32[]{:S(2)}) copy-start(bf16[16,6400]{1,0:T(8,128)(2,1)S(1)} %collective-permute-done.7.refs_7_) | copy-start | bytes 614404
  111.8 8.9 %collective-permute-start.11 = (bf16[16,6400]{1,0:T(8,128)(2,1)S(1)}, bf16[16,6400]{1,0:T(8,128)(2,1)S(1)}, u32[]{:S(2)}, u32[]{:S(2)}) collective-permute-start(bf16[16,6400]{1,0:T(8,128)(2,1)S(1)} %collective-permute-done.7.refs_7_), channel_id=1, source_target_pairs={{128,256},{256,128},{384,0},{0,384},{129,257},{257,129},{385,1},{1... | collective-permute-start | bytes 614408 | tf_op jit(solution)/shard_map/ppermute | solution.py:189
  115.1 0.8 copy-start.6
  120.7 0.7 copy-start.8
  143.7 26.3 %all-to-all-start.1 = ((f32[16,8,128]{2,1,0:T(8,128)}), f32[16,8,128]{2,1,0:T(8,128)S(1)}, u32[]{:S(2)}, u32[]{:S(2)}) async-start(f32[16,8,128]{2,1,0:T(8,128)} %bitcast.4), calls=%async_computation.1 | async-start | bytes 131072 | tf_op jit(solution)/shard_map/all_to_all | solution.py:30

commit v7 on v6

--- a/solution.py
+++ b/solution.py
@@ -126,9 +126,9 @@
 
 def transform_kernel(got, near, other, out):
     nao = out.shape[2]
-    core = lax.axis_index("c")
-    source = jnp.where(core == lax.axis_index("zh"), 0, 1)
-    totals = [[0.0, 0.0], [0.0, 0.0]]
+    part = near.shape[1] // 4
+    core, odd = lax.axis_index("c"), lax.rem(lax.axis_index("x"), 2)
+    totals = [[[0.0, 0.0] for _ in range(2)] for _ in range(C)]
     for block in range(Y):
         tiles = [got[Y * h + block] + got[ZL + Y * h + block] for h in range(2)]
         rest = jnp.concatenate(tiles, axis=0)
@@ -138,16 +138,23 @@
             rest = rest - terms[-1].astype(jnp.float32)
         terms = jnp.concatenate(terms, axis=0)
         for side in range(2):
+            local = (core == lax.axis_index("zh")) == (side == 0)
             for index, coef in enumerate((near, other)):
-                got_part = lax.dot_general(
-                    terms, coef[block, source if side == 0 else 1 - source], (((1,), (1,)), ((), ())), preferred_element_type=jnp.float32
-                )
-                totals[index][side] += (got_part[:16] + got_part[16:32]) + got_part[32:]
-    first = core == 0
+                for quarter in range(2):
+                    away = 2 + (odd if quarter == 0 else 1 - odd)
+                    start = pl.multiple_of(jnp.where(local, quarter, away) * part, 16)
+                    product = lax.dot_general(
+                        terms,
+                        coef[block, pl.ds(start, part), :],
+                        (((1,), (1,)), ((), ())),
+                        preferred_element_type=jnp.float32,
+                    )
+                    totals[index][side][quarter] += (product[:16] + product[16:32]) + product[32:]
     both = []
     for side in range(2):
-        low = jnp.where(first, totals[0][side], totals[1][side])
-        high = jnp.where(first, totals[1][side], totals[0][side])
+        halves = [jnp.concatenate(totals[index][side], axis=1) for index in range(C)]
+        low = jnp.where(core == 0, halves[0], halves[1])
+        high = jnp.where(core == 0, halves[1], halves[0])
         both.append(jnp.concatenate([low, high], axis=1))
     for source in range(X):
         for h in range(2):
@@ -185,10 +192,10 @@
     got = lax.ppermute(sent, "x", PAIR)
     chunk = jnp.concatenate([jnp.where(even, mine, got), jnp.where(even, got, mine)], axis=0)
     own = ring_gather(chunk)
-    cross = [
-        lax.ppermute(jnp.concatenate(own[first:last], axis=0), "x", CROSS)
-        for first, last in ((0, 3), (3, 5), (5, 7), (7, 8))
-    ]
+    cross = []
+    for first, last in ((0, 3), (3, 5), (5, 7), (7, 8)):
+        joined = jnp.concatenate(own[first:last], axis=0)
+        cross.append(lax.ppermute(joined, "x", CROSS))
 
     dens = jnp.pad(density.T, ((0, pad), (0, LANES - rows)))
     kept = lax.dynamic_slice(dens, (keep, 0), (depth, LANES))
@@ -196,14 +203,17 @@
     other = lax.ppermute(given, "x", PAIR)
     pieces = [kept, swap(kept, "c"), other, swap(other, "c")]
 
-    part = -(-nao // (C * LANES)) * LANES
-    coef = jnp.pad(virt_coef.T, ((0, C * part - nao), (0, LANES - virt_rows)))
-    mine = lax.dynamic_slice(coef, (core * part, 0), (part, LANES))
+    part = -(-nao // (2 * C * 16)) * 16
+    coef = jnp.pad(virt_coef.T, ((0, 2 * C * part - nao), (0, LANES - virt_rows)))
+    mine = lax.dynamic_slice(coef, (2 * core * part, 0), (2 * part, LANES))
+    quarter = lax.dynamic_slice(coef, ((2 * core + lax.rem(here, 2)) * part, 0), (part, LANES))
     mirror = [(z * ZH + h, (ZL - 1 - z) * ZH + 1 - h) for z in range(ZL) for h in range(ZH)]
-    far = lax.ppermute(mine, ("zl", "zh"), mirror)
-    pair = jnp.broadcast_to(jnp.stack([mine, far])[None], (Y, ZH, part, LANES))
+    far = lax.ppermute(quarter, ("zl", "zh"), mirror)
+    rest = lax.ppermute(far, "x", PAIR)
+    pair = jnp.concatenate([mine, far, rest], axis=0)
+    pair = jnp.broadcast_to(pair[None], (Y,) + pair.shape)
     coefs = exchange(pair, "y")
-    coefs = [coefs.reshape(Y, ZH, part, LANES), swap(coefs, "c").reshape(Y, ZH, part, LANES)]
+    coefs = [coefs, swap(coefs, "c")]
 
     gamma = contract(own, cross, pieces)
     gamma = exchange(gamma.reshape(X * Y, ZL * ZH * PIECES, LANES), ("x", "y"))

time: 173 us -> 169 us (0.977)
  the two profiles are of different devices: /device:TPU:32 before, /device:TPU:1 now
where the time goes in v7:
time: 169 us; the launch traced here: 167 us
  starting transfers between devices  103 us (61%)
  waiting for transfers between devices  30.4 us (18%)
  blocking collectives  17 us (10%)
  Pallas kernels  8.53 us (5%)
  local copies, waits for them, and re-layouts  6.86 us (4%)
    ppermute x3, starting transfers between devices, ring_gather(): up = lax.ppermute(up, 'zl', fold_ring(1))  24.7 us
    all_to_all x2, starting transfers between devices, exchange(): return lax.all_to_all(shard, axes, split_axis=0, concat_axis=0, tiled=True)  18.1 us
    ppermute x4, starting transfers between devices, on_device(): cross.append(lax.ppermute(joined, 'x', CROSS))  17.1 us
    all_to_all x1, blocking collectives, exchange(): return lax.all_to_all(shard, axes, split_axis=0, concat_axis=0, tiled=True)  17 us
    ppermute x3, starting transfers between devices, swap(): return lax.ppermute(shard, axis, [(0, 1), (1, 0)])  15.2 us
    all_to_all x2, waiting for transfers between devices, exchange(): return lax.all_to_all(shard, axes, split_axis=0, concat_axis=0, tiled=True)  11.7 us
    ppermute x1, waiting for transfers between devices, on_device(): far = lax.ppermute(quarter, ('zl', 'zh'), mirror)  6.99 us
    ppermute x1, waiting for transfers between devices, on_device(): got = lax.ppermute(sent, 'x', PAIR)  6.26 us
  transfers between devices with their start and end apart: 20, of which 4 were waited for; matrix products, arithmetic and copies ran while one was open for 1% of the time, Pallas kernels for 4%

profile of v7, /device:TPU:1, one launch (start us, length us, event | category | flops | bytes accessed | tf_op | source)
XLA Modules:
  0.0 167.0 jit_solution(9871391861540506713)
XLA Ops:
  0.0 4.7 %pad_dynamic-slice_fusion = (bf16[6400,128]{1,0:T(8,128)(2,1)S(1)}, bf16[6400,128]{1,0:T(8,128)(2,1)}) fusion(s32[]{:T(128)S(6)} %select_n.34, bf16[12500,125]{1,0:T(8,128)(2,1)} %bitcast.7, s32[]{:T(128)S(6)} %select_n.33), kind=kLoop, calls=%fused_computation | loop fusion | bytes 6401808 | tf_op jit(solution)/shard_map/dynamic_slice | solution.py:202
  4.7 3.9 %collective-permute-start.13 = (bf16[6400,128]{1,0:T(8,128)(2,1)S(1)}, bf16[6400,128]{1,0:T(8,128)(2,1)}, u32[]{:S(2)}, u32[]{:S(2)}) collective-permute-start(bf16[6400,128]{1,0:T(8,128)(2,1)S(1)} %get-tuple-element.5), channel_id=1, source_target_pairs={{0,128},{128,0},{256,384},{384,256},{1,129},{129,1},{257,385},{385... | collective-permute-start | bytes 4915208 | tf_op jit(solution)/shard_map/ppermute | solution.py:203
  8.6 6.7 %collective-permute-start.12 = (bf16[6400,128]{1,0:T(8,128)(2,1)}, bf16[6400,128]{1,0:T(8,128)(2,1)}, u32[]{:S(2)}, u32[]{:S(2)}) collective-permute-start(bf16[6400,128]{1,0:T(8,128)(2,1)} %get-tuple-element.6.refs_12_), channel_id=1, source_target_pairs={{0,8},{8,0},{1,9},{9,1},{2,10},{10,2},{3,11},{11,3},{4,12},{12,4},... | collective-permute-start | bytes 4915208 | tf_op jit(solution)/shard_map/ppermute | solution.py:26
  15.3 0.0 copy-done.7
  15.4 3.6 %collective-permute-start = (bf16[8,6400]{1,0:T(8,128)(2,1)S(1)}, bf16[8,6400]{1,0:T(8,128)(2,1)S(1)}, u32[]{:S(2)}, u32[]{:S(2)}) collective-permute-start(bf16[8,6400]{1,0:T(8,128)(2,1)S(1)} %pad_dynamic-slice_fusion.4), channel_id=1, source_target_pairs={{0,128},{128,0},{256,384},{384,256},{1,129},{129,1},{257,385},{385... | collective-permute-start | bytes 307208 | tf_op jit(solution)/shard_map/ppermute | solution.py:192
  19.1 0.0 copy-done
  19.1 0.1 pad_dynamic-slice_fusion.2
  19.1 5.8 %collective-permute-start.15 = (bf16[288,128]{1,0:T(8,128)(2,1)S(1)}, bf16[288,128]{1,0:T(8,128)(2,1)S(1)}, u32[]{:S(2)}, u32[]{:S(2)}) collective-permute-start(bf16[288,128]{1,0:T(8,128)(2,1)S(1)} %pad_dynamic-slice_fusion.2), channel_id=1, source_target_pairs={{0,113},{1,112},{16,97},{17,96},{32,81},{33,80},{48,65},{49,64},{6... | collective-permute-start | bytes 221192 | tf_op jit(solution)/shard_map/ppermute | solution.py:211
  24.9 0.1 pad_dynamic-slice_fusion.3
  25.0 7.0 %collective-permute-done.15 = bf16[288,128]{1,0:T(8,128)(2,1)S(1)} collective-permute-done((bf16[288,128]{1,0:T(8,128)(2,1)S(1)}, bf16[288,128]{1,0:T(8,128)(2,1)S(1)}, u32[]{:S(2)}, u32[]{:S(2)}) %collective-permute-start.15) | collective-permute-done | bytes 73760 | tf_op jit(solution)/shard_map/ppermute | solution.py:211
  32.0 3.1 %collective-permute-start.16 = (bf16[288,128]{1,0:T(8,128)(2,1)S(1)}, bf16[288,128]{1,0:T(8,128)(2,1)S(1)}, u32[]{:S(2)}, u32[]{:S(2)}) collective-permute-start(bf16[288,128]{1,0:T(8,128)(2,1)S(1)} %collective-permute-done.15), channel_id=1, source_target_pairs={{0,128},{128,0},{256,384},{384,256},{1,129},{129,1},{257,385},{385... | collective-permute-start | bytes 221192 | tf_op jit(solution)/shard_map/ppermute | solution.py:212
  35.1 6.3 %collective-permute-done = bf16[8,6400]{1,0:T(8,128)(2,1)S(1)} collective-permute-done((bf16[8,6400]{1,0:T(8,128)(2,1)S(1)}, bf16[8,6400]{1,0:T(8,128)(2,1)S(1)}, u32[]{:S(2)}, u32[]{:S(2)}) %collective-permute-start) | collective-permute-done | bytes 102432 | tf_op jit(solution)/shard_map/ppermute | solution.py:192
  41.4 0.1 broadcast_select_fusion.1
  41.5 0.7 pad_maximum_fusion.4.refs_0_
  42.2 9.9 %collective-permute-start.1 = (bf16[16,6400]{1,0:T(8,128)(2,1)}, bf16[16,6400]{1,0:T(8,128)(2,1)S(1)}, u32[]{:S(2)}, u32[]{:S(2)}) collective-permute-start(bf16[16,6400]{1,0:T(8,128)(2,1)} %pad_maximum_fusion.4.refs_0_), channel_id=1, source_target_pairs={{0,32},{32,64},{64,96},{96,112},{112,80},{80,48},{48,16},{16,0},{1... | collective-permute-start | bytes 614408 | tf_op jit(solution)/shard_map/ppermute | solution.py:37
  52.0 1.9 %collective-permute-start.2 = (bf16[16,6400]{1,0:T(8,128)(2,1)}, bf16[16,6400]{1,0:T(8,128)(2,1)S(1)}, u32[]{:S(2)}, u32[]{:S(2)}) collective-permute-start(bf16[16,6400]{1,0:T(8,128)(2,1)} %pad_maximum_fusion.4.refs_0_), channel_id=1, source_target_pairs={{0,16},{32,0},{64,32},{96,64},{112,96},{80,112},{48,80},{16,48},{1... | collective-permute-start | bytes 614408 | tf_op jit(solution)/shard_map/ppermute | solution.py:38
  54.0 0.0 collective-permute-done.16
  54.0 1.2 broadcast_in_dim.2
  55.2 4.2 %all-to-all-start.2 = ((bf16[4,1152,128]{2,1,0:T(8,128)(2,1)}), bf16[4,1152,128]{2,1,0:T(8,128)(2,1)S(1)}, u32[]{:S(2)}, u32[]{:S(2)}) async-start(bf16[4,1152,128]{2,1,0:T(8,128)(2,1)} %broadcast_in_dim.2), calls=%async_computation.2 | async-start | bytes 2359296 | tf_op jit(solution)/shard_map/all_to_all | solution.py:30
  59.4 0.0 collective-permute-done.1.refs_1_
  59.4 6.9 %collective-permute-start.3 = (bf16[16,6400]{1,0:T(8,128)(2,1)S(1)}, bf16[16,6400]{1,0:T(8,128)(2,1)S(1)}, u32[]{:S(2)}, u32[]{:S(2)}) collective-permute-start(bf16[16,6400]{1,0:T(8,128)(2,1)S(1)} %collective-permute-done.1.refs_1_), channel_id=1, source_target_pairs={{0,32},{32,64},{64,96},{96,112},{112,80},{80,48},{48,16},{16,0},{1... | collective-permute-start | bytes 614408 | tf_op jit(solution)/shard_map/ppermute | solution.py:37
  66.3 0.0 collective-permute-done.2.refs_2_
  66.3 0.0 copy-start.2
  66.3 1.9 %collective-permute-start.4 = (bf16[16,6400]{1,0:T(8,128)(2,1)S(1)}, bf16[16,6400]{1,0:T(8,128)(2,1)S(1)}, u32[]{:S(2)}, u32[]{:S(2)}) collective-permute-start(bf16[16,6400]{1,0:T(8,128)(2,1)S(1)} %collective-permute-done.2.refs_2_), channel_id=1, source_target_pairs={{0,16},{32,0},{64,32},{96,64},{112,96},{80,112},{48,80},{16,48},{1... | collective-permute-start | bytes 614408 | tf_op jit(solution)/shard_map/ppermute | solution.py:38
  68.3 4.4 %collective-permute-start.8 = (bf16[48,6400]{1,0:T(8,128)(2,1)S(1)}, bf16[48,6400]{1,0:T(8,128)(2,1)S(1)}, u32[]{:S(2)}, u32[]{:S(2)}) collective-permute-start(bf16[48,6400]{1,0:T(8,128)(2,1)S(1)} %pad_maximum_fusion), channel_id=1, source_target_pairs={{128,256},{256,128},{384,0},{0,384},{129,257},{257,129},{385,1},{1... | collective-permute-start | bytes 1843208 | tf_op jit(solution)/shard_map/ppermute | solution.py:198
  72.7 0.0 collective-permute-done.3.refs_3_
  72.7 0.0 copy-start.3
  72.7 8.0 %collective-permute-start.5 = (bf16[16,6400]{1,0:T(8,128)(2,1)S(1)}, bf16[16,6400]{1,0:T(8,128)(2,1)S(1)}, u32[]{:S(2)}, u32[]{:S(2)}) collective-permute-start(bf16[16,6400]{1,0:T(8,128)(2,1)S(1)} %collective-permute-done.3.refs_3_), channel_id=1, source_target_pairs={{0,32},{32,64},{64,96},{96,112},{112,80},{80,48},{48,16},{16,0},{1... | collective-permute-start | bytes 614408 | tf_op jit(solution)/shard_map/ppermute | solution.py:37
  80.7 0.0 collective-permute-done.4.refs_4_
  80.7 0.0 copy-start.4
  80.7 1.9 %collective-permute-start.6 = (bf16[16,6400]{1,0:T(8,128)(2,1)S(1)}, bf16[16,6400]{1,0:T(8,128)(2,1)S(1)}, u32[]{:S(2)}, u32[]{:S(2)}) collective-permute-start(bf16[16,6400]{1,0:T(8,128)(2,1)S(1)} %collective-permute-done.4.refs_4_), channel_id=1, source_target_pairs={{0,16},{32,0},{64,32},{96,64},{112,96},{80,112},{48,80},{16,48},{1... | collective-permute-start | bytes 614408 | tf_op jit(solution)/shard_map/ppermute | solution.py:38
  82.6 0.0 collective-permute-done.13.refs_14_
  82.6 3.7 %collective-permute-start.14 = (bf16[6400,128]{1,0:T(8,128)(2,1)}, bf16[6400,128]{1,0:T(8,128)(2,1)}, u32[]{:S(2)}, u32[]{:S(2)}) collective-permute-start(bf16[6400,128]{1,0:T(8,128)(2,1)} %collective-permute-done.13.refs_14_), channel_id=1, source_target_pairs={{0,8},{8,0},{1,9},{9,1},{2,10},{10,2},{3,11},{11,3},{4,12},{12,4},... | collective-permute-start | bytes 4915208 | tf_op jit(solution)/shard_map/ppermute | solution.py:26
  86.3 0.0 collective-permute-done.5.refs_5_
  86.3 0.0 copy-start.5
  86.4 4.4 %collective-permute-start.9 = (bf16[32,6400]{1,0:T(8,128)(2,1)S(1)}, bf16[32,6400]{1,0:T(8,128)(2,1)S(1)}, u32[]{:S(2)}, u32[]{:S(2)}) collective-permute-start(bf16[32,6400]{1,0:T(8,128)(2,1)S(1)} %pad_maximum_fusion.1), channel_id=1, source_target_pairs={{128,256},{256,128},{384,0},{0,384},{129,257},{257,129},{385,1},{1... | collective-permute-start | bytes 1228808 | tf_op jit(solution)/shard_map/ppermute | solution.py:198
  90.8 0.0 collective-permute-done.6.refs_6_
  90.8 0.0 copy-start.6
  90.8 4.2 %collective-permute-start.10 = (bf16[32,6400]{1,0:T(8,128)(2,1)S(1)}, bf16[32,6400]{1,0:T(8,128)(2,1)}, u32[]{:S(2)}, u32[]{:S(2)}) collective-permute-start(bf16[32,6400]{1,0:T(8,128)(2,1)S(1)} %pad_maximum_fusion.2), channel_id=1, source_target_pairs={{128,256},{256,128},{384,0},{0,384},{129,257},{257,129},{385,1},{1... | collective-permute-start | bytes 1228808 | tf_op jit(solution)/shard_map/ppermute | solution.py:198
  95.1 0.0 collective-permute-done.8.refs_8_
  95.1 0.0 copy-start.8
  95.1 5.5 %collective-permute-start.7 = (bf16[16,6400]{1,0:T(8,128)(2,1)S(1)}, bf16[16,6400]{1,0:T(8,128)(2,1)}, u32[]{:S(2)}, u32[]{:S(2)}) collective-permute-start(bf16[16,6400]{1,0:T(8,128)(2,1)S(1)} %collective-permute-done.5.refs_5_), channel_id=1, source_target_pairs={{0,32},{32,64},{64,96},{96,112},{112,80},{80,48},{48,16},{16,0},{1... | collective-permute-start | bytes 614408 | tf_op jit(solution)/shard_map/ppermute | solution.py:40
  100.6 0.0 copy-done.3
  100.6 0.0 copy-done.4
  100.6 0.0 copy-done.6
  100.7 0.0 collective-permute-done.9.refs_9_
  100.7 0.8 copy-done.9
  101.5 0.0 all-to-all-done.2.near
  101.5 4.8 %collective-permute-start.17 = (bf16[4,1152,128]{2,1,0:T(8,128)(2,1)S(1)}, bf16[4,1152,128]{2,1,0:T(8,128)(2,1)S(1)}, u32[]{:S(2)}, u32[]{:S(2)}) collective-permute-start(bf16[4,1152,128]{2,1,0:T(8,128)(2,1)S(1)} %all-to-all-done.2.near), channel_id=1, source_target_pairs={{0,8},{8,0},{1,9},{9,1},{2,10},{10,2},{3,11},{11,3},{4,12},{12,4},... | collective-permute-start | bytes 3538952 | tf_op jit(solution)/shard_map/ppermute | solution.py:26
  106.3 0.0 collective-permute-done.7.refs_7_
  106.3 4.1 %collective-permute-start.11 = (bf16[16,6400]{1,0:T(8,128)(2,1)}, bf16[16,6400]{1,0:T(8,128)(2,1)}, u32[]{:S(2)}, u32[]{:S(2)}) collective-permute-start(bf16[16,6400]{1,0:T(8,128)(2,1)} %collective-permute-done.7.refs_7_), channel_id=1, source_target_pairs={{128,256},{256,128},{384,0},{0,384},{129,257},{257,129},{385,1},{1... | collective-permute-start | bytes 614408 | tf_op jit(solution)/shard_map/ppermute | solution.py:198
  110.4 0.0 collective-permute-done.10.refs_10_
  110.4 5.4 %collective-permute-done.11.refs_11_ = bf16[16,6400]{1,0:T(8,128)(2,1)} collective-permute-done((bf16[16,6400]{1,0:T(8,128)(2,1)}, bf16[16,6400]{1,0:T(8,128)(2,1)}, u32[]{:S(2)}, u32[]{:S(2)}) %collective-permute-start.11) | collective-permute-done | bytes 204832 | tf_op jit(solution)/shard_map/ppermute | solution.py:198
  115.9 0.0 collective-permute-done.12.refs_13_
  115.9 0.0 collective-permute-done.14.refs_15_
  115.9 0.0 copy-done.2
  115.9 0.0 copy-done.5
  115.9 6.1 %contract.1 = f32[1024,128]{1,0:T(8,128)} custom-call(bf16[16,6400]{1,0:T(8,128)(2,1)} %pad_maximum_fusion.4.refs_0_, bf16[16,6400]{1,0:T(8,128)(2,1)} %copy-done.1, bf16[16,6400]{1,0:T(8,128)(2,1)} %copy-done.2, bf16[16,6400]{1,0:T(8,128)(2,1)} %copy-done.3, bf16[16,6400]{1,0:T(8,128)(2,1)} %copy-done.4, bf16[16,6400]{1,0:T(8,128)(2,1)} %copy-done.5, ...), custom_call_target="tpu_custom_call" | custom-call | flops 1677721600 | bytes 10485760 | tf_op jit(solution)/shard_map/contract/pallas_call | solution.py:87
  122.0 17.0 %all_to_all.15 = f32[16,64,128]{2,1,0:T(8,128)S(1)} all-to-all(f32[16,64,128]{2,1,0:T(8,128)} %bitcast.8), channel_id=1, replica_groups=mesh['x'=4,'zl'=8,'c'=2,'y'=4,'zh'=2] {'x','y'}, dimensions={0} | all-to-all | bytes 1048576 | tf_op jit(solution)/shard_map/all_to_all | solution.py:30
  139.0 0.7 regroup.1
  139.6 13.9 %all-to-all-start.1 = ((f32[16,8,128]{2,1,0:T(8,128)}), f32[16,8,128]{2,1,0:T(8,128)S(1)}, u32[]{:S(2)}, u32[]{:S(2)}) async-start(f32[16,8,128]{2,1,0:T(8,128)} %bitcast.4), calls=%async_computation.1 | async-start | bytes 131072 | tf_op jit(solution)/shard_map/all_to_all | solution.py:30
  153.5 0.0 collective-permute-done.17.other
  153.5 11.7 %all-to-all-done.1.got = f32[16,8,128]{2,1,0:T(8,128)S(1)} async-done(((f32[16,8,128]{2,1,0:T(8,128)}), f32[16,8,128]{2,1,0:T(8,128)S(1)}, u32[]{:S(2)}, u32[]{:S(2)}) %all-to-all-start.1) | async-done | bytes 65568 | tf_op jit(solution)/shard_map/all_to_all | solution.py:30
  165.2 1.8 %transform.1 = f32[8,1,1100]{2,1,0:T(1,128)} custom-call(f32[16,8,128]{2,1,0:T(8,128)S(1)} %all-to-all-done.1.got, bf16[4,1152,128]{2,1,0:T(8,128)(2,1)S(1)} %all-to-all-done.2.near, bf16[4,1152,128]{2,1,0:T(8,128)(2,1)S(1)} %collective-permute-done.17.other), custom_call_target="tpu_custom_call" | custom-call | flops 16777216 | bytes 3145728 | tf_op jit(solution)/shard_map/transform/pallas_call | solution.py:167
  (11 shorter events, 0.2 us)
Async XLA Ops:
  0.0 15.3 %copy-start.7 = (bf16[12500,8]{0,1:T(8,128)(2,1)S(1)}, bf16[12500,8]{0,1:T(8,128)(2,1)}, u32[]{:S(2)}) copy-start(bf16[12500,8]{0,1:T(8,128)(2,1)} %param.4) | copy-start | bytes 600004
  0.0 19.1 %copy-start = (bf16[125,1100]{0,1:T(8,128)(2,1)S(1)}, bf16[125,1100]{0,1:T(8,128)(2,1)}, u32[]{:S(2)}) copy-start(bf16[125,1100]{0,1:T(8,128)(2,1)} %param.5) | copy-start | bytes 825004
  4.7 77.9 %collective-permute-start.13 = (bf16[6400,128]{1,0:T(8,128)(2,1)S(1)}, bf16[6400,128]{1,0:T(8,128)(2,1)}, u32[]{:S(2)}, u32[]{:S(2)}) collective-permute-start(bf16[6400,128]{1,0:T(8,128)(2,1)S(1)} %get-tuple-element.5), channel_id=1, source_target_pairs={{0,128},{128,0},{256,384},{384,256},{1,129},{129,1},{257,385},{385... | collective-permute-start | bytes 4915208 | tf_op jit(solution)/shard_map/ppermute | solution.py:203
  8.6 107.3 %collective-permute-start.12 = (bf16[6400,128]{1,0:T(8,128)(2,1)}, bf16[6400,128]{1,0:T(8,128)(2,1)}, u32[]{:S(2)}, u32[]{:S(2)}) collective-permute-start(bf16[6400,128]{1,0:T(8,128)(2,1)} %get-tuple-element.6.refs_12_), channel_id=1, source_target_pairs={{0,8},{8,0},{1,9},{9,1},{2,10},{10,2},{3,11},{11,3},{4,12},{12,4},... | collective-permute-start | bytes 4915208 | tf_op jit(solution)/shard_map/ppermute | solution.py:26
  15.4 26.0 %collective-permute-start = (bf16[8,6400]{1,0:T(8,128)(2,1)S(1)}, bf16[8,6400]{1,0:T(8,128)(2,1)S(1)}, u32[]{:S(2)}, u32[]{:S(2)}) collective-permute-start(bf16[8,6400]{1,0:T(8,128)(2,1)S(1)} %pad_dynamic-slice_fusion.4), channel_id=1, source_target_pairs={{0,128},{128,0},{256,384},{384,256},{1,129},{129,1},{257,385},{385... | collective-permute-start | bytes 307208 | tf_op jit(solution)/shard_map/ppermute | solution.py:192
  19.1 12.9 %collective-permute-start.15 = (bf16[288,128]{1,0:T(8,128)(2,1)S(1)}, bf16[288,128]{1,0:T(8,128)(2,1)S(1)}, u32[]{:S(2)}, u32[]{:S(2)}) collective-permute-start(bf16[288,128]{1,0:T(8,128)(2,1)S(1)} %pad_dynamic-slice_fusion.2), channel_id=1, source_target_pairs={{0,113},{1,112},{16,97},{17,96},{32,81},{33,80},{48,65},{49,64},{6... | collective-permute-start | bytes 221192 | tf_op jit(solution)/shard_map/ppermute | solution.py:211
  32.0 22.0 %collective-permute-start.16 = (bf16[288,128]{1,0:T(8,128)(2,1)S(1)}, bf16[288,128]{1,0:T(8,128)(2,1)S(1)}, u32[]{:S(2)}, u32[]{:S(2)}) collective-permute-start(bf16[288,128]{1,0:T(8,128)(2,1)S(1)} %collective-permute-done.15), channel_id=1, source_target_pairs={{0,128},{128,0},{256,384},{384,256},{1,129},{129,1},{257,385},{385... | collective-permute-start | bytes 221192 | tf_op jit(solution)/shard_map/ppermute | solution.py:212
  42.2 17.2 %collective-permute-start.1 = (bf16[16,6400]{1,0:T(8,128)(2,1)}, bf16[16,6400]{1,0:T(8,128)(2,1)S(1)}, u32[]{:S(2)}, u32[]{:S(2)}) collective-permute-start(bf16[16,6400]{1,0:T(8,128)(2,1)} %pad_maximum_fusion.4.refs_0_), channel_id=1, source_target_pairs={{0,32},{32,64},{64,96},{96,112},{112,80},{80,48},{48,16},{16,0},{1... | collective-permute-start | bytes 614408 | tf_op jit(solution)/shard_map/ppermute | solution.py:37
  52.0 14.2 %collective-permute-start.2 = (bf16[16,6400]{1,0:T(8,128)(2,1)}, bf16[16,6400]{1,0:T(8,128)(2,1)S(1)}, u32[]{:S(2)}, u32[]{:S(2)}) collective-permute-start(bf16[16,6400]{1,0:T(8,128)(2,1)} %pad_maximum_fusion.4.refs_0_), channel_id=1, source_target_pairs={{0,16},{32,0},{64,32},{96,64},{112,96},{80,112},{48,80},{16,48},{1... | collective-permute-start | bytes 614408 | tf_op jit(solution)/shard_map/ppermute | solution.py:38
  55.2 46.3 %all-to-all-start.2 = ((bf16[4,1152,128]{2,1,0:T(8,128)(2,1)}), bf16[4,1152,128]{2,1,0:T(8,128)(2,1)S(1)}, u32[]{:S(2)}, u32[]{:S(2)}) async-start(bf16[4,1152,128]{2,1,0:T(8,128)(2,1)} %broadcast_in_dim.2), calls=%async_computation.2 | async-start | bytes 2359296 | tf_op jit(solution)/shard_map/all_to_all | solution.py:30
  59.4 56.5 %copy-start.1 = (bf16[16,6400]{1,0:T(8,128)(2,1)}, bf16[16,6400]{1,0:T(8,128)(2,1)S(1)}, u32[]{:S(2)}) copy-start(bf16[16,6400]{1,0:T(8,128)(2,1)S(1)} %collective-permute-done.1.refs_1_) | copy-start | bytes 614404
  59.4 13.3 %collective-permute-start.3 = (bf16[16,6400]{1,0:T(8,128)(2,1)S(1)}, bf16[16,6400]{1,0:T(8,128)(2,1)S(1)}, u32[]{:S(2)}, u32[]{:S(2)}) collective-permute-start(bf16[16,6400]{1,0:T(8,128)(2,1)S(1)} %collective-permute-done.1.refs_1_), channel_id=1, source_target_pairs={{0,32},{32,64},{64,96},{96,112},{112,80},{80,48},{48,16},{16,0},{1... | collective-permute-start | bytes 614408 | tf_op jit(solution)/shard_map/ppermute | solution.py:37
  66.3 49.6 %copy-start.2 = (bf16[16,6400]{1,0:T(8,128)(2,1)}, bf16[16,6400]{1,0:T(8,128)(2,1)S(1)}, u32[]{:S(2)}) copy-start(bf16[16,6400]{1,0:T(8,128)(2,1)S(1)} %collective-permute-done.2.refs_2_) | copy-start | bytes 614404
  66.3 14.4 %collective-permute-start.4 = (bf16[16,6400]{1,0:T(8,128)(2,1)S(1)}, bf16[16,6400]{1,0:T(8,128)(2,1)S(1)}, u32[]{:S(2)}, u32[]{:S(2)}) collective-permute-start(bf16[16,6400]{1,0:T(8,128)(2,1)S(1)} %collective-permute-done.2.refs_2_), channel_id=1, source_target_pairs={{0,16},{32,0},{64,32},{96,64},{112,96},{80,112},{48,80},{16,48},{1... | collective-permute-start | bytes 614408 | tf_op jit(solution)/shard_map/ppermute | solution.py:38
  68.3 26.8 %collective-permute-start.8 = (bf16[48,6400]{1,0:T(8,128)(2,1)S(1)}, bf16[48,6400]{1,0:T(8,128)(2,1)S(1)}, u32[]{:S(2)}, u32[]{:S(2)}) collective-permute-start(bf16[48,6400]{1,0:T(8,128)(2,1)S(1)} %pad_maximum_fusion), channel_id=1, source_target_pairs={{128,256},{256,128},{384,0},{0,384},{129,257},{257,129},{385,1},{1... | collective-permute-start | bytes 1843208 | tf_op jit(solution)/shard_map/ppermute | solution.py:198
  72.7 28.0 %copy-start.3 = (bf16[16,6400]{1,0:T(8,128)(2,1)}, bf16[16,6400]{1,0:T(8,128)(2,1)S(1)}, u32[]{:S(2)}) copy-start(bf16[16,6400]{1,0:T(8,128)(2,1)S(1)} %collective-permute-done.3.refs_3_) | copy-start | bytes 614404
  72.7 13.7 %collective-permute-start.5 = (bf16[16,6400]{1,0:T(8,128)(2,1)S(1)}, bf16[16,6400]{1,0:T(8,128)(2,1)S(1)}, u32[]{:S(2)}, u32[]{:S(2)}) collective-permute-start(bf16[16,6400]{1,0:T(8,128)(2,1)S(1)} %collective-permute-done.3.refs_3_), channel_id=1, source_target_pairs={{0,32},{32,64},{64,96},{96,112},{112,80},{80,48},{48,16},{16,0},{1... | collective-permute-start | bytes 614408 | tf_op jit(solution)/shard_map/ppermute | solution.py:37
  80.7 20.0 %copy-start.4 = (bf16[16,6400]{1,0:T(8,128)(2,1)}, bf16[16,6400]{1,0:T(8,128)(2,1)S(1)}, u32[]{:S(2)}) copy-start(bf16[16,6400]{1,0:T(8,128)(2,1)S(1)} %collective-permute-done.4.refs_4_) | copy-start | bytes 614404
  80.7 10.1 %collective-permute-start.6 = (bf16[16,6400]{1,0:T(8,128)(2,1)S(1)}, bf16[16,6400]{1,0:T(8,128)(2,1)S(1)}, u32[]{:S(2)}, u32[]{:S(2)}) collective-permute-start(bf16[16,6400]{1,0:T(8,128)(2,1)S(1)} %collective-permute-done.4.refs_4_), channel_id=1, source_target_pairs={{0,16},{32,0},{64,32},{96,64},{112,96},{80,112},{48,80},{16,48},{1... | collective-permute-start | bytes 614408 | tf_op jit(solution)/shard_map/ppermute | solution.py:38
  82.6 33.3 %collective-permute-start.14 = (bf16[6400,128]{1,0:T(8,128)(2,1)}, bf16[6400,128]{1,0:T(8,128)(2,1)}, u32[]{:S(2)}, u32[]{:S(2)}) collective-permute-start(bf16[6400,128]{1,0:T(8,128)(2,1)} %collective-permute-done.13.refs_14_), channel_id=1, source_target_pairs={{0,8},{8,0},{1,9},{9,1},{2,10},{10,2},{3,11},{11,3},{4,12},{12,4},... | collective-permute-start | bytes 4915208 | tf_op jit(solution)/shard_map/ppermute | solution.py:26
  86.3 29.6 %copy-start.5 = (bf16[16,6400]{1,0:T(8,128)(2,1)}, bf16[16,6400]{1,0:T(8,128)(2,1)S(1)}, u32[]{:S(2)}) copy-start(bf16[16,6400]{1,0:T(8,128)(2,1)S(1)} %collective-permute-done.5.refs_5_) | copy-start | bytes 614404
  86.4 14.3 %collective-permute-start.9 = (bf16[32,6400]{1,0:T(8,128)(2,1)S(1)}, bf16[32,6400]{1,0:T(8,128)(2,1)S(1)}, u32[]{:S(2)}, u32[]{:S(2)}) collective-permute-start(bf16[32,6400]{1,0:T(8,128)(2,1)S(1)} %pad_maximum_fusion.1), channel_id=1, source_target_pairs={{128,256},{256,128},{384,0},{0,384},{129,257},{257,129},{385,1},{1... | collective-permute-start | bytes 1228808 | tf_op jit(solution)/shard_map/ppermute | solution.py:198
  90.8 9.9 %copy-start.6 = (bf16[16,6400]{1,0:T(8,128)(2,1)}, bf16[16,6400]{1,0:T(8,128)(2,1)S(1)}, u32[]{:S(2)}) copy-start(bf16[16,6400]{1,0:T(8,128)(2,1)S(1)} %collective-permute-done.6.refs_6_) | copy-start | bytes 614404
  90.8 19.6 %collective-permute-start.10 = (bf16[32,6400]{1,0:T(8,128)(2,1)S(1)}, bf16[32,6400]{1,0:T(8,128)(2,1)}, u32[]{:S(2)}, u32[]{:S(2)}) collective-permute-start(bf16[32,6400]{1,0:T(8,128)(2,1)S(1)} %pad_maximum_fusion.2), channel_id=1, source_target_pairs={{128,256},{256,128},{384,0},{0,384},{129,257},{257,129},{385,1},{1... | collective-permute-start | bytes 1228808 | tf_op jit(solution)/shard_map/ppermute | solution.py:198
  95.1 5.6 %copy-start.8 = (bf16[48,6400]{1,0:T(8,128)(2,1)}, bf16[48,6400]{1,0:T(8,128)(2,1)S(1)}, u32[]{:S(2)}) copy-start(bf16[48,6400]{1,0:T(8,128)(2,1)S(1)} %collective-permute-done.8.refs_8_) | copy-start | bytes 1843204
  95.1 11.2 %collective-permute-start.7 = (bf16[16,6400]{1,0:T(8,128)(2,1)S(1)}, bf16[16,6400]{1,0:T(8,128)(2,1)}, u32[]{:S(2)}, u32[]{:S(2)}) collective-permute-start(bf16[16,6400]{1,0:T(8,128)(2,1)S(1)} %collective-permute-done.5.refs_5_), channel_id=1, source_target_pairs={{0,32},{32,64},{64,96},{96,112},{112,80},{80,48},{48,16},{16,0},{1... | collective-permute-start | bytes 614408 | tf_op jit(solution)/shard_map/ppermute | solution.py:40
  100.7 0.8 copy-start.9
  101.5 52.0 %collective-permute-start.17 = (bf16[4,1152,128]{2,1,0:T(8,128)(2,1)S(1)}, bf16[4,1152,128]{2,1,0:T(8,128)(2,1)S(1)}, u32[]{:S(2)}, u32[]{:S(2)}) collective-permute-start(bf16[4,1152,128]{2,1,0:T(8,128)(2,1)S(1)} %all-to-all-done.2.near), channel_id=1, source_target_pairs={{0,8},{8,0},{1,9},{9,1},{2,10},{10,2},{3,11},{11,3},{4,12},{12,4},... | collective-permute-start | bytes 3538952 | tf_op jit(solution)/shard_map/ppermute | solution.py:26
  106.3 9.6 %collective-permute-start.11 = (bf16[16,6400]{1,0:T(8,128)(2,1)}, bf16[16,6400]{1,0:T(8,128)(2,1)}, u32[]{:S(2)}, u32[]{:S(2)}) collective-permute-start(bf16[16,6400]{1,0:T(8,128)(2,1)} %collective-permute-done.7.refs_7_), channel_id=1, source_target_pairs={{128,256},{256,128},{384,0},{0,384},{129,257},{257,129},{385,1},{1... | collective-permute-start | bytes 614408 | tf_op jit(solution)/shard_map/ppermute | solution.py:198
  139.6 25.5 %all-to-all-start.1 = ((f32[16,8,128]{2,1,0:T(8,128)}), f32[16,8,128]{2,1,0:T(8,128)S(1)}, u32[]{:S(2)}, u32[]{:S(2)}) async-start(f32[16,8,128]{2,1,0:T(8,128)} %bitcast.4), calls=%async_computation.1 | async-start | bytes 131072 | tf_op jit(solution)/shard_map/all_to_all | solution.py:30
